TPU v7x, 256 devices: a whole 4x4x8 slice. The times are simulated.
256 devices in a mesh: stn: 64 (over y_hi, z, x), beam: 4 (over y_lo, core).
Axes of the slice: x: 4, y: 4 (y_hi: 2, y_lo: 2; y = y_hi * 2 + y_lo), z: 8, core: 2. Of those that a mesh axis runs over, the one named last changes fastest.
Arguments:
- voltages: bfloat16 [512, 2, 614400], P(('stn', 'beam')), may hold values from -6 to 6
- fir_taps: float32 [12, 8192], replicated, may hold values from -1.75 to 1.75
- delays: float32 [64, 64, 512], P('stn', 'beam'), may hold values from -16 to 16
- taper: float32 [64, 512], replicated, may hold values from 0.5 to 2
- station_map: int32 [512], replicated, may hold values from 0 to 511, each once
- beam_order: int32 [64], replicated, may hold values from 0 to 63, each once
- owners: int32 [4], replicated, may hold values from 0 to 63
Outputs:
- beams_re: float32 [64, 4096, 128], P('beam', 'stn')
- beams_im: float32 [64, 4096, 128], P('beam', 'stn')
Inputs may be any that keep to these rules, and one draw needn't show every extreme that they name: `station_map`: each station row holds a different physical station. `beam_order`: each beam slot forms a different beam.
All inputs are finite; a program needn't handle non-finite values.
Results may differ from a plain program's by a relative error of at most 0.0064.
Values may be sent and summed in bfloat16 or wider, within the bound.
No kernel may reach another device: no remote copies, remote signals or barrier semaphores. Data moves between devices by JAX's collectives and lax.ppermute only.
A program may use at most 128 MiB of HBM per device.

v0:
```python
import math

import jax
import jax.numpy as jnp
from jax import lax
from jax.sharding import PartitionSpec as P

P_SIZE = 64
Q = 128
CHANNELS = 4096


TWO_PI = 2.0 * math.pi


def from_root(value, axis, source):
    kept = jnp.where(lax.axis_index(axis) == source, value, 0).astype(value.dtype)
    return lax.psum(kept, axis)


def dft_tables():
    first_idx = jnp.arange(P_SIZE, dtype=jnp.int32)
    second_idx = jnp.arange(Q, dtype=jnp.int32)
    half_idx = jnp.arange(Q // 2, dtype=jnp.int32)
    first_angle = (
        TWO_PI / P_SIZE * (first_idx[:, None] * first_idx[None, :] % P_SIZE).astype(jnp.float32)
    )
    twist_angle = (
        TWO_PI / (P_SIZE * Q) * (first_idx[:, None] * second_idx[None, :]).astype(jnp.float32)
    )
    second_angle = TWO_PI / Q * (second_idx[:, None] * half_idx[None, :] % Q).astype(jnp.float32)
    return (
        jnp.cos(first_angle).astype(jnp.bfloat16),
        jnp.sin(first_angle).astype(jnp.bfloat16),
        jnp.cos(twist_angle),
        jnp.sin(twist_angle),
        jnp.cos(second_angle).astype(jnp.bfloat16),
        jnp.sin(second_angle).astype(jnp.bfloat16),
    )


def beam_weights(delay_cols, gain_cols, chan_ids):
    phase = (
        delay_cols[:, :, None]
        * chan_ids.astype(jnp.float32)[None, None, :]
        * (TWO_PI / (P_SIZE * Q))
    )
    weight_re = (gain_cols[:, :, None] * jnp.cos(phase)).astype(jnp.bfloat16)
    weight_im = (-(gain_cols[:, :, None] * jnp.sin(phase))).astype(jnp.bfloat16)
    left_re = jnp.concatenate((weight_re, -weight_im), axis=1)
    left_im = jnp.concatenate((weight_im, weight_re), axis=1)
    return (left_re, left_im)


def channelize(voltages, fir_taps):
    cos_one, sin_one, twist_cos, twist_sin, cos_two, sin_two = dft_tables()
    local_stations, pol_count, samples = voltages.shape
    tap_count, fft_width = fir_taps.shape
    frames = samples // fft_width - tap_count + 1
    blocks = voltages.reshape(local_stations, pol_count, frames + tap_count - 1, fft_width)
    filtered = jnp.zeros((local_stations, pol_count, frames, fft_width), jnp.float32)
    for tap_idx in range(tap_count):
        filtered = filtered + fir_taps[tap_idx] * blocks[:, :, tap_idx : tap_idx + frames].astype(
            jnp.float32
        )
    folded = filtered.astype(jnp.bfloat16).reshape(local_stations, pol_count, frames, P_SIZE, Q)
    first_table = jnp.concatenate((cos_one, -sin_one), axis=0)
    first_section = jnp.einsum(
        "spfnq,an->spfaq", folded, first_table, preferred_element_type=jnp.float32
    )
    first_re = first_section[:, :, :, :P_SIZE]
    first_im = first_section[:, :, :, P_SIZE:]
    turned = jnp.concatenate(
        (
            (first_re * twist_cos + first_im * twist_sin).astype(jnp.bfloat16),
            (first_im * twist_cos - first_re * twist_sin).astype(jnp.bfloat16),
        ),
        axis=4,
    )
    second_table = jnp.concatenate(
        (jnp.concatenate((cos_two, -sin_two), axis=1), jnp.concatenate((sin_two, cos_two), axis=1)),
        axis=0,
    )
    second = jnp.einsum("spfaq,qb->sbapf", turned, second_table, preferred_element_type=jnp.float32)
    half_q = Q // 2
    chan_re = (
        second[:, :half_q]
        .astype(jnp.bfloat16)
        .reshape(local_stations, half_q * P_SIZE, pol_count * frames)
    )
    chan_im = (
        second[:, half_q:]
        .astype(jnp.bfloat16)
        .reshape(local_stations, half_q * P_SIZE, pol_count * frames)
    )
    return jnp.stack((chan_re, chan_im), axis=0)


def combine(left_re, left_im, stacked_parts, beam_scale):
    stacked = jnp.concatenate((stacked_parts[0], stacked_parts[1]), axis=0)
    beam_re = (
        jnp.einsum("jrk,rkc->jkc", left_re, stacked, preferred_element_type=jnp.float32)
        * beam_scale
    )
    beam_im = (
        jnp.einsum("jrk,rkc->jkc", left_im, stacked, preferred_element_type=jnp.float32)
        * beam_scale
    )
    return jnp.stack((beam_re, beam_im), axis=0)


def on_device(voltages, fir_taps, delays, taper, station_map, beam_order, owners):
    stn_count = lax.axis_size("stn")
    beam_count = lax.axis_size("beam")
    stn_pos = lax.axis_index("stn")
    beam_pos = lax.axis_index("beam")
    local_stations = voltages.shape[0]
    stations = station_map.shape[0]
    group_beams = beam_order.shape[0] // beam_count
    chan_dev = CHANNELS // stn_count
    chan_ids = stn_pos * chan_dev + jnp.arange(chan_dev, dtype=jnp.int32)
    beam_scale = 1.0 / math.sqrt(P_SIZE * Q * stations)
    spectra = channelize(voltages, fir_taps)
    owner_model = from_root(delays, "stn", owners[beam_pos])[0]
    row_stn = jnp.arange(stn_count * local_stations, dtype=jnp.int32)
    all_rows = (
        (row_stn // local_stations * beam_count + jnp.arange(beam_count, dtype=jnp.int32)[:, None])
        * local_stations
        + row_stn % local_stations
    ).reshape(-1)
    phys_ids = station_map[all_rows]
    slot_gain = taper[beam_order[beam_pos * group_beams + jnp.arange(group_beams, dtype=jnp.int32)]]
    left_re, left_im = beam_weights(owner_model[:, phys_ids], slot_gain[:, phys_ids], chan_ids)
    full_rows = lax.all_gather(
        lax.all_to_all(spectra, "stn", split_axis=2, concat_axis=1, tiled=True),
        "beam",
        axis=1,
        tiled=True,
    )
    formed = combine(left_re, left_im, full_rows, beam_scale)
    return (formed[0], formed[1])


def solution(mesh):
    return jax.shard_map(
        on_device,
        mesh=mesh,
        in_specs=(P(("stn", "beam"), None, None), P(), P("stn", "beam", None), P(), P(), P(), P()),
        out_specs=(P("beam", "stn", None), P("beam", "stn", None)),
        check_vma=False,
    )
```

profile of v0, /device:TPU:16, one launch (start us, length us, event | category | flops | bytes accessed | tf_op | source)
XLA Modules:
  0.0 628.2 jit_solution(1775256071955894884)
XLA Ops:
  7.7 0.3 sine_convert_fusion
  8.2 2.6 fusion.59
  10.9 6.3 reshape.166
  17.1 28.3 %add_convert_fusion.1 = bf16[2,2,64,8192]{3,2,1,0:T(8,128)(2,1)S(1)} fusion(bf16[2,2,75,8192]{3,2,1,0:T(8,128)(2,1)} %reshape.166, f32[8192]{0:T(1024)S(1)} %bitcast.83, f32[8192]{0:T(1024)S(1)} %bitcast.84, f32[8192]{0:T(1024)S(1)} %bitcast.74, f32[8192]{0:T(1024)S(1)} %bitcast.75, f32[8192]{0:T(1024)S(1)} %bitcast.76, f32[8192]{0:T(1024)S(1)} %bitcast.77, ...), kind=kLoop, calls=%fused_computation.16 | loop fusion | flops 75497472 | bytes 54919168 | tf_op jit(solution)/shard_map/convert_element_type | solution.py:66
  45.4 1.2 copy.38
  46.6 2.4 convolution_bitcast_fusion
  49.0 2.5 add_convert_fusion
  51.6 3.1 convert_bitcast_fusion
  54.7 4.3 fusion.58
  59.0 6.3 %copy.25 = bf16[2,64,64,2,64]{2,1,4,3,0:T(8,128)(2,1)} copy(bf16[2,64,64,2,64]{1,2,4,3,0:T(8,128)(2,1)} %get-tuple-element.12) | data formatting | bytes 4194304 | tf_op jit(solution)/shard_map/slice | solution.py:87
  65.3 5.7 stack_reshape.6
  71.0 6.4 %copy.26 = bf16[2,64,64,2,64]{2,1,4,3,0:T(8,128)(2,1)} copy(bf16[2,64,64,2,64]{1,2,4,3,0:T(8,128)(2,1)} %get-tuple-element.13) | data formatting | bytes 4194304 | tf_op jit(solution)/shard_map/slice | solution.py:92
  77.3 6.6 %stack_reshape.7 = bf16[1,2,4096,128]{2,3,1,0:T(8,128)(2,1)} reshape(bf16[2,64,64,2,64]{2,1,4,3,0:T(8,128)(2,1)} %copy.26) | data formatting | bytes 4194304 | tf_op jit(solution)/shard_map/stack;reshape | solution.py:96
  83.9 3.9 pad_maximum_fusion.3
  87.8 11.1 %copy.27 = bf16[2,2,4096,128]{3,1,0,2:T(2,128)(2,1)} copy(bf16[2,2,4096,128]{2,3,1,0:T(8,128)(2,1)} %pad_maximum_fusion.3) | data formatting | bytes 8388608 | tf_op jit(solution)/shard_map/stack | solution.py:96
  99.0 108.4 %all_to_all.18 = bf16[2,2,4096,128]{3,1,0,2:T(2,128)(2,1)S(1)} all-to-all(bf16[2,2,4096,128]{3,1,0,2:T(2,128)(2,1)} %copy.27), channel_id=1, replica_groups=mesh['stn'=64,'beam'=4] {'stn'}, dimensions={2} | all-to-all | bytes 8388608 | tf_op jit(solution)/shard_map/all_to_all | solution.py:135
  207.4 2.5 copy.28
  209.9 8.5 %copy.29 = bf16[2,64,2,64,128]{4,2,1,3,0:T(2,128)(2,1)} copy(bf16[2,64,2,64,128]{4,3,1,2,0:T(8,128)(2,1)} %bitcast.69) | data formatting | bytes 8388608 | tf_op jit(solution)/shard_map/all_to_all | solution.py:135
  218.6 0.6 dynamic_slice.3
  219.9 3.5 gather_fusion.2
  223.4 359.8 %psum.7 = f32[16,512]{0,1:T(8,128)S(1)} all-reduce(f32[16,512]{0,1:T(8,128)S(1)} %select_bitcast_fusion), channel_id=1, replica_groups=mesh['stn'=64,'beam'=4] {'stn'}, use_global_device_ids=true, to_apply=%region_0.1 | all-reduce | flops 8192 | bytes 65536 | tf_op jit(solution)/shard_map/psum | solution.py:18
  583.2 1.0 gather_fusion.4
  584.4 0.7 gather_fusion
  585.1 0.6 gather_fusion.1
  585.8 1.0 gather_fusion.3
  587.0 8.3 %fusion.57 = bf16[16,512,64]{1,0,2:T(8,128)(2,1)} fusion(f32[64]{0:T(128)S(1)} %add_convert_fusion.2, f32[16,512]{1,0:T(8,128)S(1)} %copy.33, f32[16,512]{1,0:T(8,128)S(1)} %copy.31), kind=kLoop, calls=%fused_computation.93 | loop fusion | flops 4194304 | bytes 1114368 | tf_op jit(solution)/shard_map/neg | solution.py:50
  595.3 9.2 %negate_convert_fusion = (bf16[16,512,64]{1,0,2:T(8,128)(2,1)}, bf16[16,512,64]{1,0,2:T(8,128)(2,1)}) fusion(f32[64]{0:T(128)S(1)} %add_convert_fusion.2, f32[16,512]{1,0:T(8,128)S(1)} %copy.33, f32[16,512]{1,0:T(8,128)S(1)} %copy.31), kind=kLoop, calls=%fused_computation.26 | loop fusion | flops 3670016 | bytes 2162944 | tf_op jit(solution)/shard_map/convert_element_type | solution.py:49
  604.5 6.6 %slice_bitcast_fusion.1 = (bf16[512,64,128]{2,0,1:T(8,128)(2,1)S(1)}, bf16[512,64,128]{2,0,1:T(8,128)(2,1)S(1)}) fusion(bf16[2,512,64,128]{3,1,2,0:T(8,128)(2,1)} %all-gather.2.cloned.1.call-done), kind=kLoop, calls=%fused_computation.9 | loop fusion | bytes 33554432 | tf_op jit(solution)/shard_map/squeeze | solution.py:100
  611.1 4.2 fusion.17
  615.3 1.0 copy.35
  616.2 4.2 fusion.23
  620.4 1.0 copy.34
  (33 shorter events, 1.3 us)
Async XLA Ops:
  7.2 577.9 %copy-start = (f32[64,512]{1,0:T(8,128)S(1)}, f32[64,512]{1,0:T(8,128)}, u32[]{:S(2)}) copy-start(f32[64,512]{1,0:T(8,128)} %param.10) | copy-start | bytes 393220
  7.2 597.3 %all-gather.2.cloned.1.call-start = ((), (), s32[]{:S(2)}) async-start(), calls=%async_computation.1 | async-start | bytes 20971520 | tf_op jit(solution)/shard_map/all_gather | solution.py:134
  209.9 8.5 %copy-start.3 = (f32[1,16,512]{2,1,0:T(8,128)S(1)}, f32[1,16,512]{2,1,0:T(8,128)}, u32[]{:S(2)}) copy-start(f32[1,16,512]{2,1,0:T(8,128)} %param.9) | copy-start | bytes 98308
  209.9 8.7 %copy-start.4 = (s32[4]{0:T(128)S(1)}, s32[4]{0:T(128)}, u32[]{:S(2)}) copy-start(s32[4]{0:T(128)} %param.13) | copy-start | bytes 52
  209.9 10.0 %copy-start.1 = (s32[512]{0:T(512)S(1)}, s32[512]{0:T(512)}, u32[]{:S(2)}) copy-start(s32[512]{0:T(512)} %param.11) | copy-start | bytes 6148
  209.9 374.5 %copy-start.2 = (s32[64]{0:T(128)S(1)}, s32[64]{0:T(128)}, u32[]{:S(2)}) copy-start(s32[64]{0:T(128)} %param.12) | copy-start | bytes 772
Sparse Core Ops, SparseCore 0:
  218.5 152.3 all-gather.1
where the time goes:
time: 629 us; the launch traced here: 628 us
  blocking collectives  468 us (74%)
  local copies, waits for them, and re-layouts  77.8 us (12%)
  other arithmetic  53.3 us (8%)
  between operations  14.9 us (2%)
  matrix products  13.9 us (2%)
    psum x1, blocking collectives, from_root(): return lax.psum(kept, axis)  360 us
    all_to_all x1, blocking collectives, on_device(): lax.all_to_all(spectra, 'stn', split_axis=2, concat_axis=1, tiled=True)  108 us
    convert_element_type x1, other arithmetic, channelize(): filtered.astype(jnp.bfloat16)  28.3 us
    another operation x3, local copies, waits for them, and re-layouts, channelize(): return jnp.stack((chan_re, chan_im), axis=0)  23.4 us
  transfers between devices with their start and end apart: 1, of which 0 were waited for; matrix products, arithmetic and copies ran while one was open for 4% of the time, Pallas kernels for 0%

commit v1 on v0

v1 whole, which is shorter than its diff:
```python
import math

import jax
import jax.numpy as jnp
import ml_dtypes
import numpy as np
from jax import lax
from jax.experimental import pallas as pl
from jax.experimental.pallas import tpu as pltpu
from jax.sharding import Mesh
from jax.sharding import PartitionSpec as P

P_SIZE = 64
Q = 128
CHANNELS = 4096
TAPS = 12
FRAMES = 64
STATIONS = 512
TWO_PI = 2.0 * math.pi
F32 = jnp.float32
BF16 = jnp.bfloat16
VMEM_LIMIT = 56 << 20

AXES = ("yh", "zh", "zl", "x", "yl", "c")
SIZES = (2, 4, 2, 4, 2, 2)
TURN = ("yh", "zl", "x", "yl", "c")
MERGE = ("zh", "yl", "c")
FRAME_CHUNK = 16


def dft_tables():
    idx = np.arange(P_SIZE)
    wide = np.arange(Q)
    first = TWO_PI / P_SIZE * (idx[:, None] * idx[None, :] % P_SIZE)
    second = TWO_PI / Q * (wide[:, None] * idx[None, :] % Q)
    twist = TWO_PI / (P_SIZE * Q) * (idx[:, None] * wide[None, :])

    def narrow(x):
        return x.astype(np.float32).astype(ml_dtypes.bfloat16)

    cos_one, sin_one = narrow(np.cos(first)), narrow(np.sin(first))
    cos_two, sin_two = narrow(np.cos(second)).T, narrow(np.sin(second)).T
    one = np.zeros((2, 2, P_SIZE, P_SIZE, 2), ml_dtypes.bfloat16)
    for pol in range(2):
        one[pol, 0, :, :, pol] = cos_one
        one[pol, 1, :, :, pol] = -sin_one
    two = np.zeros((2, P_SIZE, 2, Q), ml_dtypes.bfloat16)
    two[0, :, 0], two[0, :, 1] = cos_two, sin_two
    two[1, :, 0], two[1, :, 1] = -sin_two, cos_two
    turn = np.stack((np.cos(twist), np.sin(twist))).astype(np.float32)
    return one.reshape(4 * P_SIZE, 2 * P_SIZE), turn, two.reshape(2 * P_SIZE, 2 * Q)


def channel_kernel(volts, taps, one, twist, two, out, folded, turned_re, turned_im, stage):
    def filter_rows(block, carry):
        row = pl.multiple_of(block * 16, 16)
        coeff = [taps[m, pl.ds(row, 16), :] for m in range(TAPS)]
        for chunk in range(FRAMES // FRAME_CHUNK):
            first = chunk * FRAME_CHUNK
            window = [
                volts[0, first + t, pl.ds(row, 16), :].astype(F32)
                for t in range(FRAME_CHUNK + TAPS - 1)
            ]
            for k in range(FRAME_CHUNK):
                acc = coeff[0] * window[k]
                for m in range(1, TAPS):
                    acc = acc + coeff[m] * window[k + m]
                frame = first + k
                lane = frame % 2 * Q
                folded[frame // 2, pl.ds(row, 16), lane : lane + Q] = acc.astype(BF16)
        return carry

    lax.fori_loop(0, 8, filter_rows, 0)

    def first_section(pair, carry):
        part = jnp.dot(one[...], folded[pair], preferred_element_type=F32)
        for pol in range(2):
            for half in range(2):
                lanes = slice(half * Q, (half + 1) * Q)
                re = part[pol * 128 : pol * 128 + 64, lanes]
                im = part[pol * 128 + 64 : pol * 128 + 128, lanes]
                row = pol * FRAMES + pair * 2 + half
                turned_re[pl.ds(row, 64, stride=128), :] = re * twist[0] + im * twist[1]
                turned_im[pl.ds(row, 64, stride=128), :] = im * twist[0] - re * twist[1]
        return carry

    lax.fori_loop(0, FRAMES // 2, first_section, 0)

    def second_section(j, carry):
        for i in range(16):
            row = pl.multiple_of((j * 16 + i) * 128, 128)
            right = jnp.concatenate(
                (
                    turned_re[pl.ds(row, 128), :].astype(BF16),
                    turned_im[pl.ds(row, 128), :].astype(BF16),
                ),
                axis=1,
            )
            part = lax.dot_general(
                two[...], right, (((1,), (1,)), ((), ())), preferred_element_type=F32
            )
            stage[0, pl.ds(i, 64, stride=16), :] = part[:64]
            stage[1, pl.ds(i, 64, stride=16), :] = part[64:]
        for b in range(64):
            yh, zh, zl, x = b // 32, b // 8 % 4, b // 4 % 2, b % 4
            for ri in range(2):
                out[yh, zl, x, j, zh, 0, ri] = stage[ri, b * 16 : (b + 1) * 16, :].astype(BF16)
        return carry

    lax.fori_loop(0, 4, second_section, 0)


def whole(*shape):
    return pl.BlockSpec(shape, lambda step: (0,) * len(shape))


def channelize(voltages, fir_taps):
    one, twist, two = dft_tables()
    volts = voltages.reshape(2, 2, 75 * P_SIZE, Q).transpose(0, 2, 1, 3).reshape(2, 75, 128, Q)
    taps = jnp.broadcast_to(fir_taps.reshape(TAPS, P_SIZE, 1, Q), (TAPS, P_SIZE, 2, Q))
    return pl.pallas_call(
        channel_kernel,
        grid=(2,),
        in_specs=[
            pl.BlockSpec((1, 75, 128, Q), lambda s: (s, 0, 0, 0)),
            whole(TAPS, 128, Q),
            whole(256, 128),
            whole(2, 64, Q),
            whole(128, 256),
        ],
        out_specs=pl.BlockSpec(
            (2, 2, 4, 4, 4, 1, 2, 16, 128), lambda s: (0, 0, 0, 0, 0, s, 0, 0, 0)
        ),
        out_shape=jax.ShapeDtypeStruct((2, 2, 4, 4, 4, 2, 2, 16, 128), BF16),
        scratch_shapes=[
            pltpu.VMEM((FRAMES // 2, 128, 256), BF16),
            pltpu.VMEM((64 * 128, Q), F32),
            pltpu.VMEM((64 * 128, Q), F32),
            pltpu.VMEM((2, 1024, 128), F32),
        ],
        compiler_params=pltpu.CompilerParams(vmem_limit_bytes=VMEM_LIMIT),
        name="channelize",
    )(volts, taps.reshape(TAPS, 128, Q), jnp.asarray(one), jnp.asarray(twist), jnp.asarray(two))


def beam_kernel(spectra, base, step, out, wide):
    for src in range(64):
        wide[src * 64 : (src + 1) * 64, :] = spectra[src, 0].astype(F32)
    cos_w, sin_w = base[0, 0], base[0, 1]
    cos_step, sin_step = step[0], step[1]
    for i in range(16):
        right = jnp.concatenate(
            [
                wide[pl.ds((s * 2 + ri) * 16 + i, 64, stride=64), :].astype(BF16)
                for ri in range(2)
                for s in range(2)
            ],
            axis=0,
        )
        cos_n, sin_n = cos_w.astype(BF16), sin_w.astype(BF16)
        left = jnp.concatenate(
            (
                jnp.concatenate((cos_n, sin_n), axis=1),
                jnp.concatenate((-sin_n, cos_n), axis=1),
            ),
            axis=0,
        )
        part = jnp.dot(left, right, preferred_element_type=F32)
        for ri in range(2):
            for group in range(4):
                row = ri * 64 + group * 16
                out[0, group, ri, i] = part[row : row + 16].astype(BF16)
        if i < 15:
            cos_w, sin_w = (
                cos_w * cos_step - sin_w * sin_step,
                sin_w * cos_step + cos_w * sin_step,
            )


def form_beams(spectra, base, step):
    return pl.pallas_call(
        beam_kernel,
        grid=(4,),
        in_specs=[
            pl.BlockSpec((64, 1, 64, 128), lambda zh: (0, zh, 0, 0)),
            pl.BlockSpec((1, 2, 64, 128), lambda zh: (zh, 0, 0, 0)),
            whole(2, 64, 128),
        ],
        out_specs=pl.BlockSpec((1, 4, 2, 16, 16, 128), lambda zh: (zh, 0, 0, 0, 0, 0)),
        out_shape=jax.ShapeDtypeStruct((4, 4, 2, 16, 16, 128), BF16),
        scratch_shapes=[pltpu.VMEM((64 * 64, 128), F32)],
        compiler_params=pltpu.CompilerParams(vmem_limit_bytes=VMEM_LIMIT),
        name="form_beams",
    )(spectra, base, step)


def merge_kernel(parts, out_re, out_im):
    scale = 1.0 / math.sqrt(P_SIZE * Q * STATIONS)
    for ri, out in ((0, out_re), (1, out_im)):
        for i in range(16):
            total = parts[0, 0, ri, i].astype(F32)
            for zh in range(1, 4):
                total = total + parts[zh, 0, ri, i].astype(F32)
            out[:, i, :] = total * scale


def merge(parts):
    spec = pl.BlockSpec((16, 16, 128), lambda j: (0, j, 0))
    shape = jax.ShapeDtypeStruct((16, 64, 128), F32)
    return pl.pallas_call(
        merge_kernel,
        grid=(4,),
        in_specs=[pl.BlockSpec((4, 1, 2, 16, 16, 128), lambda j: (0, j, 0, 0, 0, 0))],
        out_specs=[spec, spec],
        out_shape=[shape, shape],
        compiler_params=pltpu.CompilerParams(vmem_limit_bytes=VMEM_LIMIT),
        name="merge",
    )(parts)


def beam_model(delays, taper, station_map, beam_order, owners):
    yh, zh, zl, x, yl, c = [lax.axis_index(name) for name in AXES]
    stn_pos = ((yh * 4 + zh) * 2 + zl) * 4 + x
    beam_pos = yl * 2 + c
    kept = jnp.where(owners[beam_pos] == stn_pos, delays[0], 0.0)
    gains = taper[beam_order]
    phys = station_map.reshape(2, 4, 32, 2).transpose(1, 3, 0, 2).reshape(STATIONS)
    pick = (jnp.arange(STATIONS, dtype=jnp.int32)[:, None] == phys[None, :]).astype(F32)
    cols = jnp.dot(
        jnp.concatenate((kept, gains), axis=0), pick, precision=lax.Precision.HIGHEST
    )
    slots = kept.shape[0]
    by_zh = cols[:slots].reshape(slots, 4, 128).transpose(1, 0, 2)
    mine = lax.psum_scatter(by_zh, "zh", scatter_dimension=0, tiled=False)
    gain = lax.dynamic_slice_in_dim(cols[slots:], zh * 128, 128, 1)
    spread = lax.all_to_all(
        jnp.broadcast_to(mine[None], (16, slots, 128)), ("yh", "zl", "x"), 0, 0, tiled=True
    )
    owner = owners[beam_pos]
    source = (owner // 32 * 2 + owner // 4 % 2) * 4 + owner % 4
    chosen = lax.dynamic_index_in_dim(spread, source, 0, keepdims=False)
    delay = lax.all_gather(chosen, ("yl", "c"), axis=0, tiled=True)
    return delay, gain


def on_device(voltages, fir_taps, delays, taper, station_map, beam_order, owners):
    yh, zh, zl, x, yl, c = [lax.axis_index(name) for name in AXES]
    spectra = channelize(voltages, fir_taps)
    delay, gain = beam_model(delays, taper, station_map, beam_order, owners)
    first_chan = yh * 2048 + zl * 256 + x * 64 + (yl * 2 + c) * 16
    chans = (first_chan + 512 * jnp.arange(4, dtype=jnp.int32)).astype(F32)
    unit = TWO_PI / (P_SIZE * Q)
    phase = delay[None] * chans[:, None, None] * unit
    base = jnp.stack((gain * jnp.cos(phase), gain * jnp.sin(phase)), axis=1)
    step = jnp.stack((jnp.cos(delay * unit), jnp.sin(delay * unit)))
    turned = lax.all_to_all(spectra.reshape(64, 4, 64, 128), TURN, 0, 0, tiled=True)
    partial = form_beams(turned, base, step)
    parts = lax.all_to_all(partial.reshape(16, 2, 16, 16, 128), MERGE, 0, 0, tiled=True)
    out_re, out_im = merge(parts.reshape(4, 4, 2, 16, 16, 128))
    return (out_re, out_im)


def solution(mesh):
    torus = Mesh(mesh.devices.reshape(SIZES), AXES)
    stn, beam = AXES[:4], AXES[4:]
    return jax.shard_map(
        on_device,
        mesh=torus,
        in_specs=(P(AXES, None, None), P(), P(stn, beam, None), P(), P(), P(), P()),
        out_specs=(P(beam, stn, None), P(beam, stn, None)),
        check_vma=False,
    )
```

time: 629 us -> 234 us (0.37)
  the two profiles are of different devices: /device:TPU:16 before, /device:TPU:1 now
where the time goes in v1:
time: 234 us; the launch traced here: 233 us
  blocking collectives  106 us (45%)
  Pallas kernels  54 us (23%)
  waiting for transfers between devices  26.8 us (11%)
  starting transfers between devices  18.6 us (8%)
  between operations  17.4 us (7%)
  local copies, waits for them, and re-layouts  7.27 us (3%)
  other arithmetic  2.73 us (1%)
    all_to_all x1, blocking collectives, on_device(): lax.all_to_all(partial.reshape(16, 2, 16, 16, 128), MERGE, 0, 0, tiled=True)  59.3 us
    all_gather x1, blocking collectives, beam_model(): delay = lax.all_gather(chosen, ('yl', 'c'), axis=0, tiled=True)  46.7 us
    pallas_call x1, Pallas kernels, channelize(): pl.pallas_call(channel_kernel, grid=(2,), in_specs=[pl.BlockSpec((1, 75,...  41.5 us
    reduce_scatter x1, waiting for transfers between devices, beam_model(): mine = lax.psum_scatter(by_zh, 'zh', scatter_dimension=0, tiled=False)  26.8 us
    all_to_all x1, starting transfers between devices, on_device(): lax.all_to_all(spectra.reshape(64, 4, 64, 128), TURN, 0, 0, tiled=True)  11.9 us
    pallas_call x1, Pallas kernels, form_beams(): pl.pallas_call(beam_kernel, grid=(4,), in_specs=[pl.BlockSpec((64, 1, 64,...  8.67 us
    all_to_all x1, starting transfers between devices, beam_model(): lax.all_to_all(jnp.broadcast_to(mine[None], (16, slots, 128)), ('yh', 'zl...  6.64 us
  transfers between devices with their start and end apart: 3, of which 1 were waited for; matrix products, arithmetic and copies ran while one was open for 2% of the time, Pallas kernels for 18%

profile of v1, /device:TPU:1, one launch (start us, length us, event | category | flops | bytes accessed | tf_op | source)
XLA Modules:
  0.0 233.4 jit_solution(17794675369829643078)
XLA Ops:
  7.2 0.0 copy-start
  7.2 0.0 reduce-scatter.2.cloned.1.call-start
  7.2 0.8 reshape.64
  8.1 0.1 copy.15
  8.2 0.1 eq.23
  8.3 0.7 compare_select_fusion
  8.9 0.0 copy-done
  8.9 0.7 gather_fusion
  9.6 1.2 dynamic_slice.11
  11.5 0.5 fusion
  12.0 0.6 bitcast_bitcast_fusion
  12.6 0.0 reduce-scatter.2.cloned.1.call-update
  12.7 26.8 %reduce-scatter.2.cloned.1.call-done = f32[1,16,128]{2,1,0:T(8,128)} async-done(((f32[4,16,128]{2,1,0:T(8,128)}), f32[1,16,128]{2,1,0:T(8,128)}) %reduce-scatter.2.cloned.1.call-update) | async-done | bytes 8208 | tf_op jit(solution)/shard_map/reduce_scatter | solution.py:234
  39.5 1.4 broadcast_in_dim.31
  40.8 6.6 %all-to-all-start.1 = ((f32[16,16,128]{2,1,0:T(8,128)}), f32[16,16,128]{2,1,0:T(8,128)S(1)}, u32[]{:S(2)}, u32[]{:S(2)}) async-start(f32[16,16,128]{2,1,0:T(8,128)} %broadcast_in_dim.31), calls=%async_computation.2 | async-start | bytes 262144 | tf_op jit(solution)/shard_map/all_to_all | solution.py:236
  47.5 1.1 copy.18
  48.7 1.2 broadcast_in_dim.27
  49.8 41.5 %channelize.1 = bf16[2,2,4,4,4,2,2,16,128]{8,7,6,5,4,3,2,1,0:T(8,128)(2,1)} custom-call(bf16[2,75,128,128]{3,2,1,0:T(8,128)(2,1)} %bitcast.34, f32[12,128,128]{2,1,0:T(8,128)} %bitcast.35, bf16[256,128]{1,0:T(8,128)(2,1)} %constant.99.clone.one, f32[2,64,128]{2,1,0:T(8,128)} %constant.100.clone.twist, bf16[128,256]{1,0:T(8,128)(2,1)} %constant.101.clone.two), custom_call_target="tpu_custom_call" | custom-call | tf_op jit(solution)/shard_map/channelize/pallas_call | solution.py:121
  91.3 0.0 all-to-all-done.1
  91.3 11.9 %all-to-all-start = ((bf16[64,4,64,128]{3,2,1,0:T(8,128)(2,1)}), bf16[64,4,64,128]{3,2,1,0:T(8,128)(2,1)}, u32[]{:S(2)}, u32[]{:S(2)}) async-start(bf16[64,4,64,128]{3,2,1,0:T(8,128)(2,1)} %bitcast.31), calls=%async_computation | async-start | bytes 8388608 | tf_op jit(solution)/shard_map/all_to_all | solution.py:256
  106.0 46.7 %all-gather = f32[1,64,128]{2,1,0:T(8,128)S(1)} all-gather(f32[1,16,128]{2,1,0:T(8,128)S(1)} %constant_dynamic-slice_fusion), channel_id=2, replica_groups=mesh['yh'=2,'zh'=4,'zl'=2,'x'=4,'yl'=2,'c'=2] {'yl','c'}, dimensions={1}, use_global_device_ids=true | all-gather | bytes 40960 | tf_op jit(solution)/shard_map/all_gather | solution.py:242
  152.7 0.1 cosine_bitcast_fusion
  152.8 0.6 pad_maximum_fusion.1.step
  153.4 0.5 cosine_multiply_fusion
  154.0 0.7 pad_maximum_fusion.base
  154.7 0.0 all-to-all-done.spectra
  154.7 8.7 %form_beams.1 = bf16[4,4,2,16,16,128]{5,4,3,2,1,0:T(8,128)(2,1)} custom-call(bf16[64,4,64,128]{3,2,1,0:T(8,128)(2,1)} %all-to-all-done.spectra, f32[4,2,64,128]{3,2,1,0:T(8,128)} %pad_maximum_fusion.base, f32[2,64,128]{2,1,0:T(8,128)} %pad_maximum_fusion.1.step), custom_call_target="tpu_custom_call" | custom-call | tf_op jit(solution)/shard_map/form_beams/pallas_call | solution.py:181
  163.4 59.3 %all_to_all.15 = bf16[16,2,16,16,128]{4,3,2,1,0:T(8,128)(2,1)} all-to-all(bf16[16,2,16,16,128]{4,3,2,1,0:T(8,128)(2,1)} %bitcast.32), channel_id=1, replica_groups=mesh['yh'=2,'zh'=4,'zl'=2,'x'=4,'yl'=2,'c'=2] {'zh','yl','c'}, dimensions={0} | all-to-all | bytes 4194304 | tf_op jit(solution)/shard_map/all_to_all | solution.py:258
  222.7 3.9 %merge.1 = (f32[16,64,128]{2,1,0:T(8,128)}, f32[16,64,128]{2,1,0:T(8,128)}) custom-call(bf16[4,4,2,16,16,128]{5,4,3,2,1,0:T(8,128)(2,1)} %bitcast.33), custom_call_target="tpu_custom_call" | custom-call | tf_op jit(solution)/shard_map/merge/pallas_call | solution.py:210
  (7 shorter events, 0.1 us)
Async XLA Ops:
  7.2 1.8 copy-start
  7.2 32.3 %reduce-scatter.2.cloned.1.call-start = ((), (), s32[]{:S(2)}) async-start(), calls=%async_computation.4 | async-start | bytes 40960 | tf_op jit(solution)/shard_map/reduce_scatter | solution.py:234
  40.8 50.5 %all-to-all-start.1 = ((f32[16,16,128]{2,1,0:T(8,128)}), f32[16,16,128]{2,1,0:T(8,128)S(1)}, u32[]{:S(2)}, u32[]{:S(2)}) async-start(f32[16,16,128]{2,1,0:T(8,128)} %broadcast_in_dim.31), calls=%async_computation.2 | async-start | bytes 262144 | tf_op jit(solution)/shard_map/all_to_all | solution.py:236
  91.3 63.4 %all-to-all-start = ((bf16[64,4,64,128]{3,2,1,0:T(8,128)(2,1)}), bf16[64,4,64,128]{3,2,1,0:T(8,128)(2,1)}, u32[]{:S(2)}, u32[]{:S(2)}) async-start(bf16[64,4,64,128]{3,2,1,0:T(8,128)(2,1)} %bitcast.31), calls=%async_computation | async-start | bytes 8388608 | tf_op jit(solution)/shard_map/all_to_all | solution.py:256
Sparse Core Ops, SparseCore 0:
  12.8 26.6 reduce-scatter.1

commit v2 on v1

v2 whole, which is shorter than its diff:
```python
import math

import jax
import jax.numpy as jnp
import ml_dtypes
import numpy as np
from jax import lax
from jax.experimental import pallas as pl
from jax.experimental.pallas import tpu as pltpu
from jax.sharding import Mesh
from jax.sharding import PartitionSpec as P

P_SIZE = 64
Q = 128
CHANNELS = 4096
TAPS = 12
FRAMES = 64
STATIONS = 512
TWO_PI = 2.0 * math.pi
F32 = jnp.float32
BF16 = jnp.bfloat16
VMEM_LIMIT = 56 << 20

AXES = ("yh", "zh", "zl", "x", "yl", "c")
SIZES = (2, 4, 2, 4, 2, 2)
TURN = ("yh", "zl", "x", "yl", "c")
MERGE = ("zh", "yl", "c")
FRAME_CHUNK = 16
TURN_ROWS = 136
STAGE_ROWS = 24
WIDE_ROWS = 40


def dft_tables():
    idx = np.arange(P_SIZE)
    wide = np.arange(Q)
    first = TWO_PI / P_SIZE * (idx[:, None] * idx[None, :] % P_SIZE)
    second = TWO_PI / Q * (wide[:, None] * idx[None, :] % Q)
    twist = TWO_PI / (P_SIZE * Q) * (idx[:, None] * wide[None, :])

    def narrow(x):
        return x.astype(np.float32).astype(ml_dtypes.bfloat16)

    cos_one, sin_one = narrow(np.cos(first)), narrow(np.sin(first))
    cos_two, sin_two = narrow(np.cos(second)).T, narrow(np.sin(second)).T
    one = np.zeros((2, 2, P_SIZE, P_SIZE, 2), ml_dtypes.bfloat16)
    for pol in range(2):
        one[pol, 0, :, :, pol] = cos_one
        one[pol, 1, :, :, pol] = -sin_one
    two = np.zeros((2, P_SIZE, 2, Q), ml_dtypes.bfloat16)
    two[0, :, 0], two[0, :, 1] = cos_two, sin_two
    two[1, :, 0], two[1, :, 1] = -sin_two, cos_two
    turn = np.stack((np.cos(twist), np.sin(twist))).astype(np.float32)
    return one.reshape(4 * P_SIZE, 2 * P_SIZE), turn, two.reshape(2 * P_SIZE, 2 * Q)


def channel_kernel(volts, taps, one, twist, two, *refs):
    out_lo, out_hi, coeff_rows, folded, turned_re, turned_im, stage = refs[-7:]
    block = pl.program_id(0)
    for pol in range(2):
        for m in range(TAPS):
            coeff_rows[m, pl.ds(pol, 8, stride=2), :] = taps[m]
    coeff = [coeff_rows[m] for m in range(TAPS)]
    row0 = pl.multiple_of(block * 16, 16)
    for chunk in range(FRAMES // FRAME_CHUNK):
        first = chunk * FRAME_CHUNK
        window = [volts[0, first + t].astype(F32) for t in range(FRAME_CHUNK + TAPS - 1)]
        for k in range(FRAME_CHUNK):
            acc = coeff[0] * window[k]
            for m in range(1, TAPS):
                acc = acc + coeff[m] * window[k + m]
            frame = first + k
            lane = frame % 2 * Q
            folded[frame // 2, pl.ds(row0, 16), lane : lane + Q] = acc.astype(BF16)

    def first_section(pair, carry):
        part = jnp.dot(one[...], folded[pair], preferred_element_type=F32)
        for pol in range(2):
            for half in range(2):
                lanes = slice(half * Q, (half + 1) * Q)
                re = part[pol * 128 : pol * 128 + 64, lanes]
                im = part[pol * 128 + 64 : pol * 128 + 128, lanes]
                row = pol * FRAMES + pair * 2 + half
                turned_re[pl.ds(row, 64, stride=TURN_ROWS), :] = re * twist[0] + im * twist[1]
                turned_im[pl.ds(row, 64, stride=TURN_ROWS), :] = im * twist[0] - re * twist[1]
        return carry

    def second_section(j, carry):
        for i in range(16):
            row = pl.multiple_of((j * 16 + i) * TURN_ROWS, 8)
            right = jnp.concatenate(
                (
                    turned_re[pl.ds(row, 128), :].astype(BF16),
                    turned_im[pl.ds(row, 128), :].astype(BF16),
                ),
                axis=1,
            )
            part = lax.dot_general(
                two[...], right, (((1,), (1,)), ((), ())), preferred_element_type=F32
            )
            for ri in range(2):
                rows = pl.ds(ri * 8 + i % 8, 64, stride=STAGE_ROWS)
                stage[i // 8, rows, :] = part[ri * 64 : ri * 64 + 64]
        for b in range(64):
            yh, zh, zl, x = b // 32, b // 8 % 4, b // 4 % 2, b % 4
            rows = slice(b * STAGE_ROWS, b * STAGE_ROWS + 16)
            out_lo[yh, zl, x, j, zh, 0] = stage[0, rows, :].astype(BF16)
            out_hi[yh, zl, x, j, zh, 0] = stage[1, rows, :].astype(BF16)
        return carry

    @pl.when(block == 7)
    def _():
        lax.fori_loop(0, FRAMES // 2, first_section, 0)
        lax.fori_loop(0, 4, second_section, 0)


def whole(*shape):
    return pl.BlockSpec(shape, lambda step: (0,) * len(shape))


def channelize(volts, taps, station, earlier=()):
    one, twist, two = dft_tables()
    out_spec = pl.BlockSpec(
        (2, 2, 4, 4, 4, 1, 16, 128), lambda r: (0, 0, 0, 0, 0, station, 0, 0)
    )
    out_shape = jax.ShapeDtypeStruct((2, 2, 4, 4, 4, 2, 16, 128), BF16)
    return pl.pallas_call(
        channel_kernel,
        grid=(8,),
        in_specs=[
            pl.BlockSpec((1, 75, 16, Q), lambda r: (station, 0, r, 0)),
            pl.BlockSpec((TAPS, 8, Q), lambda r: (0, r, 0)),
            whole(256, 128),
            whole(2, 64, Q),
            whole(128, 256),
        ]
        + [pl.BlockSpec(memory_space=pl.ANY)] * len(earlier),
        out_specs=[out_spec, out_spec],
        out_shape=[out_shape, out_shape],
        input_output_aliases={5: 0, 6: 1} if earlier else {},
        scratch_shapes=[
            pltpu.VMEM((TAPS, 16, Q), F32),
            pltpu.VMEM((FRAMES // 2, 128, 256), BF16),
            pltpu.VMEM((64 * TURN_ROWS, Q), F32),
            pltpu.VMEM((64 * TURN_ROWS, Q), F32),
            pltpu.VMEM((2, 64 * STAGE_ROWS, 128), F32),
        ],
        compiler_params=pltpu.CompilerParams(vmem_limit_bytes=VMEM_LIMIT),
        name="channelize",
    )(volts, taps, jnp.asarray(one), jnp.asarray(twist), jnp.asarray(two), *earlier)


def beam_kernel(spectra, base, step, out, wide):
    for src in range(64):
        wide[src * WIDE_ROWS : src * WIDE_ROWS + 32, :] = spectra[src, 0].astype(F32)
    cos_w, sin_w = base[0, 0], base[0, 1]
    cos_step, sin_step = step[0], step[1]
    for i in range(8):
        right = jnp.concatenate(
            [
                wide[pl.ds(s * 16 + ri * 8 + i, 64, stride=WIDE_ROWS), :].astype(BF16)
                for ri in range(2)
                for s in range(2)
            ],
            axis=0,
        )
        cos_n, sin_n = cos_w.astype(BF16), sin_w.astype(BF16)
        left = jnp.concatenate(
            (
                jnp.concatenate((cos_n, sin_n), axis=1),
                jnp.concatenate((-sin_n, cos_n), axis=1),
            ),
            axis=0,
        )
        part = jnp.dot(left, right, preferred_element_type=F32)
        for ri in range(2):
            for group in range(4):
                row = ri * 64 + group * 16
                out[0, group, ri, i] = part[row : row + 16].astype(BF16)
        if i < 7:
            cos_w, sin_w = (
                cos_w * cos_step - sin_w * sin_step,
                sin_w * cos_step + cos_w * sin_step,
            )


def form_beams(spectra, base, step):
    return pl.pallas_call(
        beam_kernel,
        grid=(4,),
        in_specs=[
            pl.BlockSpec((64, 1, 32, 128), lambda zh: (0, zh, 0, 0)),
            pl.BlockSpec((1, 2, 64, 128), lambda zh: (zh, 0, 0, 0)),
            whole(2, 64, 128),
        ],
        out_specs=pl.BlockSpec((1, 4, 2, 8, 16, 128), lambda zh: (zh, 0, 0, 0, 0, 0)),
        out_shape=jax.ShapeDtypeStruct((4, 4, 2, 8, 16, 128), BF16),
        scratch_shapes=[pltpu.VMEM((64 * WIDE_ROWS, 128), F32)],
        compiler_params=pltpu.CompilerParams(vmem_limit_bytes=VMEM_LIMIT),
        name="form_beams",
    )(spectra, base, step)


def merge_kernel(parts, *refs):
    scale = 1.0 / math.sqrt(P_SIZE * Q * STATIONS)
    for ri, out in enumerate(refs[-2:]):
        for i in range(8):
            total = parts[0, 0, ri, i].astype(F32)
            for zh in range(1, 4):
                total = total + parts[zh, 0, ri, i].astype(F32)
            out[:, i, :] = total * scale


def merge(parts, half, earlier=()):
    spec = pl.BlockSpec((16, 8, 128), lambda j: (0, 2 * j + half, 0))
    shape = jax.ShapeDtypeStruct((16, 64, 128), F32)
    return pl.pallas_call(
        merge_kernel,
        grid=(4,),
        in_specs=[pl.BlockSpec((4, 1, 2, 8, 16, 128), lambda j: (0, j, 0, 0, 0, 0))]
        + [pl.BlockSpec(memory_space=pl.ANY)] * len(earlier),
        out_specs=[spec, spec],
        out_shape=[shape, shape],
        input_output_aliases={1: 0, 2: 1} if earlier else {},
        compiler_params=pltpu.CompilerParams(vmem_limit_bytes=VMEM_LIMIT),
        name="merge",
    )(parts, *earlier)


def station_pick(station_map):
    phys = station_map.reshape(2, 4, 32, 2).transpose(1, 3, 0, 2).reshape(STATIONS)
    return (jnp.arange(STATIONS, dtype=jnp.int32)[:, None] == phys[None, :]).astype(F32)


def pick_columns(values, pick):
    return jnp.dot(values, pick, precision=lax.Precision.HIGHEST)


def on_device(voltages, fir_taps, delays, taper, station_map, beam_order, owners):
    yh, zh, zl, x, yl, c = [lax.axis_index(name) for name in AXES]
    volts = voltages.reshape(2, 2, 75 * P_SIZE, Q).transpose(0, 2, 1, 3).reshape(2, 75, 128, Q)
    taps = fir_taps.reshape(TAPS, P_SIZE, Q)
    slots = delays.shape[1]

    pick = station_pick(station_map)
    model = pick_columns(delays[0], pick).reshape(slots, 4, 128).transpose(1, 0, 2)
    model = jnp.broadcast_to(model[None, :, None], (2, 4, 8, slots, 128))
    models = lax.all_to_all(model.reshape(64, slots, 128), AXES[:4], 0, 0, tiled=True)
    spectra = channelize(volts, taps, 0)
    models, spectra = lax.optimization_barrier((models, spectra))
    delay = lax.dynamic_index_in_dim(models, owners[yl * 2 + c], 0, keepdims=False)
    delay = lax.all_to_all(
        jnp.broadcast_to(delay[None], (4, slots, 128)), ("yl", "c"), 0, 0, tiled=True
    ).reshape(4 * slots, 128)
    spectra = channelize(volts, taps, 1, spectra)
    delay, lo, hi = lax.optimization_barrier((delay, *spectra))

    turned = [
        lax.all_to_all(half.reshape(64, 4, 32, 128), TURN, 0, 0, tiled=True) for half in (lo, hi)
    ]
    gain = pick_columns(taper[beam_order], pick)
    gain = lax.dynamic_slice_in_dim(gain, zh * 128, 128, 1)
    first_chan = yh * 2048 + zl * 256 + x * 64 + (yl * 2 + c) * 16
    unit = TWO_PI / (P_SIZE * Q)
    step = jnp.stack((jnp.cos(delay * unit), jnp.sin(delay * unit)))
    sums = []
    for half in range(2):
        chans = (first_chan + 8 * half + 512 * jnp.arange(4, dtype=jnp.int32)).astype(F32)
        phase = delay[None] * chans[:, None, None] * unit
        base = jnp.stack((gain * jnp.cos(phase), gain * jnp.sin(phase)), axis=1)
        partial = form_beams(turned[half], base, step)
        parts = lax.all_to_all(partial.reshape(16, 2, 8, 16, 128), MERGE, 0, 0, tiled=True)
        sums.append(parts.reshape(4, 4, 2, 8, 16, 128))
    out_re, out_im = merge(sums[1], 1, merge(sums[0], 0))
    return (out_re, out_im)


def solution(mesh):
    torus = Mesh(mesh.devices.reshape(SIZES), AXES)
    stn, beam = AXES[:4], AXES[4:]
    return jax.shard_map(
        on_device,
        mesh=torus,
        in_specs=(P(AXES, None, None), P(), P(stn, beam, None), P(), P(), P(), P()),
        out_specs=(P(beam, stn, None), P(beam, stn, None)),
        check_vma=False,
    )
```

time: 234 us -> 204 us (0.87)
  the two profiles are of different devices: /device:TPU:1 before, /device:TPU:2 now
where the time goes in v2:
time: 204 us; the launch traced here: 203 us
  waiting for transfers between devices  69.3 us (34%)
  Pallas kernels  48.6 us (24%)
  blocking collectives  38 us (19%)
  starting transfers between devices  33.9 us (17%)
  local copies, waits for them, and re-layouts  5.76 us (3%)
  other arithmetic  3.23 us (2%)
  between operations  2.75 us (1%)
    all_to_all x2, waiting for transfers between devices, on_device(): lax.all_to_all(partial.reshape(16, 2, 8, 16, 128), MERGE, 0, 0, tiled=True)  48.8 us
    all_to_all x1, blocking collectives, on_device(): lax.all_to_all(half.reshape(64, 4, 32, 128), TURN, 0, 0, tiled=True)  38 us
    pallas_call x2, Pallas kernels, channelize(): pl.pallas_call(channel_kernel, grid=(8,), in_specs=[pl.BlockSpec((1, 75,...  33.2 us
    all_to_all x1, waiting for transfers between devices, on_device(): lax.all_to_all(half.reshape(64, 4, 32, 128), TURN, 0, 0, tiled=True)  20.5 us
    all_to_all x1, starting transfers between devices, on_device(): lax.all_to_all(model.reshape(64, slots, 128), AXES[:4], 0, 0, tiled=True)  14.6 us
    all_to_all x2, starting transfers between devices, on_device(): lax.all_to_all(partial.reshape(16, 2, 8, 16, 128), MERGE, 0, 0, tiled=True)  9.83 us
    pallas_call x2, Pallas kernels, form_beams(): pl.pallas_call(beam_kernel, grid=(4,), in_specs=[pl.BlockSpec((64, 1, 32,...  8.69 us
    pallas_call x2, Pallas kernels, merge(): pl.pallas_call(merge_kernel, grid=(4,), in_specs=[pl.BlockSpec((4, 1, 2,...  6.76 us
  transfers between devices with their start and end apart: 5, of which 3 were waited for; matrix products, arithmetic and copies ran while one was open for 3% of the time, Pallas kernels for 22%

profile of v2, /device:TPU:2, one launch (start us, length us, event | category | flops | bytes accessed | tf_op | source)
XLA Modules:
  0.0 203.3 jit_solution(10821117112268215920)
XLA Ops:
  0.7 0.9 reshape.93
  1.6 0.1 copy.21
  1.7 0.1 eq.16
  1.8 1.2 convolution_bitcast_fusion
  3.0 0.8 broadcast_in_dim.8
  3.8 14.6 %all-to-all-start = ((f32[64,16,128]{2,1,0:T(8,128)}), f32[64,16,128]{2,1,0:T(8,128)S(1)}, u32[]{:S(2)}, u32[]{:S(2)}) async-start(f32[64,16,128]{2,1,0:T(8,128)} %bitcast.4), calls=%async_computation | async-start | bytes 1048576 | tf_op jit(solution)/shard_map/all_to_all | solution.py:248
  18.5 0.6 dynamic_slice.10
  20.4 0.1 copy.24
  20.5 0.8 slice.2.taps
  21.9 16.6 %channelize.2 = (bf16[2,2,4,4,4,2,16,128]{7,6,5,4,3,2,1,0:T(8,128)(2,1)}, bf16[2,2,4,4,4,2,16,128]{7,6,5,4,3,2,1,0:T(8,128)(2,1)}) custom-call(bf16[2,75,128,128]{3,2,1,0:T(8,128)(2,1)} %bitcast.31, f32[12,64,128]{2,1,0:T(8,128)} %slice.2.taps, bf16[256,128]{1,0:T(8,128)(2,1)} %constant.59.clone.one, f32[2,64,128]{2,1,0:T(8,128)} %constant.60.clone.twist, ...), custom_call_target="tpu_custom_call" | custom-call | tf_op jit(solution)/shard_map/channelize/pallas_call | solution.py:127
  38.5 0.6 broadcast_in_dim.10
  39.1 3.3 %all-to-all-start.1 = ((f32[4,16,128]{2,1,0:T(8,128)}), f32[4,16,128]{2,1,0:T(8,128)S(1)}, u32[]{:S(2)}, u32[]{:S(2)}) async-start(f32[4,16,128]{2,1,0:T(8,128)} %broadcast_in_dim.10), calls=%async_computation.1 | async-start | bytes 65536 | tf_op jit(solution)/shard_map/all_to_all | solution.py:252
  42.4 16.6 %channelize.3 = (bf16[2,2,4,4,4,2,16,128]{7,6,5,4,3,2,1,0:T(8,128)(2,1)}, bf16[2,2,4,4,4,2,16,128]{7,6,5,4,3,2,1,0:T(8,128)(2,1)}) custom-call(bf16[2,75,128,128]{3,2,1,0:T(8,128)(2,1)} %bitcast.32, f32[12,64,128]{2,1,0:T(8,128)} %slice.2.taps, bf16[256,128]{1,0:T(8,128)(2,1)} %constant.59.clone.one, ...), custom_call_target="tpu_custom_call", output_to_operand_aliasing={{0}: (5, {}), {1}: (6, {})} | custom-call | tf_op jit(solution)/shard_map/channelize/pallas_call | solution.py:127
  59.0 38.0 %all_to_all.30.spectra = bf16[64,4,32,128]{3,2,1,0:T(8,128)(2,1)} all-to-all(bf16[64,4,32,128]{3,2,1,0:T(8,128)(2,1)} %bitcast.33), channel_id=1, replica_groups=mesh['yh'=2,'zh'=4,'zl'=2,'x'=4,'yl'=2,'c'=2] {'yh','zl','x','yl','c'}, dimensions={0} | all-to-all | bytes 4194304 | tf_op jit(solution)/shard_map/all_to_all | solution.py:259
  97.0 6.2 %all-to-all-start.2 = ((bf16[64,4,32,128]{3,2,1,0:T(8,128)(2,1)}), bf16[64,4,32,128]{3,2,1,0:T(8,128)(2,1)S(1)}, u32[]{:S(2)}, u32[]{:S(2)}) async-start(bf16[64,4,32,128]{3,2,1,0:T(8,128)(2,1)} %bitcast.13), calls=%async_computation.2 | async-start | bytes 4194304 | tf_op jit(solution)/shard_map/all_to_all | solution.py:259
  103.2 0.7 gather_fusion
  103.9 0.5 fusion
  104.4 0.1 cosine_bitcast_fusion
  104.6 0.6 pad_maximum_fusion.2.step
  105.2 1.0 cosine_multiply_fusion
  106.2 0.7 pad_maximum_fusion.1.base
  106.9 4.3 %form_beams.3 = bf16[4,4,2,8,16,128]{5,4,3,2,1,0:T(8,128)(2,1)} custom-call(bf16[64,4,32,128]{3,2,1,0:T(8,128)(2,1)} %all_to_all.30.spectra, f32[4,2,64,128]{3,2,1,0:T(8,128)} %pad_maximum_fusion.1.base, f32[2,64,128]{2,1,0:T(8,128)} %pad_maximum_fusion.2.step), custom_call_target="tpu_custom_call" | custom-call | tf_op jit(solution)/shard_map/form_beams/pallas_call | solution.py:188
  111.3 20.5 %all-to-all-done.2.spectra = bf16[64,4,32,128]{3,2,1,0:T(8,128)(2,1)S(1)} async-done(((bf16[64,4,32,128]{3,2,1,0:T(8,128)(2,1)}), bf16[64,4,32,128]{3,2,1,0:T(8,128)(2,1)S(1)}, u32[]{:S(2)}, u32[]{:S(2)}) %all-to-all-start.2) | async-done | bytes 2097184 | tf_op jit(solution)/shard_map/all_to_all | solution.py:259
  131.8 6.0 %all-to-all-start.5 = ((bf16[16,2,8,16,128]{4,3,2,1,0:T(8,128)(2,1)}), bf16[16,2,8,16,128]{4,3,2,1,0:T(8,128)(2,1)S(1)}, u32[]{:S(2)}, u32[]{:S(2)}) async-start(bf16[16,2,8,16,128]{4,3,2,1,0:T(8,128)(2,1)} %bitcast.35), calls=%async_computation.5 | async-start | bytes 2097152 | tf_op jit(solution)/shard_map/all_to_all | solution.py:272
  137.7 0.7 pad_maximum_fusion.base
  138.5 4.3 %form_beams.2 = bf16[4,4,2,8,16,128]{5,4,3,2,1,0:T(8,128)(2,1)} custom-call(bf16[64,4,32,128]{3,2,1,0:T(8,128)(2,1)} %copy-done.1, f32[4,2,64,128]{3,2,1,0:T(8,128)} %pad_maximum_fusion.base, f32[2,64,128]{2,1,0:T(8,128)} %pad_maximum_fusion.2.step), custom_call_target="tpu_custom_call" | custom-call | tf_op jit(solution)/shard_map/form_beams/pallas_call | solution.py:188
  142.8 23.5 %all-to-all-done.5 = bf16[16,2,8,16,128]{4,3,2,1,0:T(8,128)(2,1)S(1)} async-done(((bf16[16,2,8,16,128]{4,3,2,1,0:T(8,128)(2,1)}), bf16[16,2,8,16,128]{4,3,2,1,0:T(8,128)(2,1)S(1)}, u32[]{:S(2)}, u32[]{:S(2)}) %all-to-all-start.5) | async-done | bytes 1048608 | tf_op jit(solution)/shard_map/all_to_all | solution.py:272
  166.4 3.9 %all-to-all-start.3 = ((bf16[16,2,8,16,128]{4,3,2,1,0:T(8,128)(2,1)}), bf16[16,2,8,16,128]{4,3,2,1,0:T(8,128)(2,1)S(1)}, u32[]{:S(2)}, u32[]{:S(2)}) async-start(bf16[16,2,8,16,128]{4,3,2,1,0:T(8,128)(2,1)} %bitcast.36), calls=%async_computation.3 | async-start | bytes 2097152 | tf_op jit(solution)/shard_map/all_to_all | solution.py:272
  170.2 3.4 %merge.2 = (f32[16,64,128]{2,1,0:T(8,128)}, f32[16,64,128]{2,1,0:T(8,128)}) custom-call(bf16[4,4,2,8,16,128]{5,4,3,2,1,0:T(8,128)(2,1)} %bitcast.34), custom_call_target="tpu_custom_call" | custom-call | tf_op jit(solution)/shard_map/merge/pallas_call | solution.py:217
  173.6 25.3 %all-to-all-done.3 = bf16[16,2,8,16,128]{4,3,2,1,0:T(8,128)(2,1)S(1)} async-done(((bf16[16,2,8,16,128]{4,3,2,1,0:T(8,128)(2,1)}), bf16[16,2,8,16,128]{4,3,2,1,0:T(8,128)(2,1)S(1)}, u32[]{:S(2)}, u32[]{:S(2)}) %all-to-all-start.3) | async-done | bytes 1048608 | tf_op jit(solution)/shard_map/all_to_all | solution.py:272
  198.9 1.0 copy-done.3
  199.9 3.4 %merge.3 = (f32[16,64,128]{2,1,0:T(8,128)}, f32[16,64,128]{2,1,0:T(8,128)}) custom-call(bf16[4,4,2,8,16,128]{5,4,3,2,1,0:T(8,128)(2,1)} %bitcast.37, f32[16,64,128]{2,1,0:T(8,128)} %get-tuple-element.24.refs_0_, f32[16,64,128]{2,1,0:T(8,128)} %get-tuple-element.25.refs_1_), custom_call_target="tpu_custom_call", output_to_operand_aliasing={{0}: (1, {}), {1}: (2, {})} | custom-call | tf_op jit(solution)/shard_map/merge/pallas_call | solution.py:217
  (22 shorter events, 0.1 us)
Async XLA Ops:
  0.6 102.6 %copy-start = (f32[64,512]{1,0:T(8,128)S(1)}, f32[64,512]{1,0:T(8,128)}, u32[]{:S(2)}) copy-start(f32[64,512]{1,0:T(8,128)} %param.16) | copy-start | bytes 393220
  0.6 17.8 %copy-start.5 = (s32[4]{0:T(128)S(1)}, s32[4]{0:T(128)}, u32[]{:S(2)}) copy-start(s32[4]{0:T(128)} %param.19) | copy-start | bytes 52
  0.7 19.7 %copy-start.4 = (f32[12,8192]{1,0:T(8,128)S(1)}, f32[12,8192]{1,0:T(8,128)}, u32[]{:S(2)}) copy-start(f32[12,8192]{1,0:T(8,128)} %param.14) | copy-start | bytes 1179652
  3.8 34.7 %all-to-all-start = ((f32[64,16,128]{2,1,0:T(8,128)}), f32[64,16,128]{2,1,0:T(8,128)S(1)}, u32[]{:S(2)}, u32[]{:S(2)}) async-start(f32[64,16,128]{2,1,0:T(8,128)} %bitcast.4), calls=%async_computation | async-start | bytes 1048576 | tf_op jit(solution)/shard_map/all_to_all | solution.py:248
  39.1 19.8 %all-to-all-start.1 = ((f32[4,16,128]{2,1,0:T(8,128)}), f32[4,16,128]{2,1,0:T(8,128)S(1)}, u32[]{:S(2)}, u32[]{:S(2)}) async-start(f32[4,16,128]{2,1,0:T(8,128)} %broadcast_in_dim.10), calls=%async_computation.1 | async-start | bytes 65536 | tf_op jit(solution)/shard_map/all_to_all | solution.py:252
  97.0 6.2 %copy-start.6 = (s32[64]{0:T(128)S(1)}, s32[64]{0:T(128)}, u32[]{:S(2)}) copy-start(s32[64]{0:T(128)} %param.18) | copy-start | bytes 772
  97.0 34.8 %all-to-all-start.2 = ((bf16[64,4,32,128]{3,2,1,0:T(8,128)(2,1)}), bf16[64,4,32,128]{3,2,1,0:T(8,128)(2,1)S(1)}, u32[]{:S(2)}, u32[]{:S(2)}) async-start(bf16[64,4,32,128]{3,2,1,0:T(8,128)(2,1)} %bitcast.13), calls=%async_computation.2 | async-start | bytes 4194304 | tf_op jit(solution)/shard_map/all_to_all | solution.py:259
  131.8 6.7 %copy-start.1 = (bf16[64,4,32,128]{3,2,1,0:T(8,128)(2,1)}, bf16[64,4,32,128]{3,2,1,0:T(8,128)(2,1)S(1)}, u32[]{:S(2)}) copy-start(bf16[64,4,32,128]{3,2,1,0:T(8,128)(2,1)S(1)} %all-to-all-done.2.spectra) | copy-start | bytes 6291460
  131.8 34.6 %all-to-all-start.5 = ((bf16[16,2,8,16,128]{4,3,2,1,0:T(8,128)(2,1)}), bf16[16,2,8,16,128]{4,3,2,1,0:T(8,128)(2,1)S(1)}, u32[]{:S(2)}, u32[]{:S(2)}) async-start(bf16[16,2,8,16,128]{4,3,2,1,0:T(8,128)(2,1)} %bitcast.35), calls=%async_computation.5 | async-start | bytes 2097152 | tf_op jit(solution)/shard_map/all_to_all | solution.py:272
  166.4 3.9 %copy-start.2 = (bf16[16,2,8,16,128]{4,3,2,1,0:T(8,128)(2,1)}, bf16[16,2,8,16,128]{4,3,2,1,0:T(8,128)(2,1)S(1)}, u32[]{:S(2)}) copy-start(bf16[16,2,8,16,128]{4,3,2,1,0:T(8,128)(2,1)S(1)} %all-to-all-done.5) | copy-start | bytes 3145732
  166.4 32.5 %all-to-all-start.3 = ((bf16[16,2,8,16,128]{4,3,2,1,0:T(8,128)(2,1)}), bf16[16,2,8,16,128]{4,3,2,1,0:T(8,128)(2,1)S(1)}, u32[]{:S(2)}, u32[]{:S(2)}) async-start(bf16[16,2,8,16,128]{4,3,2,1,0:T(8,128)(2,1)} %bitcast.36), calls=%async_computation.3 | async-start | bytes 2097152 | tf_op jit(solution)/shard_map/all_to_all | solution.py:272
  198.9 1.0 copy-start.3

commit v3 on v2

v3 whole, which is shorter than its diff:
```python
import math

import jax
import jax.numpy as jnp
import ml_dtypes
import numpy as np
from jax import lax
from jax.experimental import pallas as pl
from jax.experimental.pallas import tpu as pltpu
from jax.sharding import Mesh
from jax.sharding import PartitionSpec as P

P_SIZE = 64
Q = 128
CHANNELS = 4096
TAPS = 12
FRAMES = 64
STATIONS = 512
TWO_PI = 2.0 * math.pi
F32 = jnp.float32
BF16 = jnp.bfloat16
VMEM_LIMIT = 56 << 20

AXES = ("yh", "zh", "zl", "x", "yl", "c")
SIZES = (2, 4, 2, 4, 2, 2)
TURN = ("yh", "zl", "x", "yl", "c")
FRAME_CHUNK = 16
TURN_ROWS = 136
STAGE_ROWS = 40
WIDE_ROWS = 72
BEAM_ROWS = 24


def dft_tables():
    idx = np.arange(P_SIZE)
    wide = np.arange(Q)
    first = TWO_PI / P_SIZE * (idx[:, None] * idx[None, :] % P_SIZE)
    second = TWO_PI / Q * (wide[:, None] * idx[None, :] % Q)
    twist = TWO_PI / (P_SIZE * Q) * (idx[:, None] * wide[None, :])

    def narrow(x):
        return x.astype(np.float32).astype(ml_dtypes.bfloat16)

    cos_one, sin_one = narrow(np.cos(first)), narrow(np.sin(first))
    cos_two, sin_two = narrow(np.cos(second)).T, narrow(np.sin(second)).T
    one = np.zeros((2, 2, P_SIZE, P_SIZE, 2), ml_dtypes.bfloat16)
    for pol in range(2):
        one[pol, 0, :, :, pol] = cos_one
        one[pol, 1, :, :, pol] = -sin_one
    two = np.zeros((2, P_SIZE, 2, Q), ml_dtypes.bfloat16)
    two[0, :, 0], two[0, :, 1] = cos_two, sin_two
    two[1, :, 0], two[1, :, 1] = -sin_two, cos_two
    turn = np.stack((np.cos(twist), np.sin(twist))).astype(np.float32)
    return one.reshape(4 * P_SIZE, 2 * P_SIZE), turn, two.reshape(2 * P_SIZE, 2 * Q)


def channel_kernel(
    volts, taps, one, twist, two, out, coeff_rows, folded, turned_re, turned_im, stage
):
    block = pl.program_id(1)
    for pol in range(2):
        for m in range(TAPS):
            coeff_rows[m, pl.ds(pol, 8, stride=2), :] = taps[m]
    coeff = [coeff_rows[m] for m in range(TAPS)]
    row0 = pl.multiple_of(block * 16, 16)
    for chunk in range(FRAMES // FRAME_CHUNK):
        first = chunk * FRAME_CHUNK
        window = [volts[0, first + t].astype(F32) for t in range(FRAME_CHUNK + TAPS - 1)]
        for k in range(FRAME_CHUNK):
            acc = coeff[0] * window[k]
            for m in range(1, TAPS):
                acc = acc + coeff[m] * window[k + m]
            frame = first + k
            lane = frame % 2 * Q
            folded[frame // 2, pl.ds(row0, 16), lane : lane + Q] = acc.astype(BF16)

    def first_section(pair, carry):
        part = jnp.dot(one[...], folded[pair], preferred_element_type=F32)
        for pol in range(2):
            for half in range(2):
                lanes = slice(half * Q, (half + 1) * Q)
                re = part[pol * 128 : pol * 128 + 64, lanes]
                im = part[pol * 128 + 64 : pol * 128 + 128, lanes]
                row = pol * FRAMES + pair * 2 + half
                turned_re[pl.ds(row, 64, stride=TURN_ROWS), :] = re * twist[0] + im * twist[1]
                turned_im[pl.ds(row, 64, stride=TURN_ROWS), :] = im * twist[0] - re * twist[1]
        return carry

    def second_section(j, carry):
        for i in range(16):
            row = pl.multiple_of((j * 16 + i) * TURN_ROWS, 8)
            right = jnp.concatenate(
                (
                    turned_re[pl.ds(row, 128), :].astype(BF16),
                    turned_im[pl.ds(row, 128), :].astype(BF16),
                ),
                axis=1,
            )
            part = lax.dot_general(
                two[...], right, (((1,), (1,)), ((), ())), preferred_element_type=F32
            )
            for ri in range(2):
                rows = pl.ds(ri * 16 + i, 64, stride=STAGE_ROWS)
                stage[rows, :] = part[ri * 64 : ri * 64 + 64]
        for b in range(64):
            yh, zh, zl, x = b // 32, b // 8 % 4, b // 4 % 2, b % 4
            rows = slice(b * STAGE_ROWS, b * STAGE_ROWS + 32)
            out[yh, zl, x, j, zh, 0] = stage[rows, :].astype(BF16)
        return carry

    @pl.when(block == 7)
    def _():
        lax.fori_loop(0, FRAMES // 2, first_section, 0)
        lax.fori_loop(0, 4, second_section, 0)


def whole(*shape):
    return pl.BlockSpec(shape, lambda *step: (0,) * len(shape))


def channelize(volts, taps):
    one, twist, two = dft_tables()
    return pl.pallas_call(
        channel_kernel,
        grid=(2, 8),
        in_specs=[
            pl.BlockSpec((1, 75, 16, Q), lambda s, r: (s, 0, r, 0)),
            pl.BlockSpec((TAPS, 8, Q), lambda s, r: (0, r, 0)),
            whole(256, 128),
            whole(2, 64, Q),
            whole(128, 256),
        ],
        out_specs=pl.BlockSpec((2, 2, 4, 4, 4, 1, 32, 128), lambda s, r: (0, 0, 0, 0, 0, s, 0, 0)),
        out_shape=jax.ShapeDtypeStruct((2, 2, 4, 4, 4, 2, 32, 128), BF16),
        scratch_shapes=[
            pltpu.VMEM((TAPS, 16, Q), F32),
            pltpu.VMEM((FRAMES // 2, 128, 256), BF16),
            pltpu.VMEM((64 * TURN_ROWS, Q), F32),
            pltpu.VMEM((64 * TURN_ROWS, Q), F32),
            pltpu.VMEM((64 * STAGE_ROWS, 128), F32),
        ],
        compiler_params=pltpu.CompilerParams(vmem_limit_bytes=VMEM_LIMIT),
        name="channelize",
    )(volts, taps, jnp.asarray(one), jnp.asarray(twist), jnp.asarray(two))


def beam_kernel(where, spectra, base, step, out, wide):
    del where
    for src in range(64):
        wide[src * WIDE_ROWS : src * WIDE_ROWS + 64, :] = spectra[src, 0].astype(F32)
    cos_w, sin_w = base[0], base[1]
    cos_step, sin_step = step[0], step[1]
    for i in range(16):
        right = jnp.concatenate(
            [
                wide[pl.ds(s * 32 + ri * 16 + i, 64, stride=WIDE_ROWS), :].astype(BF16)
                for ri in range(2)
                for s in range(2)
            ],
            axis=0,
        )
        cos_n, sin_n = cos_w.astype(BF16), sin_w.astype(BF16)
        left = jnp.concatenate(
            (
                jnp.concatenate((cos_n, sin_n), axis=1),
                jnp.concatenate((-sin_n, cos_n), axis=1),
            ),
            axis=0,
        )
        part = jnp.dot(left, right, preferred_element_type=F32)
        for ri in range(2):
            for group in range(4):
                row = ri * 64 + group * 16
                out[group, ri, i] = part[row : row + 16].astype(BF16)
        if i < 15:
            cos_w, sin_w = (
                cos_w * cos_step - sin_w * sin_step,
                sin_w * cos_step + cos_w * sin_step,
            )


def form_beams(where, spectra, base, step):
    return pl.pallas_call(
        beam_kernel,
        grid_spec=pltpu.PrefetchScalarGridSpec(
            num_scalar_prefetch=1,
            grid=(1,),
            in_specs=[
                pl.BlockSpec((64, 1, 64, 128), lambda n, zh: (0, zh[0], 0, 0)),
                whole(2, 64, 128),
                whole(2, 64, 128),
            ],
            out_specs=whole(4, 2, 16, 16, 128),
            scratch_shapes=[pltpu.VMEM((64 * WIDE_ROWS, 128), F32)],
        ),
        out_shape=jax.ShapeDtypeStruct((4, 2, 16, 16, 128), BF16),
        compiler_params=pltpu.CompilerParams(vmem_limit_bytes=VMEM_LIMIT),
        name="form_beams",
    )(where, spectra, base, step)


def add_kernel(group, *refs):
    del group
    total = refs[0][0].astype(F32)
    for part in refs[1:-1]:
        total = total + part[0].astype(F32)
    refs[-1][...] = total.astype(BF16)


def add_group(group, parts):
    part_spec = pl.BlockSpec((1, 2, 16, 16, 128), lambda n, g: (g[0], 0, 0, 0, 0))
    return pl.pallas_call(
        add_kernel,
        grid_spec=pltpu.PrefetchScalarGridSpec(
            num_scalar_prefetch=1,
            grid=(1,),
            in_specs=[part_spec] * len(parts),
            out_specs=whole(2, 16, 16, 128),
        ),
        out_shape=jax.ShapeDtypeStruct((2, 16, 16, 128), BF16),
        compiler_params=pltpu.CompilerParams(vmem_limit_bytes=VMEM_LIMIT),
        name="add_group",
    )(group, *parts)


def merge_kernel(order, *refs):
    del order
    parts, outs, stage = refs[:4], refs[4:6], refs[6]
    scale = 1.0 / math.sqrt(P_SIZE * Q * STATIONS)
    for n, part in enumerate(parts):

        @pl.when(pl.program_id(0) == n)
        def _(part=part):
            for ri in range(2):
                for i in range(16):
                    stage[ri, pl.ds(i, 16, stride=BEAM_ROWS), :] = part[ri, i].astype(F32) * scale
                for beam in range(16):
                    row = beam * BEAM_ROWS
                    outs[ri][beam] = stage[ri, row : row + 16, :]


def merge(order, parts):
    spec = pl.BlockSpec((16, 16, 128), lambda n, order: (0, order[n], 0))
    shape = jax.ShapeDtypeStruct((16, 64, 128), F32)
    return pl.pallas_call(
        merge_kernel,
        grid_spec=pltpu.PrefetchScalarGridSpec(
            num_scalar_prefetch=1,
            grid=(4,),
            in_specs=[whole(2, 16, 16, 128)] * 4,
            out_specs=[spec, spec],
            scratch_shapes=[pltpu.VMEM((2, 16 * BEAM_ROWS, 128), F32)],
        ),
        out_shape=[shape, shape],
        compiler_params=pltpu.CompilerParams(vmem_limit_bytes=VMEM_LIMIT),
        name="merge",
    )(order, *parts)


def swap_beam(value, offset):
    return lax.ppermute(value, ("yl", "c"), [(b, b ^ offset) for b in range(4)])


def station_pick(station_map):
    phys = station_map.reshape(2, 4, 32, 2).transpose(1, 3, 0, 2).reshape(STATIONS)
    return (jnp.arange(STATIONS, dtype=jnp.int32)[:, None] == phys[None, :]).astype(F32)


def pick_columns(values, pick):
    return jnp.dot(values, pick, precision=lax.Precision.HIGHEST)


def on_device(voltages, fir_taps, delays, taper, station_map, beam_order, owners):
    yh, zh, zl, x, yl, c = [lax.axis_index(name) for name in AXES]
    volts = voltages.reshape(2, 2, 75 * P_SIZE, Q).transpose(0, 2, 1, 3).reshape(2, 75, 128, Q)
    taps = fir_taps.reshape(TAPS, P_SIZE, Q)
    slots = delays.shape[1]
    stn_pos = ((yh * 4 + zh) * 2 + zl) * 4 + x
    beam_pos = yl * 2 + c
    owner = owners[beam_pos]

    pick = station_pick(station_map)
    kept = jnp.where(owner == stn_pos, delays[0], 0.0)
    model = pick_columns(kept, pick).reshape(slots, 4, 128).transpose(1, 0, 2)
    model = lax.psum_scatter(model, "zh", scatter_dimension=0, tiled=False)
    spectra = channelize(volts, taps)
    model, spectra = lax.optimization_barrier((model, spectra))
    models = lax.all_to_all(
        jnp.broadcast_to(model[None], (16, slots, 128)), ("yh", "zl", "x"), 0, 0, tiled=True
    )
    source = (owner // 32 * 2 + owner // 4 % 2) * 4 + owner % 4
    delay = lax.dynamic_index_in_dim(models, source, 0, keepdims=False)
    delay, spectra = lax.optimization_barrier((delay, spectra))
    delays_by_offset = [delay] + [swap_beam(delay, n) for n in range(1, 4)]
    turned = lax.all_to_all(spectra.reshape(64, 4, 64, 128), TURN, 0, 0, tiled=True)

    delay = jnp.stack(delays_by_offset)
    delay = jnp.where(beam_pos % 2 == 1, delay[jnp.array((1, 0, 3, 2))], delay)
    delay = jnp.where(beam_pos // 2 == 1, delay[jnp.array((2, 3, 0, 1))], delay)
    delay = delay.reshape(4 * slots, 128)
    gain = pick_columns(taper[beam_order], pick)
    gain = lax.dynamic_slice_in_dim(gain, zh * 128, 128, 1)
    first_chan = yh * 2048 + zl * 256 + x * 64 + beam_pos * 16
    unit = TWO_PI / (P_SIZE * Q)
    step = jnp.stack((jnp.cos(delay * unit), jnp.sin(delay * unit)))
    parts = []
    for dz in (2, 1, 3, 0):
        target = (zh + dz) % 4
        phase = delay * (first_chan + 512 * target).astype(F32) * unit
        base = jnp.stack((gain * jnp.cos(phase), gain * jnp.sin(phase)))
        part = form_beams(target[None], turned, base, step)
        if dz:
            part = lax.ppermute(part, "zh", [(z, (z + dz) % 4) for z in range(4)])
        parts.append(part)
    order = beam_pos ^ jnp.arange(4, dtype=jnp.int32)
    quarters = [add_group(order[n : n + 1], parts) for n in (2, 3, 1, 0)]
    quarters = [swap_beam(q, n) if n else q for q, n in zip(quarters, (2, 3, 1, 0))]
    out_re, out_im = merge(order[jnp.array((2, 3, 1, 0))], quarters)
    return (out_re, out_im)


def solution(mesh):
    torus = Mesh(mesh.devices.reshape(SIZES), AXES)
    stn, beam = AXES[:4], AXES[4:]
    return jax.shard_map(
        on_device,
        mesh=torus,
        in_specs=(P(AXES, None, None), P(), P(stn, beam, None), P(), P(), P(), P()),
        out_specs=(P(beam, stn, None), P(beam, stn, None)),
        check_vma=False,
    )
```

time: 204 us -> 208 us (1.020)
  the two profiles are of different devices: /device:TPU:2 before, /device:TPU:1 now
where the time goes in v3:
time: 208 us; the launch traced here: 206 us
  waiting for transfers between devices  85.3 us (41%)
  Pallas kernels  55.9 us (27%)
  starting transfers between devices  31.2 us (15%)
  between operations  17.4 us (8%)
  local copies, waits for them, and re-layouts  11.2 us (5%)
  other arithmetic  3.53 us (2%)
    ppermute x6, waiting for transfers between devices, swap_beam(): return lax.ppermute(value, ('yl', 'c'), [(b, b ^ offset) for b in range(4)])  44.9 us
    ppermute x3, waiting for transfers between devices, on_device(): part = lax.ppermute(part, 'zh', [(z, (z + dz) % 4) for z in range(4)])  34.7 us
    pallas_call x1, Pallas kernels, channelize(): pl.pallas_call(channel_kernel, grid=(2, 8), in_specs=[pl.BlockSpec((1, 75...  31.7 us
    pallas_call x4, Pallas kernels, form_beams(): pl.pallas_call(beam_kernel, grid_spec=pltpu.PrefetchScalarGridSpec(num_sc...  11.2 us
    pallas_call x4, Pallas kernels, add_group(): pl.pallas_call(add_kernel, grid_spec=pltpu.PrefetchScalarGridSpec(num_sca...  9.62 us
    ppermute x3, starting transfers between devices, on_device(): part = lax.ppermute(part, 'zh', [(z, (z + dz) % 4) for z in range(4)])  9.58 us
    all_to_all x1, starting transfers between devices, on_device(): lax.all_to_all(jnp.broadcast_to(model[None], (16, slots, 128)), ('yh', 'z...  8.94 us
    all_to_all x1, starting transfers between devices, on_device(): lax.all_to_all(spectra.reshape(64, 4, 64, 128), TURN, 0, 0, tiled=True)  7.17 us
  transfers between devices with their start and end apart: 12, of which 5 were waited for; matrix products, arithmetic and copies ran while one was open for 4% of the time, Pallas kernels for 23%

profile of v3, /device:TPU:1, one launch (start us, length us, event | category | flops | bytes accessed | tf_op | source)
XLA Modules:
  0.0 206.3 jit_solution(13395703990201445536)
XLA Ops:
  7.2 0.8 reshape.131
  8.5 1.3 dynamic_slice.10
  10.4 1.2 convolution_bitcast_fusion
  11.6 1.1 copy.18
  12.7 0.8 slice.24.taps
  13.5 31.7 %channelize.1 = bf16[2,2,4,4,4,2,32,128]{7,6,5,4,3,2,1,0:T(8,128)(2,1)} custom-call(bf16[2,75,128,128]{3,2,1,0:T(8,128)(2,1)} %bitcast.58, f32[12,64,128]{2,1,0:T(8,128)} %slice.24.taps, bf16[256,128]{1,0:T(8,128)(2,1)} %constant.135.clone.one, f32[2,64,128]{2,1,0:T(8,128)} %constant.136.clone.twist, bf16[128,256]{1,0:T(8,128)(2,1)} %constant.137.clone.two), custom_call_target="tpu_custom_call" | custom-call | tf_op jit(solution)/shard_map/channelize/pallas_call | solution.py:123
  45.2 1.4 broadcast_in_dim.38
  46.6 8.9 %all-to-all-start = ((f32[16,16,128]{2,1,0:T(8,128)}), f32[16,16,128]{2,1,0:T(8,128)S(1)}, u32[]{:S(2)}, u32[]{:S(2)}) async-start(f32[16,16,128]{2,1,0:T(8,128)} %broadcast_in_dim.38), calls=%async_computation.1 | async-start | bytes 262144 | tf_op jit(solution)/shard_map/all_to_all | solution.py:288
  58.0 5.6 %all-to-all-done = f32[16,16,128]{2,1,0:T(8,128)S(1)} async-done(((f32[16,16,128]{2,1,0:T(8,128)}), f32[16,16,128]{2,1,0:T(8,128)S(1)}, u32[]{:S(2)}, u32[]{:S(2)}) %all-to-all-start) | async-done | bytes 131104 | tf_op jit(solution)/shard_map/all_to_all | solution.py:288
  63.7 7.2 %all-to-all-start.1 = ((bf16[64,4,64,128]{3,2,1,0:T(8,128)(2,1)}), bf16[64,4,64,128]{3,2,1,0:T(8,128)(2,1)}, u32[]{:S(2)}, u32[]{:S(2)}) async-start(bf16[64,4,64,128]{3,2,1,0:T(8,128)(2,1)} %bitcast.57), calls=%async_computation.2 | async-start | bytes 8388608 | tf_op jit(solution)/shard_map/all_to_all | solution.py:295
  70.9 0.7 gather_fusion.1
  72.1 1.7 collective-permute-start.2
  74.4 44.9 %collective-permute-done.2 = f32[16,128]{1,0:T(8,128)S(1)} collective-permute-done((f32[16,128]{1,0:T(8,128)S(1)}, f32[16,128]{1,0:T(8,128)S(1)}, u32[]{:S(2)}, u32[]{:S(2)}) %collective-permute-start.2) | collective-permute-done | bytes 8224 | tf_op jit(solution)/shard_map/ppermute | solution.py:261
  122.5 0.6 pad_maximum_fusion
  123.1 2.8 %form_beams.4 = bf16[4,2,16,16,128]{4,3,2,1,0:T(8,128)(2,1)} custom-call(s32[1]{0:T(128)} %bitcast.where, bf16[64,4,64,128]{3,2,1,0:T(8,128)(2,1)} %all-to-all-done.1.spectra, f32[2,64,128]{2,1,0:T(8,128)} %get-tuple-element.33.base, f32[2,64,128]{2,1,0:T(8,128)} %get-tuple-element.34.step), custom_call_target="tpu_custom_call" | custom-call | tf_op jit(solution)/shard_map/form_beams/pallas_call | solution.py:183
  125.9 6.0 %collective-permute-start.3 = (bf16[4,2,16,16,128]{4,3,2,1,0:T(8,128)(2,1)}, bf16[4,2,16,16,128]{4,3,2,1,0:T(8,128)(2,1)S(1)}, u32[]{:S(2)}, u32[]{:S(2)}) collective-permute-start(bf16[4,2,16,16,128]{4,3,2,1,0:T(8,128)(2,1)} %form_beams.4), channel_id=1, source_target_pairs={{0,64},{32,96},{64,0},{96,32},{1,65},{33,97},{65,1},{97,33},{2,66}... | collective-permute-start | bytes 1572872 | tf_op jit(solution)/shard_map/ppermute | solution.py:313
  131.9 2.8 %form_beams.5 = bf16[4,2,16,16,128]{4,3,2,1,0:T(8,128)(2,1)} custom-call(s32[1]{0:T(128)} %bitcast.23.where, bf16[64,4,64,128]{3,2,1,0:T(8,128)(2,1)} %all-to-all-done.1.spectra, f32[2,64,128]{2,1,0:T(8,128)} %pad_maximum_fusion.2.base, f32[2,64,128]{2,1,0:T(8,128)} %get-tuple-element.34.step), custom_call_target="tpu_custom_call" | custom-call | tf_op jit(solution)/shard_map/form_beams/pallas_call | solution.py:183
  134.7 1.2 collective-permute-start.4
  135.9 2.8 %form_beams.6 = bf16[4,2,16,16,128]{4,3,2,1,0:T(8,128)(2,1)} custom-call(s32[1]{0:T(128)} %bitcast.28.where, bf16[64,4,64,128]{3,2,1,0:T(8,128)(2,1)} %all-to-all-done.1.spectra, f32[2,64,128]{2,1,0:T(8,128)} %pad_maximum_fusion.3.base, f32[2,64,128]{2,1,0:T(8,128)} %get-tuple-element.34.step), custom_call_target="tpu_custom_call" | custom-call | tf_op jit(solution)/shard_map/form_beams/pallas_call | solution.py:183
  138.7 2.4 %collective-permute-start.5 = (bf16[4,2,16,16,128]{4,3,2,1,0:T(8,128)(2,1)}, bf16[4,2,16,16,128]{4,3,2,1,0:T(8,128)(2,1)S(1)}, u32[]{:S(2)}, u32[]{:S(2)}) collective-permute-start(bf16[4,2,16,16,128]{4,3,2,1,0:T(8,128)(2,1)} %form_beams.6), channel_id=1, source_target_pairs={{0,96},{32,0},{64,32},{96,64},{1,97},{33,1},{65,33},{97,65},{2,98}... | collective-permute-start | bytes 1572872 | tf_op jit(solution)/shard_map/ppermute | solution.py:313
  142.3 2.8 %form_beams.7.refs_3_ = bf16[4,2,16,16,128]{4,3,2,1,0:T(8,128)(2,1)} custom-call(s32[1]{0:T(128)} %bitcast.33.where, bf16[64,4,64,128]{3,2,1,0:T(8,128)(2,1)} %all-to-all-done.1.spectra, f32[2,64,128]{2,1,0:T(8,128)} %pad_maximum_fusion.4.base, f32[2,64,128]{2,1,0:T(8,128)} %get-tuple-element.34.step), custom_call_target="tpu_custom_call" | custom-call | tf_op jit(solution)/shard_map/form_beams/pallas_call | solution.py:183
  145.1 1.3 collective-permute-done.3.refs_0_
  146.4 20.8 %collective-permute-done.4.refs_1_ = bf16[4,2,16,16,128]{4,3,2,1,0:T(8,128)(2,1)S(1)} collective-permute-done((bf16[4,2,16,16,128]{4,3,2,1,0:T(8,128)(2,1)}, bf16[4,2,16,16,128]{4,3,2,1,0:T(8,128)(2,1)S(1)}, u32[]{:S(2)}, u32[]{:S(2)}) %collective-permute-start.4) | collective-permute-done | bytes 524320 | tf_op jit(solution)/shard_map/ppermute | solution.py:313
  167.2 12.6 %collective-permute-done.5.refs_2_ = bf16[4,2,16,16,128]{4,3,2,1,0:T(8,128)(2,1)S(1)} collective-permute-done((bf16[4,2,16,16,128]{4,3,2,1,0:T(8,128)(2,1)}, bf16[4,2,16,16,128]{4,3,2,1,0:T(8,128)(2,1)S(1)}, u32[]{:S(2)}, u32[]{:S(2)}) %collective-permute-start.5) | collective-permute-done | bytes 524320 | tf_op jit(solution)/shard_map/ppermute | solution.py:313
  179.9 0.8 copy-done.3
  180.7 2.4 %add_group.4 = bf16[2,16,16,128]{3,2,1,0:T(8,128)(2,1)} custom-call(s32[1]{0:T(128)} %get-tuple-element.32.group, bf16[4,2,16,16,128]{4,3,2,1,0:T(8,128)(2,1)} %copy-done.1, bf16[4,2,16,16,128]{4,3,2,1,0:T(8,128)(2,1)} %copy-done.2, bf16[4,2,16,16,128]{4,3,2,1,0:T(8,128)(2,1)} %copy-done.3, bf16[4,2,16,16,128]{4,3,2,1,0:T(8,128)(2,1)} %form_beams.7.refs_3_), custom_call_target="tpu_custom_call" | custom-call | tf_op jit(solution)/shard_map/add_group/pallas_call | solution.py:212
  183.0 2.4 %collective-permute-start.6 = (bf16[2,16,16,128]{3,2,1,0:T(8,128)(2,1)}, bf16[2,16,16,128]{3,2,1,0:T(8,128)(2,1)S(1)}, u32[]{:S(2)}, u32[]{:S(2)}) collective-permute-start(bf16[2,16,16,128]{3,2,1,0:T(8,128)(2,1)} %add_group.4), channel_id=1, source_target_pairs={{0,2},{1,3},{2,0},{3,1},{4,6},{5,7},{6,4},{7,5},{8,10},{9,11},{10,... | collective-permute-start | bytes 393224 | tf_op jit(solution)/shard_map/ppermute | solution.py:261
  185.4 2.4 %add_group.5 = bf16[2,16,16,128]{3,2,1,0:T(8,128)(2,1)} custom-call(s32[1]{0:T(128)} %get-tuple-element.31.group, bf16[4,2,16,16,128]{4,3,2,1,0:T(8,128)(2,1)} %copy-done.1, bf16[4,2,16,16,128]{4,3,2,1,0:T(8,128)(2,1)} %copy-done.2, bf16[4,2,16,16,128]{4,3,2,1,0:T(8,128)(2,1)} %copy-done.3, bf16[4,2,16,16,128]{4,3,2,1,0:T(8,128)(2,1)} %form_beams.7.refs_3_), custom_call_target="tpu_custom_call" | custom-call | tf_op jit(solution)/shard_map/add_group/pallas_call | solution.py:212
  188.3 2.4 %add_group.6 = bf16[2,16,16,128]{3,2,1,0:T(8,128)(2,1)} custom-call(s32[1]{0:T(128)} %get-tuple-element.30.group, bf16[4,2,16,16,128]{4,3,2,1,0:T(8,128)(2,1)} %copy-done.1, bf16[4,2,16,16,128]{4,3,2,1,0:T(8,128)(2,1)} %copy-done.2, bf16[4,2,16,16,128]{4,3,2,1,0:T(8,128)(2,1)} %copy-done.3, bf16[4,2,16,16,128]{4,3,2,1,0:T(8,128)(2,1)} %form_beams.7.refs_3_), custom_call_target="tpu_custom_call" | custom-call | tf_op jit(solution)/shard_map/add_group/pallas_call | solution.py:212
  191.1 1.1 gather_fusion
  192.3 2.4 %add_group.7.refs_3_ = bf16[2,16,16,128]{3,2,1,0:T(8,128)(2,1)} custom-call(s32[1]{0:T(128)} %get-tuple-element.29.group, bf16[4,2,16,16,128]{4,3,2,1,0:T(8,128)(2,1)} %copy-done.1, bf16[4,2,16,16,128]{4,3,2,1,0:T(8,128)(2,1)} %copy-done.2, bf16[4,2,16,16,128]{4,3,2,1,0:T(8,128)(2,1)} %copy-done.3, bf16[4,2,16,16,128]{4,3,2,1,0:T(8,128)(2,1)} %form_beams.7.refs_3_), custom_call_target="tpu_custom_call" | custom-call | tf_op jit(solution)/shard_map/add_group/pallas_call | solution.py:212
  196.0 3.5 %merge.1 = (f32[16,64,128]{2,1,0:T(8,128)}, f32[16,64,128]{2,1,0:T(8,128)}) custom-call(s32[4]{0:T(128)} %gather_fusion, bf16[2,16,16,128]{3,2,1,0:T(8,128)(2,1)} %copy-done.4, bf16[2,16,16,128]{3,2,1,0:T(8,128)(2,1)} %copy-done.5, bf16[2,16,16,128]{3,2,1,0:T(8,128)(2,1)} %copy-done.6, bf16[2,16,16,128]{3,2,1,0:T(8,128)(2,1)} %add_group.7.refs_3_), custom_call_target="tpu_custom_call" | custom-call | tf_op jit(solution)/shard_map/merge/pallas_call | solution.py:245
  (56 shorter events, 8.1 us)
Async XLA Ops:
  7.2 63.7 %copy-start = (f32[64,512]{1,0:T(8,128)S(1)}, f32[64,512]{1,0:T(8,128)}, u32[]{:S(2)}) copy-start(f32[64,512]{1,0:T(8,128)} %param.16) | copy-start | bytes 393220
  7.2 38.1 %reduce-scatter.2.cloned.1.call-start = ((), (), s32[]{:S(2)}) async-start(), calls=%async_computation.3 | async-start | bytes 40960 | tf_op jit(solution)/shard_map/reduce_scatter | solution.py:285
  46.6 17.1 %all-to-all-start = ((f32[16,16,128]{2,1,0:T(8,128)}), f32[16,16,128]{2,1,0:T(8,128)S(1)}, u32[]{:S(2)}, u32[]{:S(2)}) async-start(f32[16,16,128]{2,1,0:T(8,128)} %broadcast_in_dim.38), calls=%async_computation.1 | async-start | bytes 262144 | tf_op jit(solution)/shard_map/all_to_all | solution.py:288
  63.7 7.2 %copy-start.10 = (s32[64]{0:T(128)S(1)}, s32[64]{0:T(128)}, u32[]{:S(2)}) copy-start(s32[64]{0:T(128)} %param.18) | copy-start | bytes 772
  63.7 7.9 %copy-start.9 = (s32[4]{0:T(128)S(1)}, s32[4]{0:T(128)}, u32[]{:S(2)}) copy-start(s32[4]{0:T(128)} %constant.156) | copy-start | bytes 52
  63.7 10.6 %copy-start.8 = (s32[4]{0:T(128)S(1)}, s32[4]{0:T(128)}, u32[]{:S(2)}) copy-start(s32[4]{0:T(128)} %constant.157) | copy-start | bytes 52
  63.7 59.5 %all-to-all-start.1 = ((bf16[64,4,64,128]{3,2,1,0:T(8,128)(2,1)}), bf16[64,4,64,128]{3,2,1,0:T(8,128)(2,1)}, u32[]{:S(2)}, u32[]{:S(2)}) async-start(bf16[64,4,64,128]{3,2,1,0:T(8,128)(2,1)} %bitcast.57), calls=%async_computation.2 | async-start | bytes 8388608 | tf_op jit(solution)/shard_map/all_to_all | solution.py:295
  72.1 47.2 %collective-permute-start.2 = (f32[16,128]{1,0:T(8,128)S(1)}, f32[16,128]{1,0:T(8,128)S(1)}, u32[]{:S(2)}, u32[]{:S(2)}) collective-permute-start(f32[16,128]{1,0:T(8,128)S(1)} %dynamic-slice_bitcast_fusion), channel_id=1, source_target_pairs={{0,3},{1,2},{2,1},{3,0},{4,7},{5,6},{6,5},{7,4},{8,11},{9,10},{10,... | collective-permute-start | bytes 24584 | tf_op jit(solution)/shard_map/ppermute | solution.py:261
  73.8 45.5 %collective-permute-start.1 = (f32[16,128]{1,0:T(8,128)S(1)}, f32[16,128]{1,0:T(8,128)S(1)}, u32[]{:S(2)}, u32[]{:S(2)}) collective-permute-start(f32[16,128]{1,0:T(8,128)S(1)} %dynamic-slice_bitcast_fusion), channel_id=1, source_target_pairs={{0,2},{1,3},{2,0},{3,1},{4,6},{5,7},{6,4},{7,5},{8,10},{9,11},{10,... | collective-permute-start | bytes 24584 | tf_op jit(solution)/shard_map/ppermute | solution.py:261
  74.2 45.2 %collective-permute-start = (f32[16,128]{1,0:T(8,128)S(1)}, f32[16,128]{1,0:T(8,128)S(1)}, u32[]{:S(2)}, u32[]{:S(2)}) collective-permute-start(f32[16,128]{1,0:T(8,128)S(1)} %dynamic-slice_bitcast_fusion), channel_id=1, source_target_pairs={{0,1},{1,0},{2,3},{3,2},{4,5},{5,4},{6,7},{7,6},{8,9},{9,8},{10,11... | collective-permute-start | bytes 24584 | tf_op jit(solution)/shard_map/ppermute | solution.py:261
  125.9 20.5 %collective-permute-start.3 = (bf16[4,2,16,16,128]{4,3,2,1,0:T(8,128)(2,1)}, bf16[4,2,16,16,128]{4,3,2,1,0:T(8,128)(2,1)S(1)}, u32[]{:S(2)}, u32[]{:S(2)}) collective-permute-start(bf16[4,2,16,16,128]{4,3,2,1,0:T(8,128)(2,1)} %form_beams.4), channel_id=1, source_target_pairs={{0,64},{32,96},{64,0},{96,32},{1,65},{33,97},{65,1},{97,33},{2,66}... | collective-permute-start | bytes 1572872 | tf_op jit(solution)/shard_map/ppermute | solution.py:313
  134.7 32.5 %collective-permute-start.4 = (bf16[4,2,16,16,128]{4,3,2,1,0:T(8,128)(2,1)}, bf16[4,2,16,16,128]{4,3,2,1,0:T(8,128)(2,1)S(1)}, u32[]{:S(2)}, u32[]{:S(2)}) collective-permute-start(bf16[4,2,16,16,128]{4,3,2,1,0:T(8,128)(2,1)} %form_beams.5), channel_id=1, source_target_pairs={{0,32},{32,64},{64,96},{96,0},{1,33},{33,65},{65,97},{97,1},{2,34}... | collective-permute-start | bytes 1572872 | tf_op jit(solution)/shard_map/ppermute | solution.py:313
  138.7 41.1 %collective-permute-start.5 = (bf16[4,2,16,16,128]{4,3,2,1,0:T(8,128)(2,1)}, bf16[4,2,16,16,128]{4,3,2,1,0:T(8,128)(2,1)S(1)}, u32[]{:S(2)}, u32[]{:S(2)}) collective-permute-start(bf16[4,2,16,16,128]{4,3,2,1,0:T(8,128)(2,1)} %form_beams.6), channel_id=1, source_target_pairs={{0,96},{32,0},{64,32},{96,64},{1,97},{33,1},{65,33},{97,65},{2,98}... | collective-permute-start | bytes 1572872 | tf_op jit(solution)/shard_map/ppermute | solution.py:313
  145.1 46.0 %copy-start.7 = (s32[4]{0:T(128)S(1)}, s32[4]{0:T(128)}, u32[]{:S(2)}) copy-start(s32[4]{0:T(128)} %constant.155) | copy-start | bytes 52
  146.4 33.4 %copy-start.1 = (bf16[4,2,16,16,128]{4,3,2,1,0:T(8,128)(2,1)}, bf16[4,2,16,16,128]{4,3,2,1,0:T(8,128)(2,1)S(1)}, u32[]{:S(2)}) copy-start(bf16[4,2,16,16,128]{4,3,2,1,0:T(8,128)(2,1)S(1)} %collective-permute-done.3.refs_0_) | copy-start | bytes 1572868
  167.2 12.6 %copy-start.2 = (bf16[4,2,16,16,128]{4,3,2,1,0:T(8,128)(2,1)}, bf16[4,2,16,16,128]{4,3,2,1,0:T(8,128)(2,1)S(1)}, u32[]{:S(2)}) copy-start(bf16[4,2,16,16,128]{4,3,2,1,0:T(8,128)(2,1)S(1)} %collective-permute-done.4.refs_1_) | copy-start | bytes 1572868
  179.8 0.8 copy-start.3
  183.0 11.7 %collective-permute-start.6 = (bf16[2,16,16,128]{3,2,1,0:T(8,128)(2,1)}, bf16[2,16,16,128]{3,2,1,0:T(8,128)(2,1)S(1)}, u32[]{:S(2)}, u32[]{:S(2)}) collective-permute-start(bf16[2,16,16,128]{3,2,1,0:T(8,128)(2,1)} %add_group.4), channel_id=1, source_target_pairs={{0,2},{1,3},{2,0},{3,1},{4,6},{5,7},{6,4},{7,5},{8,10},{9,11},{10,... | collective-permute-start | bytes 393224 | tf_op jit(solution)/shard_map/ppermute | solution.py:261
  187.9 6.8 %collective-permute-start.7 = (bf16[2,16,16,128]{3,2,1,0:T(8,128)(2,1)}, bf16[2,16,16,128]{3,2,1,0:T(8,128)(2,1)S(1)}, u32[]{:S(2)}, u32[]{:S(2)}) collective-permute-start(bf16[2,16,16,128]{3,2,1,0:T(8,128)(2,1)} %add_group.5), channel_id=1, source_target_pairs={{0,3},{1,2},{2,1},{3,0},{4,7},{5,6},{6,5},{7,4},{8,11},{9,10},{10,... | collective-permute-start | bytes 393224 | tf_op jit(solution)/shard_map/ppermute | solution.py:261
  190.7 4.0 %collective-permute-start.8 = (bf16[2,16,16,128]{3,2,1,0:T(8,128)(2,1)}, bf16[2,16,16,128]{3,2,1,0:T(8,128)(2,1)S(1)}, u32[]{:S(2)}, u32[]{:S(2)}) collective-permute-start(bf16[2,16,16,128]{3,2,1,0:T(8,128)(2,1)} %add_group.6), channel_id=1, source_target_pairs={{0,1},{1,0},{2,3},{3,2},{4,5},{5,4},{6,7},{7,6},{8,9},{9,8},{10,11... | collective-permute-start | bytes 393224 | tf_op jit(solution)/shard_map/ppermute | solution.py:261
  194.7 0.7 copy-start.4
  194.7 0.7 copy-start.5
  195.4 0.6 copy-start.6
Sparse Core Ops, SparseCore 0:
  11.7 26.7 reduce-scatter.1

commit v4 on v3

--- a/solution.py
+++ b/solution.py
@@ -1,3 +1,4 @@
+import functools
 import math
 
 import jax
@@ -20,14 +21,15 @@
 F32 = jnp.float32
 BF16 = jnp.bfloat16
 VMEM_LIMIT = 56 << 20
+SMALL_LIMIT = 12 << 20
 
 AXES = ("yh", "zh", "zl", "x", "yl", "c")
 SIZES = (2, 4, 2, 4, 2, 2)
 TURN = ("yh", "zl", "x", "yl", "c")
 FRAME_CHUNK = 16
-TURN_ROWS = 136
-STAGE_ROWS = 40
-WIDE_ROWS = 72
+TURN_ROWS = 132
+STAGE_ROWS = 36
+WIDE_ROWS = 68
 BEAM_ROWS = 24
 
 
@@ -88,7 +90,7 @@
 
     def second_section(j, carry):
         for i in range(16):
-            row = pl.multiple_of((j * 16 + i) * TURN_ROWS, 8)
+            row = pl.multiple_of((j * 16 + i) * TURN_ROWS, 4)
             right = jnp.concatenate(
                 (
                     turned_re[pl.ds(row, 128), :].astype(BF16),
@@ -110,8 +112,16 @@
 
     @pl.when(block == 7)
     def _():
-        lax.fori_loop(0, FRAMES // 2, first_section, 0)
-        lax.fori_loop(0, 4, second_section, 0)
+        lax.fori_loop(0, FRAMES // 2, first_section, 0, unroll=16)
+        lax.fori_loop(0, 4, second_section, 0, unroll=4)
+
+
+CHIP = pl.BlockSpec(memory_space=pltpu.VMEM)
+SCALAR = pl.BlockSpec(memory_space=pltpu.SMEM)
+
+
+def on_chip(value):
+    return pltpu.with_memory_space_constraint(value, pltpu.VMEM)
 
 
 def whole(*shape):
@@ -187,44 +197,39 @@
             grid=(1,),
             in_specs=[
                 pl.BlockSpec((64, 1, 64, 128), lambda n, zh: (0, zh[0], 0, 0)),
-                whole(2, 64, 128),
-                whole(2, 64, 128),
+                CHIP,
+                CHIP,
             ],
-            out_specs=whole(4, 2, 16, 16, 128),
+            out_specs=CHIP,
             scratch_shapes=[pltpu.VMEM((64 * WIDE_ROWS, 128), F32)],
         ),
-        out_shape=jax.ShapeDtypeStruct((4, 2, 16, 16, 128), BF16),
-        compiler_params=pltpu.CompilerParams(vmem_limit_bytes=VMEM_LIMIT),
+        out_shape=pltpu.VMEM((4, 2, 16, 16, 128), BF16),
+        compiler_params=pltpu.CompilerParams(vmem_limit_bytes=SMALL_LIMIT),
         name="form_beams",
-    )(where, spectra, base, step)
-
-
-def add_kernel(group, *refs):
-    del group
-    total = refs[0][0].astype(F32)
+    )(where, spectra, on_chip(base), on_chip(step))
+
+
+def add_kernel(offset, beam_pos, *refs):
+    group = beam_pos[0] ^ offset
+    total = refs[0][group].astype(F32)
     for part in refs[1:-1]:
-        total = total + part[0].astype(F32)
+        total = total + part[group].astype(F32)
     refs[-1][...] = total.astype(BF16)
 
 
-def add_group(group, parts):
-    part_spec = pl.BlockSpec((1, 2, 16, 16, 128), lambda n, g: (g[0], 0, 0, 0, 0))
+def add_group(offset, beam_pos, parts):
     return pl.pallas_call(
-        add_kernel,
-        grid_spec=pltpu.PrefetchScalarGridSpec(
-            num_scalar_prefetch=1,
-            grid=(1,),
-            in_specs=[part_spec] * len(parts),
-            out_specs=whole(2, 16, 16, 128),
-        ),
-        out_shape=jax.ShapeDtypeStruct((2, 16, 16, 128), BF16),
-        compiler_params=pltpu.CompilerParams(vmem_limit_bytes=VMEM_LIMIT),
+        functools.partial(add_kernel, offset),
+        in_specs=[SCALAR] + [CHIP] * len(parts),
+        out_specs=CHIP,
+        out_shape=pltpu.VMEM((2, 16, 16, 128), BF16),
+        compiler_params=pltpu.CompilerParams(vmem_limit_bytes=SMALL_LIMIT),
         name="add_group",
-    )(group, *parts)
-
-
-def merge_kernel(order, *refs):
-    del order
+    )(beam_pos, *[on_chip(part) for part in parts])
+
+
+def merge_kernel(beam_pos, *refs):
+    del beam_pos
     parts, outs, stage = refs[:4], refs[4:6], refs[6]
     scale = 1.0 / math.sqrt(P_SIZE * Q * STATIONS)
     for n, part in enumerate(parts):
@@ -239,22 +244,22 @@
                     outs[ri][beam] = stage[ri, row : row + 16, :]
 
 
-def merge(order, parts):
-    spec = pl.BlockSpec((16, 16, 128), lambda n, order: (0, order[n], 0))
+def merge(beam_pos, parts):
+    spec = pl.BlockSpec((16, 16, 128), lambda n, pos: (0, pos[0] ^ n, 0))
     shape = jax.ShapeDtypeStruct((16, 64, 128), F32)
     return pl.pallas_call(
         merge_kernel,
         grid_spec=pltpu.PrefetchScalarGridSpec(
             num_scalar_prefetch=1,
             grid=(4,),
-            in_specs=[whole(2, 16, 16, 128)] * 4,
+            in_specs=[CHIP] * 4,
             out_specs=[spec, spec],
             scratch_shapes=[pltpu.VMEM((2, 16 * BEAM_ROWS, 128), F32)],
         ),
         out_shape=[shape, shape],
-        compiler_params=pltpu.CompilerParams(vmem_limit_bytes=VMEM_LIMIT),
+        compiler_params=pltpu.CompilerParams(vmem_limit_bytes=SMALL_LIMIT),
         name="merge",
-    )(order, *parts)
+    )(beam_pos, *[on_chip(part) for part in parts])
 
 
 def swap_beam(value, offset):
@@ -294,10 +299,11 @@
     delays_by_offset = [delay] + [swap_beam(delay, n) for n in range(1, 4)]
     turned = lax.all_to_all(spectra.reshape(64, 4, 64, 128), TURN, 0, 0, tiled=True)
 
-    delay = jnp.stack(delays_by_offset)
-    delay = jnp.where(beam_pos % 2 == 1, delay[jnp.array((1, 0, 3, 2))], delay)
-    delay = jnp.where(beam_pos // 2 == 1, delay[jnp.array((2, 3, 0, 1))], delay)
-    delay = delay.reshape(4 * slots, 128)
+    models = delays_by_offset
+    for bit in (1, 2):
+        odd = beam_pos & bit != 0
+        models = [jnp.where(odd, models[n ^ bit], models[n]) for n in range(4)]
+    delay = jnp.concatenate(models, axis=0)
     gain = pick_columns(taper[beam_order], pick)
     gain = lax.dynamic_slice_in_dim(gain, zh * 128, 128, 1)
     first_chan = yh * 2048 + zl * 256 + x * 64 + beam_pos * 16
@@ -312,10 +318,12 @@
         if dz:
             part = lax.ppermute(part, "zh", [(z, (z + dz) % 4) for z in range(4)])
         parts.append(part)
-    order = beam_pos ^ jnp.arange(4, dtype=jnp.int32)
-    quarters = [add_group(order[n : n + 1], parts) for n in (2, 3, 1, 0)]
-    quarters = [swap_beam(q, n) if n else q for q, n in zip(quarters, (2, 3, 1, 0))]
-    out_re, out_im = merge(order[jnp.array((2, 3, 1, 0))], quarters)
+    pos = beam_pos.astype(jnp.int32)[None]
+    quarters = {}
+    for n in (2, 3, 1, 0):
+        quarter = add_group(n, pos, parts)
+        quarters[n] = swap_beam(quarter, n) if n else quarter
+    out_re, out_im = merge(pos, [quarters[n] for n in range(4)])
     return (out_re, out_im)
 
 

time: 208 us -> 190 us (0.913)
  Pallas kernels: 55.9 us -> 29.4 us
  waiting for transfers between devices: 85.3 us -> 104 us
  local copies, waits for them, and re-layouts: 11.2 us -> 6.23 us
  starting transfers between devices: 31.2 us -> 27.8 us
  other arithmetic: 3.53 us -> 1.33 us
    pallas_call x1, Pallas kernels: 31.7 us -> 20 us  [channelize(): pl.pallas_call(channel_kernel, grid=(2, 8), in_specs=[pl.BlockSpec((1, 75...]
    pallas_call x4, Pallas kernels: 9.62 us -> 0.27 us  [add_group(): pl.pallas_call(functools.partial(add_kernel, offset), in_specs=[SCALAR] +...]
    ppermute x6, waiting for transfers between devices: 44.9 us -> 51.4 us  [swap_beam(): return lax.ppermute(value, ('yl', 'c'), [(b, b ^ offset) for b in range(4)])]
    ppermute x3, waiting for transfers between devices: 34.7 us -> 41 us  [on_device(): part = lax.ppermute(part, 'zh', [(z, (z + dz) % 4) for z in range(4)])]
    reduce_scatter x1, waiting for transfers between devices: 0.01 us -> 4.88 us  [on_device(): model = lax.psum_scatter(model, 'zh', scatter_dimension=0, tiled=False)]
    pallas_call x4, Pallas kernels: 11.2 us -> 7.41 us  [form_beams(): pl.pallas_call(beam_kernel, grid_spec=pltpu.PrefetchScalarGridSpec(num_sc...]
    ppermute x3, starting transfers between devices: 9.58 us -> 6.6 us  [on_device(): part = lax.ppermute(part, 'zh', [(z, (z + dz) % 4) for z in range(4)])]
    all_to_all x1, starting transfers between devices: 8.94 us -> 6.64 us  [on_device(): lax.all_to_all(jnp.broadcast_to(model[None], (16, slots, 128)), ('yh', 'z...]
  transfers between devices with their start and end apart: 12 -> 12, of which waited for: 5 -> 9; matrix products, arithmetic and copies ran while one was open for 4% -> 2% of each run, Pallas kernels for 23% -> 14%
where the time goes in v4:
time: 190 us; the launch traced here: 188 us
  waiting for transfers between devices  104 us (55%)
  Pallas kernels  29.4 us (15%)
  starting transfers between devices  27.8 us (15%)
  between operations  17.5 us (9%)
  local copies, waits for them, and re-layouts  6.23 us (3%)
    ppermute x6, waiting for transfers between devices, swap_beam(): return lax.ppermute(value, ('yl', 'c'), [(b, b ^ offset) for b in range(4)])  51.4 us
    ppermute x3, waiting for transfers between devices, on_device(): part = lax.ppermute(part, 'zh', [(z, (z + dz) % 4) for z in range(4)])  41 us
    pallas_call x1, Pallas kernels, channelize(): pl.pallas_call(channel_kernel, grid=(2, 8), in_specs=[pl.BlockSpec((1, 75...  20 us
    all_to_all x1, starting transfers between devices, on_device(): lax.all_to_all(spectra.reshape(64, 4, 64, 128), TURN, 0, 0, tiled=True)  9.46 us
    pallas_call x4, Pallas kernels, form_beams(): pl.pallas_call(beam_kernel, grid_spec=pltpu.PrefetchScalarGridSpec(num_sc...  7.41 us
    all_to_all x1, starting transfers between devices, on_device(): lax.all_to_all(jnp.broadcast_to(model[None], (16, slots, 128)), ('yh', 'z...  6.64 us
    ppermute x3, starting transfers between devices, on_device(): part = lax.ppermute(part, 'zh', [(z, (z + dz) % 4) for z in range(4)])  6.6 us
    all_to_all x1, waiting for transfers between devices, on_device(): lax.all_to_all(jnp.broadcast_to(model[None], (16, slots, 128)), ('yh', 'z...  5.48 us
  transfers between devices with their start and end apart: 12, of which 9 were waited for; matrix products, arithmetic and copies ran while one was open for 2% of the time, Pallas kernels for 14%

profile of v4, /device:TPU:1, one launch (start us, length us, event | category | flops | bytes accessed | tf_op | source)
XLA Modules:
  0.0 188.2 jit_solution(6731620921954160386)
XLA Ops:
  7.2 0.8 reshape.128
  8.5 1.3 dynamic_slice.10
  10.4 1.2 convolution_bitcast_fusion
  11.6 1.1 copy.15
  12.7 0.8 slice.2.taps
  13.5 20.0 %channelize.1 = bf16[2,2,4,4,4,2,32,128]{7,6,5,4,3,2,1,0:T(8,128)(2,1)} custom-call(bf16[2,75,128,128]{3,2,1,0:T(8,128)(2,1)} %bitcast.49, f32[12,64,128]{2,1,0:T(8,128)} %slice.2.taps, bf16[256,128]{1,0:T(8,128)(2,1)} %constant.115.clone.one, f32[2,64,128]{2,1,0:T(8,128)} %constant.116.clone.twist, bf16[128,256]{1,0:T(8,128)(2,1)} %constant.117.clone.two), custom_call_target="tpu_custom_call" | custom-call | tf_op jit(solution)/shard_map/channelize/pallas_call | solution.py:133
  33.5 4.9 %reduce-scatter.2.cloned.1.call-done = f32[1,16,128]{2,1,0:T(8,128)} async-done(((f32[4,16,128]{2,1,0:T(8,128)}), f32[1,16,128]{2,1,0:T(8,128)}) %reduce-scatter.2.cloned.1.call-update) | async-done | bytes 8208 | tf_op jit(solution)/shard_map/reduce_scatter | solution.py:290
  38.4 1.4 broadcast_in_dim.32
  39.8 6.6 %all-to-all-start = ((f32[16,16,128]{2,1,0:T(8,128)}), f32[16,16,128]{2,1,0:T(8,128)S(1)}, u32[]{:S(2)}, u32[]{:S(2)}) async-start(f32[16,16,128]{2,1,0:T(8,128)} %broadcast_in_dim.32), calls=%async_computation.1 | async-start | bytes 262144 | tf_op jit(solution)/shard_map/all_to_all | solution.py:293
  49.0 5.5 %all-to-all-done = f32[16,16,128]{2,1,0:T(8,128)S(1)} async-done(((f32[16,16,128]{2,1,0:T(8,128)}), f32[16,16,128]{2,1,0:T(8,128)S(1)}, u32[]{:S(2)}, u32[]{:S(2)}) %all-to-all-start) | async-done | bytes 131104 | tf_op jit(solution)/shard_map/all_to_all | solution.py:293
  54.5 9.5 %all-to-all-start.1 = ((bf16[64,4,64,128]{3,2,1,0:T(8,128)(2,1)}), bf16[64,4,64,128]{3,2,1,0:T(8,128)(2,1)}, u32[]{:S(2)}, u32[]{:S(2)}) async-start(bf16[64,4,64,128]{3,2,1,0:T(8,128)(2,1)} %bitcast.48), calls=%async_computation.2 | async-start | bytes 8388608 | tf_op jit(solution)/shard_map/all_to_all | solution.py:300
  64.0 0.7 gather_fusion
  64.6 1.7 collective-permute-start
  66.3 0.4 collective-permute-start.1
  66.9 0.5 fusion
  67.4 45.0 %collective-permute-done = f32[16,128]{1,0:T(8,128)S(1)} collective-permute-done((f32[16,128]{1,0:T(8,128)S(1)}, f32[16,128]{1,0:T(8,128)S(1)}, u32[]{:S(2)}, u32[]{:S(2)}) %collective-permute-start) | collective-permute-done | bytes 8224 | tf_op jit(solution)/shard_map/ppermute | solution.py:266
  113.5 1.6 all-to-all-done.1.spectra
  115.1 1.9 form_beams.4
  117.0 2.7 %collective-permute-start.3 = (bf16[4,2,16,16,128]{4,3,2,1,0:T(8,128)(2,1)S(1)}, bf16[4,2,16,16,128]{4,3,2,1,0:T(8,128)(2,1)S(1)}, u32[]{:S(2)}, u32[]{:S(2)}) collective-permute-start(bf16[4,2,16,16,128]{4,3,2,1,0:T(8,128)(2,1)S(1)} %form_beams.4), channel_id=1, source_target_pairs={{0,64},{32,96},{64,0},{96,32},{1,65},{33,97},{65,1},{97,33},{2,66}... | collective-permute-start | bytes 1572872 | tf_op jit(solution)/shard_map/ppermute | solution.py:319
  119.7 1.9 form_beams.5
  121.5 1.5 collective-permute-start.4
  123.0 1.8 form_beams.6
  124.9 2.4 %collective-permute-start.5 = (bf16[4,2,16,16,128]{4,3,2,1,0:T(8,128)(2,1)S(1)}, bf16[4,2,16,16,128]{4,3,2,1,0:T(8,128)(2,1)S(1)}, u32[]{:S(2)}, u32[]{:S(2)}) collective-permute-start(bf16[4,2,16,16,128]{4,3,2,1,0:T(8,128)(2,1)S(1)} %form_beams.6), channel_id=1, source_target_pairs={{0,96},{32,0},{64,32},{96,64},{1,97},{33,1},{65,33},{97,65},{2,98}... | collective-permute-start | bytes 1572872 | tf_op jit(solution)/shard_map/ppermute | solution.py:319
  127.3 1.9 form_beams.7.refs_3_
  129.2 6.1 %collective-permute-done.3.refs_0_ = bf16[4,2,16,16,128]{4,3,2,1,0:T(8,128)(2,1)S(1)} collective-permute-done((bf16[4,2,16,16,128]{4,3,2,1,0:T(8,128)(2,1)S(1)}, bf16[4,2,16,16,128]{4,3,2,1,0:T(8,128)(2,1)S(1)}, u32[]{:S(2)}, u32[]{:S(2)}) %collective-permute-start.3) | collective-permute-done | bytes 524320 | tf_op jit(solution)/shard_map/ppermute | solution.py:319
  135.3 21.8 %collective-permute-done.4.refs_1_ = bf16[4,2,16,16,128]{4,3,2,1,0:T(8,128)(2,1)S(1)} collective-permute-done((bf16[4,2,16,16,128]{4,3,2,1,0:T(8,128)(2,1)S(1)}, bf16[4,2,16,16,128]{4,3,2,1,0:T(8,128)(2,1)S(1)}, u32[]{:S(2)}, u32[]{:S(2)}) %collective-permute-start.4) | collective-permute-done | bytes 524320 | tf_op jit(solution)/shard_map/ppermute | solution.py:319
  157.1 13.0 %collective-permute-done.5.refs_2_ = bf16[4,2,16,16,128]{4,3,2,1,0:T(8,128)(2,1)S(1)} collective-permute-done((bf16[4,2,16,16,128]{4,3,2,1,0:T(8,128)(2,1)S(1)}, bf16[4,2,16,16,128]{4,3,2,1,0:T(8,128)(2,1)S(1)}, u32[]{:S(2)}, u32[]{:S(2)}) %collective-permute-start.5) | collective-permute-done | bytes 524320 | tf_op jit(solution)/shard_map/ppermute | solution.py:319
  170.2 0.6 collective-permute-start.6
  170.9 2.2 %collective-permute-start.7 = (bf16[2,16,16,128]{3,2,1,0:T(8,128)(2,1)S(1)}, bf16[2,16,16,128]{3,2,1,0:T(8,128)(2,1)S(1)}, u32[]{:S(2)}, u32[]{:S(2)}) collective-permute-start(bf16[2,16,16,128]{3,2,1,0:T(8,128)(2,1)S(1)} %add_group.6), channel_id=1, source_target_pairs={{0,2},{1,3},{2,0},{3,1},{4,6},{5,7},{6,4},{7,5},{8,10},{9,11},{10,... | collective-permute-start | bytes 393224 | tf_op jit(solution)/shard_map/ppermute | solution.py:266
  173.3 3.6 %collective-permute-done.7.refs_2_ = bf16[2,16,16,128]{3,2,1,0:T(8,128)(2,1)S(1)} collective-permute-done((bf16[2,16,16,128]{3,2,1,0:T(8,128)(2,1)S(1)}, bf16[2,16,16,128]{3,2,1,0:T(8,128)(2,1)S(1)}, u32[]{:S(2)}, u32[]{:S(2)}) %collective-permute-start.7) | collective-permute-done | bytes 131104 | tf_op jit(solution)/shard_map/ppermute | solution.py:266
  176.9 2.8 %collective-permute-done.8.refs_3_ = bf16[2,16,16,128]{3,2,1,0:T(8,128)(2,1)S(1)} collective-permute-done((bf16[2,16,16,128]{3,2,1,0:T(8,128)(2,1)S(1)}, bf16[2,16,16,128]{3,2,1,0:T(8,128)(2,1)S(1)}, u32[]{:S(2)}, u32[]{:S(2)}) %collective-permute-start.8) | collective-permute-done | bytes 131104 | tf_op jit(solution)/shard_map/ppermute | solution.py:266
  179.7 1.6 merge.1
  (31 shorter events, 2.1 us)
Async XLA Ops:
  7.2 56.8 %copy-start = (f32[64,512]{1,0:T(8,128)S(1)}, f32[64,512]{1,0:T(8,128)}, u32[]{:S(2)}) copy-start(f32[64,512]{1,0:T(8,128)} %param.13) | copy-start | bytes 393220
  7.2 31.2 %reduce-scatter.2.cloned.1.call-start = ((), (), s32[]{:S(2)}) async-start(), calls=%async_computation.3 | async-start | bytes 40960 | tf_op jit(solution)/shard_map/reduce_scatter | solution.py:290
  39.8 14.7 %all-to-all-start = ((f32[16,16,128]{2,1,0:T(8,128)}), f32[16,16,128]{2,1,0:T(8,128)S(1)}, u32[]{:S(2)}, u32[]{:S(2)}) async-start(f32[16,16,128]{2,1,0:T(8,128)} %broadcast_in_dim.32), calls=%async_computation.1 | async-start | bytes 262144 | tf_op jit(solution)/shard_map/all_to_all | solution.py:293
  54.5 9.5 %copy-start.1 = (s32[64]{0:T(128)S(1)}, s32[64]{0:T(128)}, u32[]{:S(2)}) copy-start(s32[64]{0:T(128)} %param.15) | copy-start | bytes 772
  54.5 60.7 %all-to-all-start.1 = ((bf16[64,4,64,128]{3,2,1,0:T(8,128)(2,1)}), bf16[64,4,64,128]{3,2,1,0:T(8,128)(2,1)}, u32[]{:S(2)}, u32[]{:S(2)}) async-start(bf16[64,4,64,128]{3,2,1,0:T(8,128)(2,1)} %bitcast.48), calls=%async_computation.2 | async-start | bytes 8388608 | tf_op jit(solution)/shard_map/all_to_all | solution.py:300
  64.6 47.8 %collective-permute-start = (f32[16,128]{1,0:T(8,128)S(1)}, f32[16,128]{1,0:T(8,128)S(1)}, u32[]{:S(2)}, u32[]{:S(2)}) collective-permute-start(f32[16,128]{1,0:T(8,128)S(1)} %dynamic-slice_bitcast_fusion), channel_id=1, source_target_pairs={{0,3},{1,2},{2,1},{3,0},{4,7},{5,6},{6,5},{7,4},{8,11},{9,10},{10,... | collective-permute-start | bytes 24584 | tf_op jit(solution)/shard_map/ppermute | solution.py:266
  66.3 46.0 %collective-permute-start.1 = (f32[16,128]{1,0:T(8,128)S(1)}, f32[16,128]{1,0:T(8,128)S(1)}, u32[]{:S(2)}, u32[]{:S(2)}) collective-permute-start(f32[16,128]{1,0:T(8,128)S(1)} %dynamic-slice_bitcast_fusion), channel_id=1, source_target_pairs={{0,2},{1,3},{2,0},{3,1},{4,6},{5,7},{6,4},{7,5},{8,10},{9,11},{10,... | collective-permute-start | bytes 24584 | tf_op jit(solution)/shard_map/ppermute | solution.py:266
  66.7 45.7 %collective-permute-start.2 = (f32[16,128]{1,0:T(8,128)S(1)}, f32[16,128]{1,0:T(8,128)S(1)}, u32[]{:S(2)}, u32[]{:S(2)}) collective-permute-start(f32[16,128]{1,0:T(8,128)S(1)} %dynamic-slice_bitcast_fusion), channel_id=1, source_target_pairs={{0,1},{1,0},{2,3},{3,2},{4,5},{5,4},{6,7},{7,6},{8,9},{9,8},{10,11... | collective-permute-start | bytes 24584 | tf_op jit(solution)/shard_map/ppermute | solution.py:266
  117.0 18.3 %collective-permute-start.3 = (bf16[4,2,16,16,128]{4,3,2,1,0:T(8,128)(2,1)S(1)}, bf16[4,2,16,16,128]{4,3,2,1,0:T(8,128)(2,1)S(1)}, u32[]{:S(2)}, u32[]{:S(2)}) collective-permute-start(bf16[4,2,16,16,128]{4,3,2,1,0:T(8,128)(2,1)S(1)} %form_beams.4), channel_id=1, source_target_pairs={{0,64},{32,96},{64,0},{96,32},{1,65},{33,97},{65,1},{97,33},{2,66}... | collective-permute-start | bytes 1572872 | tf_op jit(solution)/shard_map/ppermute | solution.py:319
  121.5 35.6 %collective-permute-start.4 = (bf16[4,2,16,16,128]{4,3,2,1,0:T(8,128)(2,1)S(1)}, bf16[4,2,16,16,128]{4,3,2,1,0:T(8,128)(2,1)S(1)}, u32[]{:S(2)}, u32[]{:S(2)}) collective-permute-start(bf16[4,2,16,16,128]{4,3,2,1,0:T(8,128)(2,1)S(1)} %form_beams.5), channel_id=1, source_target_pairs={{0,32},{32,64},{64,96},{96,0},{1,33},{33,65},{65,97},{97,1},{2,34}... | collective-permute-start | bytes 1572872 | tf_op jit(solution)/shard_map/ppermute | solution.py:319
  124.9 45.2 %collective-permute-start.5 = (bf16[4,2,16,16,128]{4,3,2,1,0:T(8,128)(2,1)S(1)}, bf16[4,2,16,16,128]{4,3,2,1,0:T(8,128)(2,1)S(1)}, u32[]{:S(2)}, u32[]{:S(2)}) collective-permute-start(bf16[4,2,16,16,128]{4,3,2,1,0:T(8,128)(2,1)S(1)} %form_beams.6), channel_id=1, source_target_pairs={{0,96},{32,0},{64,32},{96,64},{1,97},{33,1},{65,33},{97,65},{2,98}... | collective-permute-start | bytes 1572872 | tf_op jit(solution)/shard_map/ppermute | solution.py:319
  170.2 3.1 %collective-permute-start.6 = (bf16[2,16,16,128]{3,2,1,0:T(8,128)(2,1)S(1)}, bf16[2,16,16,128]{3,2,1,0:T(8,128)(2,1)S(1)}, u32[]{:S(2)}, u32[]{:S(2)}) collective-permute-start(bf16[2,16,16,128]{3,2,1,0:T(8,128)(2,1)S(1)} %add_group.5), channel_id=1, source_target_pairs={{0,1},{1,0},{2,3},{3,2},{4,5},{5,4},{6,7},{7,6},{8,9},{9,8},{10,11... | collective-permute-start | bytes 393224 | tf_op jit(solution)/shard_map/ppermute | solution.py:266
  170.9 6.0 %collective-permute-start.7 = (bf16[2,16,16,128]{3,2,1,0:T(8,128)(2,1)S(1)}, bf16[2,16,16,128]{3,2,1,0:T(8,128)(2,1)S(1)}, u32[]{:S(2)}, u32[]{:S(2)}) collective-permute-start(bf16[2,16,16,128]{3,2,1,0:T(8,128)(2,1)S(1)} %add_group.6), channel_id=1, source_target_pairs={{0,2},{1,3},{2,0},{3,1},{4,6},{5,7},{6,4},{7,5},{8,10},{9,11},{10,... | collective-permute-start | bytes 393224 | tf_op jit(solution)/shard_map/ppermute | solution.py:266
  173.1 6.6 %collective-permute-start.8 = (bf16[2,16,16,128]{3,2,1,0:T(8,128)(2,1)S(1)}, bf16[2,16,16,128]{3,2,1,0:T(8,128)(2,1)S(1)}, u32[]{:S(2)}, u32[]{:S(2)}) collective-permute-start(bf16[2,16,16,128]{3,2,1,0:T(8,128)(2,1)S(1)} %add_group.7), channel_id=1, source_target_pairs={{0,3},{1,2},{2,1},{3,0},{4,7},{5,6},{6,5},{7,4},{8,11},{9,10},{10,... | collective-permute-start | bytes 393224 | tf_op jit(solution)/shard_map/ppermute | solution.py:266
Sparse Core Ops, SparseCore 0:
  11.7 26.6 reduce-scatter.1

commit v5 on v4

--- a/solution.py
+++ b/solution.py
@@ -56,14 +56,13 @@
     return one.reshape(4 * P_SIZE, 2 * P_SIZE), turn, two.reshape(2 * P_SIZE, 2 * Q)
 
 
-def channel_kernel(
-    volts, taps, one, twist, two, out, coeff_rows, folded, turned_re, turned_im, stage
-):
-    block = pl.program_id(1)
-    for pol in range(2):
-        for m in range(TAPS):
-            coeff_rows[m, pl.ds(pol, 8, stride=2), :] = taps[m]
-    coeff = [coeff_rows[m] for m in range(TAPS)]
+def channel_kernel(volts, taps, one, twist, two, *refs):
+    out, coeff_rows, folded, turned_re, turned_im, stage = refs[-6:]
+    block = pl.program_id(0)
+    for row in range(16):
+        lane = row // 2 * Q
+        coeff_rows[pl.ds(row, TAPS, stride=16), :] = taps[:, lane : lane + Q]
+    coeff = [coeff_rows[m * 16 : (m + 1) * 16, :] for m in range(TAPS)]
     row0 = pl.multiple_of(block * 16, 16)
     for chunk in range(FRAMES // FRAME_CHUNK):
         first = chunk * FRAME_CHUNK
@@ -128,22 +127,26 @@
     return pl.BlockSpec(shape, lambda *step: (0,) * len(shape))
 
 
-def channelize(volts, taps):
+def channelize(volts, taps, station, earlier=()):
     one, twist, two = dft_tables()
     return pl.pallas_call(
         channel_kernel,
-        grid=(2, 8),
+        grid=(8,),
         in_specs=[
-            pl.BlockSpec((1, 75, 16, Q), lambda s, r: (s, 0, r, 0)),
-            pl.BlockSpec((TAPS, 8, Q), lambda s, r: (0, r, 0)),
+            pl.BlockSpec((1, 75, 16, Q), lambda r: (station, 0, r, 0)),
+            pl.BlockSpec((TAPS, 8 * Q), lambda r: (0, r)),
             whole(256, 128),
             whole(2, 64, Q),
             whole(128, 256),
-        ],
-        out_specs=pl.BlockSpec((2, 2, 4, 4, 4, 1, 32, 128), lambda s, r: (0, 0, 0, 0, 0, s, 0, 0)),
+        ]
+        + [pl.BlockSpec(memory_space=pl.ANY)] * len(earlier),
+        out_specs=pl.BlockSpec(
+            (2, 2, 4, 4, 4, 1, 32, 128), lambda r: (0, 0, 0, 0, 0, station, 0, 0)
+        ),
         out_shape=jax.ShapeDtypeStruct((2, 2, 4, 4, 4, 2, 32, 128), BF16),
+        input_output_aliases={5: 0} if earlier else {},
         scratch_shapes=[
-            pltpu.VMEM((TAPS, 16, Q), F32),
+            pltpu.VMEM((TAPS * 16, Q), F32),
             pltpu.VMEM((FRAMES // 2, 128, 256), BF16),
             pltpu.VMEM((64 * TURN_ROWS, Q), F32),
             pltpu.VMEM((64 * TURN_ROWS, Q), F32),
@@ -151,7 +154,7 @@
         ],
         compiler_params=pltpu.CompilerParams(vmem_limit_bytes=VMEM_LIMIT),
         name="channelize",
-    )(volts, taps, jnp.asarray(one), jnp.asarray(twist), jnp.asarray(two))
+    )(volts, taps, jnp.asarray(one), jnp.asarray(twist), jnp.asarray(two), *earlier)
 
 
 def beam_kernel(where, spectra, base, step, out, wide):
@@ -262,50 +265,60 @@
     )(beam_pos, *[on_chip(part) for part in parts])
 
 
-def swap_beam(value, offset):
-    return lax.ppermute(value, ("yl", "c"), [(b, b ^ offset) for b in range(4)])
-
-
-def station_pick(station_map):
+def station_pick(station_map, zh):
     phys = station_map.reshape(2, 4, 32, 2).transpose(1, 3, 0, 2).reshape(STATIONS)
+    phys = lax.dynamic_slice_in_dim(jnp.concatenate((phys, phys)), zh * 128, STATIONS)
     return (jnp.arange(STATIONS, dtype=jnp.int32)[:, None] == phys[None, :]).astype(F32)
 
 
 def pick_columns(values, pick):
     return jnp.dot(values, pick, precision=lax.Precision.HIGHEST)
+
+
+def shift(value, axis, offset):
+    return lax.ppermute(value, axis, [(n, (n + offset) % 4) for n in range(4)])
+
+
+def swap(value, axes, offset):
+    return lax.ppermute(value, axes, [(n, n ^ offset) for n in range(4)])
+
+
+def choose(index, values):
+    low = jnp.where(index == 0, values[0], values[1])
+    high = jnp.where(index == 2, values[2], values[3])
+    return jnp.where(index < 2, low, high)
 
 
 def on_device(voltages, fir_taps, delays, taper, station_map, beam_order, owners):
     yh, zh, zl, x, yl, c = [lax.axis_index(name) for name in AXES]
     volts = voltages.reshape(2, 2, 75 * P_SIZE, Q).transpose(0, 2, 1, 3).reshape(2, 75, 128, Q)
-    taps = fir_taps.reshape(TAPS, P_SIZE, Q)
     slots = delays.shape[1]
-    stn_pos = ((yh * 4 + zh) * 2 + zl) * 4 + x
     beam_pos = yl * 2 + c
-    owner = owners[beam_pos]
-
-    pick = station_pick(station_map)
-    kept = jnp.where(owner == stn_pos, delays[0], 0.0)
-    model = pick_columns(kept, pick).reshape(slots, 4, 128).transpose(1, 0, 2)
-    model = lax.psum_scatter(model, "zh", scatter_dimension=0, tiled=False)
-    spectra = channelize(volts, taps)
-    model, spectra = lax.optimization_barrier((model, spectra))
-    models = lax.all_to_all(
-        jnp.broadcast_to(model[None], (16, slots, 128)), ("yh", "zl", "x"), 0, 0, tiled=True
-    )
-    source = (owner // 32 * 2 + owner // 4 % 2) * 4 + owner % 4
-    delay = lax.dynamic_index_in_dim(models, source, 0, keepdims=False)
+    owner = jnp.sum(jnp.where(jnp.arange(4, dtype=jnp.int32) == beam_pos, owners, 0))
+    own_yh, own_zh, own_zl, own_x = owner // 32, owner // 8 % 4, owner // 4 % 2, owner % 4
+
+    pick = station_pick(station_map, zh)
+    model = pick_columns(delays[0], pick).reshape(slots, 4, 128).transpose(1, 0, 2)
+    models = [model[0]] + [shift(model[n], "zh", n) for n in range(1, 4)]
+    spectra = channelize(volts, fir_taps, 0)
+    *models, spectra = lax.optimization_barrier((*models, spectra))
+    delay = choose((zh - own_zh) % 4, models)
+    models = [delay] + [shift(delay, "x", n) for n in range(1, 4)]
+    spectra = channelize(volts, fir_taps, 1, (spectra,))
+    *models, spectra = lax.optimization_barrier((*models, spectra))
+    delay = choose((x - own_x) % 4, models)
+    models = [delay] + [swap(delay, ("yh", "zl"), n) for n in range(1, 4)]
+    gain = pick_columns(taper[beam_order], pick[:, :128])
+    *models, gain = lax.optimization_barrier((*models, gain))
+    delay = choose((yh * 2 + zl) ^ (own_yh * 2 + own_zl), models)
     delay, spectra = lax.optimization_barrier((delay, spectra))
-    delays_by_offset = [delay] + [swap_beam(delay, n) for n in range(1, 4)]
+    models = [delay] + [swap(delay, ("yl", "c"), n) for n in range(1, 4)]
     turned = lax.all_to_all(spectra.reshape(64, 4, 64, 128), TURN, 0, 0, tiled=True)
 
-    models = delays_by_offset
     for bit in (1, 2):
         odd = beam_pos & bit != 0
         models = [jnp.where(odd, models[n ^ bit], models[n]) for n in range(4)]
     delay = jnp.concatenate(models, axis=0)
-    gain = pick_columns(taper[beam_order], pick)
-    gain = lax.dynamic_slice_in_dim(gain, zh * 128, 128, 1)
     first_chan = yh * 2048 + zl * 256 + x * 64 + beam_pos * 16
     unit = TWO_PI / (P_SIZE * Q)
     step = jnp.stack((jnp.cos(delay * unit), jnp.sin(delay * unit)))
@@ -316,13 +329,13 @@
         base = jnp.stack((gain * jnp.cos(phase), gain * jnp.sin(phase)))
         part = form_beams(target[None], turned, base, step)
         if dz:
-            part = lax.ppermute(part, "zh", [(z, (z + dz) % 4) for z in range(4)])
+            part = shift(part, "zh", dz)
         parts.append(part)
     pos = beam_pos.astype(jnp.int32)[None]
     quarters = {}
     for n in (2, 3, 1, 0):
         quarter = add_group(n, pos, parts)
-        quarters[n] = swap_beam(quarter, n) if n else quarter
+        quarters[n] = swap(quarter, ("yl", "c"), n) if n else quarter
     out_re, out_im = merge(pos, [quarters[n] for n in range(4)])
     return (out_re, out_im)
 

time: 190 us -> 181 us (0.953)
  between operations: 17.5 us -> 3.56 us
  starting transfers between devices: 27.8 us -> 39.2 us
  waiting for transfers between devices: 104 us -> 99.5 us
  local copies, waits for them, and re-layouts: 6.23 us -> 1.81 us
    ppermute x9 -> x18, starting transfers between devices: 11.7 us -> 30.2 us  [the longest x9 20.8 us: shift(): return lax.ppermute(value, axis, [(n, (n + offset) % 4) for n in range(4)])]
    all_to_all x1 -> x0, starting transfers between devices: 6.64 us -> none  [on_device(): lax.all_to_all(jnp.broadcast_to(model[None], (16, slots, 128)), ('yh', 'z...]
    all_to_all x1 -> x0, waiting for transfers between devices: 5.48 us -> none  [on_device(): lax.all_to_all(jnp.broadcast_to(model[None], (16, slots, 128)), ('yh', 'z...]
    ppermute x9 -> x18, waiting for transfers between devices: 92.3 us -> 97.5 us  [the longest x9 56.7 us: swap(): return lax.ppermute(value, axes, [(n, n ^ offset) for n in range(4)])]
    reduce_scatter x1 -> x0, waiting for transfers between devices: 4.88 us -> none  [on_device(): model = lax.psum_scatter(model, 'zh', scatter_dimension=0, tiled=False)]
    pallas_call x1 -> x2, Pallas kernels: 20 us -> 21.7 us  [channelize(): pl.pallas_call(channel_kernel, grid=(8,), in_specs=[pl.BlockSpec((1, 75,...]
  transfers between devices with their start and end apart: 12 -> 19, of which waited for: 9 -> 9; matrix products, arithmetic and copies ran while one was open for 2% -> 2% of each run, Pallas kernels for 14% -> 15%
where the time goes in v5:
time: 181 us; the launch traced here: 179 us
  waiting for transfers between devices  99.5 us (55%)
  starting transfers between devices  39.2 us (22%)
  Pallas kernels  31.1 us (17%)
  between operations  3.56 us (2%)
  other arithmetic  2.82 us (2%)
  local copies, waits for them, and re-layouts  1.81 us (1%)
    ppermute x9, waiting for transfers between devices, swap(): return lax.ppermute(value, axes, [(n, n ^ offset) for n in range(4)])  56.7 us
    ppermute x9, waiting for transfers between devices, shift(): return lax.ppermute(value, axis, [(n, (n + offset) % 4) for n in range(4)])  40.8 us
    pallas_call x2, Pallas kernels, channelize(): pl.pallas_call(channel_kernel, grid=(8,), in_specs=[pl.BlockSpec((1, 75,...  21.7 us
    ppermute x9, starting transfers between devices, shift(): return lax.ppermute(value, axis, [(n, (n + offset) % 4) for n in range(4)])  20.8 us
    ppermute x9, starting transfers between devices, swap(): return lax.ppermute(value, axes, [(n, n ^ offset) for n in range(4)])  9.34 us
    all_to_all x1, starting transfers between devices, on_device(): lax.all_to_all(spectra.reshape(64, 4, 64, 128), TURN, 0, 0, tiled=True)  9.08 us
    pallas_call x4, Pallas kernels, form_beams(): pl.pallas_call(beam_kernel, grid_spec=pltpu.PrefetchScalarGridSpec(num_sc...  7.44 us
  transfers between devices with their start and end apart: 19, of which 9 were waited for; matrix products, arithmetic and copies ran while one was open for 2% of the time, Pallas kernels for 15%

profile of v5, /device:TPU:1, one launch (start us, length us, event | category | flops | bytes accessed | tf_op | source)
XLA Modules:
  0.0 179.5 jit_solution(13627094434165409132)
XLA Ops:
  0.7 0.9 reshape.100
  1.8 1.2 convolution_bitcast_fusion
  3.0 3.9 %collective-permute-start = (f32[16,128]{1,0:T(8,128)S(1)}, f32[16,128]{1,0:T(8,128)S(1)}, u32[]{:S(2)}, u32[]{:S(2)}) collective-permute-start(f32[16,128]{1,0:T(8,128)S(1)} %get-tuple-element.52), channel_id=1, source_target_pairs={{0,32},{32,64},{64,96},{96,0},{1,33},{33,65},{65,97},{97,1},{2,34}... | collective-permute-start | bytes 24584 | tf_op jit(solution)/shard_map/ppermute | solution.py:279
  6.9 5.1 %collective-permute-start.1 = (f32[16,128]{1,0:T(8,128)S(1)}, f32[16,128]{1,0:T(8,128)S(1)}, u32[]{:S(2)}, u32[]{:S(2)}) collective-permute-start(f32[16,128]{1,0:T(8,128)S(1)} %get-tuple-element.51), channel_id=1, source_target_pairs={{0,64},{32,96},{64,0},{96,32},{1,65},{33,97},{65,1},{97,33},{2,66}... | collective-permute-start | bytes 24584 | tf_op jit(solution)/shard_map/ppermute | solution.py:279
  12.0 2.4 %collective-permute-start.2 = (f32[16,128]{1,0:T(8,128)S(1)}, f32[16,128]{1,0:T(8,128)S(1)}, u32[]{:S(2)}, u32[]{:S(2)}) collective-permute-start(f32[16,128]{1,0:T(8,128)S(1)} %get-tuple-element.50), channel_id=1, source_target_pairs={{0,96},{32,0},{64,32},{96,64},{1,97},{33,1},{65,33},{97,65},{2,98}... | collective-permute-start | bytes 24584 | tf_op jit(solution)/shard_map/ppermute | solution.py:279
  15.2 1.3 fusion.5
  19.2 10.8 %channelize.2.refs_0_ = bf16[2,2,4,4,4,2,32,128]{7,6,5,4,3,2,1,0:T(8,128)(2,1)} custom-call(bf16[2,75,128,128]{3,2,1,0:T(8,128)(2,1)} %bitcast.54, f32[12,8192]{1,0:T(8,128)} %taps.3, bf16[256,128]{1,0:T(8,128)(2,1)} %constant.133.clone.one, f32[2,64,128]{2,1,0:T(8,128)} %constant.134.clone.twist, bf16[128,256]{1,0:T(8,128)(2,1)} %constant.135.clone.two), custom_call_target="tpu_custom_call" | custom-call | tf_op jit(solution)/shard_map/channelize/pallas_call | solution.py:132
  30.0 1.3 collective-permute-start.3
  31.3 2.5 %collective-permute-start.4 = (f32[16,128]{1,0:T(8,128)S(1)}, f32[16,128]{1,0:T(8,128)S(1)}, u32[]{:S(2)}, u32[]{:S(2)}) collective-permute-start(f32[16,128]{1,0:T(8,128)S(1)} %select_select_fusion.2), channel_id=1, source_target_pairs={{0,8},{4,12},{8,0},{12,4},{1,9},{5,13},{9,1},{13,5},{2,10},{6,14},... | collective-permute-start | bytes 24584 | tf_op jit(solution)/shard_map/ppermute | solution.py:279
  33.8 1.1 collective-permute-start.5
  35.6 10.9 %channelize.3 = bf16[2,2,4,4,4,2,32,128]{7,6,5,4,3,2,1,0:T(8,128)(2,1)} custom-call(bf16[2,75,128,128]{3,2,1,0:T(8,128)(2,1)} %bitcast.55, f32[12,8192]{1,0:T(8,128)} %taps.3, bf16[256,128]{1,0:T(8,128)(2,1)} %constant.133.clone.one, f32[2,64,128]{2,1,0:T(8,128)} %constant.134.clone.twist, ...), custom_call_target="tpu_custom_call", output_to_operand_aliasing={{}: (5, {})} | custom-call | tf_op jit(solution)/shard_map/channelize/pallas_call | solution.py:132
  46.5 0.8 collective-permute-start.6
  47.3 2.9 %collective-permute-start.7 = (f32[16,128]{1,0:T(8,128)S(1)}, f32[16,128]{1,0:T(8,128)S(1)}, u32[]{:S(2)}, u32[]{:S(2)}) collective-permute-start(f32[16,128]{1,0:T(8,128)S(1)} %select_select_fusion.1), channel_id=1, source_target_pairs={{0,128},{16,144},{128,0},{144,16},{1,129},{17,145},{129,1},{145,17... | collective-permute-start | bytes 24584 | tf_op jit(solution)/shard_map/ppermute | solution.py:283
  51.3 3.8 %collective-permute-done.8 = f32[16,128]{1,0:T(8,128)S(1)} collective-permute-done((f32[16,128]{1,0:T(8,128)S(1)}, f32[16,128]{1,0:T(8,128)S(1)}, u32[]{:S(2)}, u32[]{:S(2)}) %collective-permute-start.8) | collective-permute-done | bytes 8224 | tf_op jit(solution)/shard_map/ppermute | solution.py:283
  55.2 9.1 %all-to-all-start = ((bf16[64,4,64,128]{3,2,1,0:T(8,128)(2,1)}), bf16[64,4,64,128]{3,2,1,0:T(8,128)(2,1)}, u32[]{:S(2)}, u32[]{:S(2)}) async-start(bf16[64,4,64,128]{3,2,1,0:T(8,128)(2,1)} %bitcast.53), calls=%async_computation | async-start | bytes 8388608 | tf_op jit(solution)/shard_map/all_to_all | solution.py:316
  64.3 1.7 collective-permute-start.9
  66.5 46.2 %collective-permute-done.9 = f32[16,128]{1,0:T(8,128)S(1)} collective-permute-done((f32[16,128]{1,0:T(8,128)S(1)}, f32[16,128]{1,0:T(8,128)S(1)}, u32[]{:S(2)}, u32[]{:S(2)}) %collective-permute-start.9) | collective-permute-done | bytes 8224 | tf_op jit(solution)/shard_map/ppermute | solution.py:283
  113.5 2.0 %all-to-all-done.spectra = bf16[64,4,64,128]{3,2,1,0:T(8,128)(2,1)} async-done(((bf16[64,4,64,128]{3,2,1,0:T(8,128)(2,1)}), bf16[64,4,64,128]{3,2,1,0:T(8,128)(2,1)}, u32[]{:S(2)}, u32[]{:S(2)}) %all-to-all-start) | async-done | bytes 4194336 | tf_op jit(solution)/shard_map/all_to_all | solution.py:316
  115.5 1.9 %form_beams.4 = bf16[4,2,16,16,128]{4,3,2,1,0:T(8,128)(2,1)S(1)} custom-call(s32[1]{0:T(128)} %bitcast.1.where, bf16[64,4,64,128]{3,2,1,0:T(8,128)(2,1)} %all-to-all-done.spectra, f32[2,64,128]{2,1,0:T(8,128)S(1)} %pad_maximum_fusion.base, f32[2,64,128]{2,1,0:T(8,128)S(1)} %get-tuple-element.54.step), custom_call_target="tpu_custom_call" | custom-call | tf_op jit(solution)/shard_map/form_beams/pallas_call | solution.py:196
  117.3 0.8 collective-permute-start.12
  118.2 1.9 %form_beams.5 = bf16[4,2,16,16,128]{4,3,2,1,0:T(8,128)(2,1)S(1)} custom-call(s32[1]{0:T(128)} %bitcast.22.where, bf16[64,4,64,128]{3,2,1,0:T(8,128)(2,1)} %all-to-all-done.spectra, f32[2,64,128]{2,1,0:T(8,128)S(1)} %pad_maximum_fusion.2.base, f32[2,64,128]{2,1,0:T(8,128)S(1)} %get-tuple-element.54.step), custom_call_target="tpu_custom_call" | custom-call | tf_op jit(solution)/shard_map/form_beams/pallas_call | solution.py:196
  120.0 1.2 collective-permute-start.13
  121.2 1.9 %form_beams.6 = bf16[4,2,16,16,128]{4,3,2,1,0:T(8,128)(2,1)S(1)} custom-call(s32[1]{0:T(128)} %bitcast.25.where, bf16[64,4,64,128]{3,2,1,0:T(8,128)(2,1)} %all-to-all-done.spectra, f32[2,64,128]{2,1,0:T(8,128)S(1)} %get-tuple-element.55.base, f32[2,64,128]{2,1,0:T(8,128)S(1)} %get-tuple-element.54.step), custom_call_target="tpu_custom_call" | custom-call | tf_op jit(solution)/shard_map/form_beams/pallas_call | solution.py:196
  123.1 2.6 %collective-permute-start.14 = (bf16[4,2,16,16,128]{4,3,2,1,0:T(8,128)(2,1)S(1)}, bf16[4,2,16,16,128]{4,3,2,1,0:T(8,128)(2,1)S(1)}, u32[]{:S(2)}, u32[]{:S(2)}) collective-permute-start(bf16[4,2,16,16,128]{4,3,2,1,0:T(8,128)(2,1)S(1)} %form_beams.6), channel_id=1, source_target_pairs={{0,96},{32,0},{64,32},{96,64},{1,97},{33,1},{65,33},{97,65},{2,98}... | collective-permute-start | bytes 1572872 | tf_op jit(solution)/shard_map/ppermute | solution.py:279
  125.6 1.9 %form_beams.7.refs_3_ = bf16[4,2,16,16,128]{4,3,2,1,0:T(8,128)(2,1)S(1)} custom-call(s32[1]{0:T(128)} %bitcast.28.where, bf16[64,4,64,128]{3,2,1,0:T(8,128)(2,1)} %all-to-all-done.spectra, f32[2,64,128]{2,1,0:T(8,128)S(1)} %pad_maximum_fusion.4.base, f32[2,64,128]{2,1,0:T(8,128)S(1)} %get-tuple-element.54.step), custom_call_target="tpu_custom_call" | custom-call | tf_op jit(solution)/shard_map/form_beams/pallas_call | solution.py:196
  127.5 16.6 %collective-permute-done.12.refs_0_ = bf16[4,2,16,16,128]{4,3,2,1,0:T(8,128)(2,1)S(1)} collective-permute-done((bf16[4,2,16,16,128]{4,3,2,1,0:T(8,128)(2,1)S(1)}, bf16[4,2,16,16,128]{4,3,2,1,0:T(8,128)(2,1)S(1)}, u32[]{:S(2)}, u32[]{:S(2)}) %collective-permute-start.12) | collective-permute-done | bytes 524320 | tf_op jit(solution)/shard_map/ppermute | solution.py:279
  144.1 9.8 %collective-permute-done.13.refs_1_ = bf16[4,2,16,16,128]{4,3,2,1,0:T(8,128)(2,1)S(1)} collective-permute-done((bf16[4,2,16,16,128]{4,3,2,1,0:T(8,128)(2,1)S(1)}, bf16[4,2,16,16,128]{4,3,2,1,0:T(8,128)(2,1)S(1)}, u32[]{:S(2)}, u32[]{:S(2)}) %collective-permute-start.13) | collective-permute-done | bytes 524320 | tf_op jit(solution)/shard_map/ppermute | solution.py:279
  153.9 14.3 %collective-permute-done.14.refs_2_ = bf16[4,2,16,16,128]{4,3,2,1,0:T(8,128)(2,1)S(1)} collective-permute-done((bf16[4,2,16,16,128]{4,3,2,1,0:T(8,128)(2,1)S(1)}, bf16[4,2,16,16,128]{4,3,2,1,0:T(8,128)(2,1)S(1)}, u32[]{:S(2)}, u32[]{:S(2)}) %collective-permute-start.14) | collective-permute-done | bytes 524320 | tf_op jit(solution)/shard_map/ppermute | solution.py:279
  169.0 2.2 %collective-permute-start.16 = (bf16[2,16,16,128]{3,2,1,0:T(8,128)(2,1)S(1)}, bf16[2,16,16,128]{3,2,1,0:T(8,128)(2,1)S(1)}, u32[]{:S(2)}, u32[]{:S(2)}) collective-permute-start(bf16[2,16,16,128]{3,2,1,0:T(8,128)(2,1)S(1)} %add_group.6), channel_id=1, source_target_pairs={{0,2},{1,3},{2,0},{3,1},{4,6},{5,7},{6,4},{7,5},{8,10},{9,11},{10,... | collective-permute-start | bytes 393224 | tf_op jit(solution)/shard_map/ppermute | solution.py:283
  171.4 3.6 %collective-permute-done.16.refs_2_ = bf16[2,16,16,128]{3,2,1,0:T(8,128)(2,1)S(1)} collective-permute-done((bf16[2,16,16,128]{3,2,1,0:T(8,128)(2,1)S(1)}, bf16[2,16,16,128]{3,2,1,0:T(8,128)(2,1)S(1)}, u32[]{:S(2)}, u32[]{:S(2)}) %collective-permute-start.16) | collective-permute-done | bytes 131104 | tf_op jit(solution)/shard_map/ppermute | solution.py:283
  175.0 2.8 %collective-permute-done.17.refs_3_ = bf16[2,16,16,128]{3,2,1,0:T(8,128)(2,1)S(1)} collective-permute-done((bf16[2,16,16,128]{3,2,1,0:T(8,128)(2,1)S(1)}, bf16[2,16,16,128]{3,2,1,0:T(8,128)(2,1)S(1)}, u32[]{:S(2)}, u32[]{:S(2)}) %collective-permute-start.17) | collective-permute-done | bytes 131104 | tf_op jit(solution)/shard_map/ppermute | solution.py:283
  177.8 1.6 merge.1
  (44 shorter events, 5.0 us)
Async XLA Ops:
  0.6 34.3 %copy-start = (f32[64,512]{1,0:T(8,128)S(1)}, f32[64,512]{1,0:T(8,128)}, u32[]{:S(2)}) copy-start(f32[64,512]{1,0:T(8,128)} %param.16) | copy-start | bytes 393220
  3.0 27.0 %collective-permute-start = (f32[16,128]{1,0:T(8,128)S(1)}, f32[16,128]{1,0:T(8,128)S(1)}, u32[]{:S(2)}, u32[]{:S(2)}) collective-permute-start(f32[16,128]{1,0:T(8,128)S(1)} %get-tuple-element.52), channel_id=1, source_target_pairs={{0,32},{32,64},{64,96},{96,0},{1,33},{33,65},{65,97},{97,1},{2,34}... | collective-permute-start | bytes 24584 | tf_op jit(solution)/shard_map/ppermute | solution.py:279
  6.9 23.1 %collective-permute-start.1 = (f32[16,128]{1,0:T(8,128)S(1)}, f32[16,128]{1,0:T(8,128)S(1)}, u32[]{:S(2)}, u32[]{:S(2)}) collective-permute-start(f32[16,128]{1,0:T(8,128)S(1)} %get-tuple-element.51), channel_id=1, source_target_pairs={{0,64},{32,96},{64,0},{96,32},{1,65},{33,97},{65,1},{97,33},{2,66}... | collective-permute-start | bytes 24584 | tf_op jit(solution)/shard_map/ppermute | solution.py:279
  12.0 18.0 %collective-permute-start.2 = (f32[16,128]{1,0:T(8,128)S(1)}, f32[16,128]{1,0:T(8,128)S(1)}, u32[]{:S(2)}, u32[]{:S(2)}) collective-permute-start(f32[16,128]{1,0:T(8,128)S(1)} %get-tuple-element.50), channel_id=1, source_target_pairs={{0,96},{32,0},{64,32},{96,64},{1,97},{33,1},{65,33},{97,65},{2,98}... | collective-permute-start | bytes 24584 | tf_op jit(solution)/shard_map/ppermute | solution.py:279
  30.0 16.4 %collective-permute-start.3 = (f32[16,128]{1,0:T(8,128)S(1)}, f32[16,128]{1,0:T(8,128)S(1)}, u32[]{:S(2)}, u32[]{:S(2)}) collective-permute-start(f32[16,128]{1,0:T(8,128)S(1)} %select_select_fusion.2), channel_id=1, source_target_pairs={{0,4},{4,8},{8,12},{12,0},{1,5},{5,9},{9,13},{13,1},{2,6},{6,10},{... | collective-permute-start | bytes 24584 | tf_op jit(solution)/shard_map/ppermute | solution.py:279
  31.3 15.2 %collective-permute-start.4 = (f32[16,128]{1,0:T(8,128)S(1)}, f32[16,128]{1,0:T(8,128)S(1)}, u32[]{:S(2)}, u32[]{:S(2)}) collective-permute-start(f32[16,128]{1,0:T(8,128)S(1)} %select_select_fusion.2), channel_id=1, source_target_pairs={{0,8},{4,12},{8,0},{12,4},{1,9},{5,13},{9,1},{13,5},{2,10},{6,14},... | collective-permute-start | bytes 24584 | tf_op jit(solution)/shard_map/ppermute | solution.py:279
  33.8 12.7 %collective-permute-start.5 = (f32[16,128]{1,0:T(8,128)S(1)}, f32[16,128]{1,0:T(8,128)S(1)}, u32[]{:S(2)}, u32[]{:S(2)}) collective-permute-start(f32[16,128]{1,0:T(8,128)S(1)} %select_select_fusion.2), channel_id=1, source_target_pairs={{0,12},{4,0},{8,4},{12,8},{1,13},{5,1},{9,5},{13,9},{2,14},{6,2},{... | collective-permute-start | bytes 24584 | tf_op jit(solution)/shard_map/ppermute | solution.py:279
  46.5 4.5 %collective-permute-start.6 = (f32[16,128]{1,0:T(8,128)S(1)}, f32[16,128]{1,0:T(8,128)S(1)}, u32[]{:S(2)}, u32[]{:S(2)}) collective-permute-start(f32[16,128]{1,0:T(8,128)S(1)} %select_select_fusion.1), channel_id=1, source_target_pairs={{0,16},{16,0},{128,144},{144,128},{1,17},{17,1},{129,145},{145,129... | collective-permute-start | bytes 24584 | tf_op jit(solution)/shard_map/ppermute | solution.py:283
  47.3 4.0 %collective-permute-start.7 = (f32[16,128]{1,0:T(8,128)S(1)}, f32[16,128]{1,0:T(8,128)S(1)}, u32[]{:S(2)}, u32[]{:S(2)}) collective-permute-start(f32[16,128]{1,0:T(8,128)S(1)} %select_select_fusion.1), channel_id=1, source_target_pairs={{0,128},{16,144},{128,0},{144,16},{1,129},{17,145},{129,1},{145,17... | collective-permute-start | bytes 24584 | tf_op jit(solution)/shard_map/ppermute | solution.py:283
  50.3 4.9 %collective-permute-start.8 = (f32[16,128]{1,0:T(8,128)S(1)}, f32[16,128]{1,0:T(8,128)S(1)}, u32[]{:S(2)}, u32[]{:S(2)}) collective-permute-start(f32[16,128]{1,0:T(8,128)S(1)} %select_select_fusion.1), channel_id=1, source_target_pairs={{0,144},{16,128},{128,16},{144,0},{1,145},{17,129},{129,17},{145,1... | collective-permute-start | bytes 24584 | tf_op jit(solution)/shard_map/ppermute | solution.py:283
  55.2 60.3 %all-to-all-start = ((bf16[64,4,64,128]{3,2,1,0:T(8,128)(2,1)}), bf16[64,4,64,128]{3,2,1,0:T(8,128)(2,1)}, u32[]{:S(2)}, u32[]{:S(2)}) async-start(bf16[64,4,64,128]{3,2,1,0:T(8,128)(2,1)} %bitcast.53), calls=%async_computation | async-start | bytes 8388608 | tf_op jit(solution)/shard_map/all_to_all | solution.py:316
  64.3 48.5 %collective-permute-start.9 = (f32[16,128]{1,0:T(8,128)S(1)}, f32[16,128]{1,0:T(8,128)S(1)}, u32[]{:S(2)}, u32[]{:S(2)}) collective-permute-start(f32[16,128]{1,0:T(8,128)S(1)} %select_select_fusion), channel_id=1, source_target_pairs={{0,3},{1,2},{2,1},{3,0},{4,7},{5,6},{6,5},{7,4},{8,11},{9,10},{10,... | collective-permute-start | bytes 24584 | tf_op jit(solution)/shard_map/ppermute | solution.py:283
  66.0 46.7 %collective-permute-start.10 = (f32[16,128]{1,0:T(8,128)S(1)}, f32[16,128]{1,0:T(8,128)S(1)}, u32[]{:S(2)}, u32[]{:S(2)}) collective-permute-start(f32[16,128]{1,0:T(8,128)S(1)} %select_select_fusion), channel_id=1, source_target_pairs={{0,2},{1,3},{2,0},{3,1},{4,6},{5,7},{6,4},{7,5},{8,10},{9,11},{10,... | collective-permute-start | bytes 24584 | tf_op jit(solution)/shard_map/ppermute | solution.py:283
  66.3 46.4 %collective-permute-start.11 = (f32[16,128]{1,0:T(8,128)S(1)}, f32[16,128]{1,0:T(8,128)S(1)}, u32[]{:S(2)}, u32[]{:S(2)}) collective-permute-start(f32[16,128]{1,0:T(8,128)S(1)} %select_select_fusion), channel_id=1, source_target_pairs={{0,1},{1,0},{2,3},{3,2},{4,5},{5,4},{6,7},{7,6},{8,9},{9,8},{10,11... | collective-permute-start | bytes 24584 | tf_op jit(solution)/shard_map/ppermute | solution.py:283
  117.3 26.8 %collective-permute-start.12 = (bf16[4,2,16,16,128]{4,3,2,1,0:T(8,128)(2,1)S(1)}, bf16[4,2,16,16,128]{4,3,2,1,0:T(8,128)(2,1)S(1)}, u32[]{:S(2)}, u32[]{:S(2)}) collective-permute-start(bf16[4,2,16,16,128]{4,3,2,1,0:T(8,128)(2,1)S(1)} %form_beams.4), channel_id=1, source_target_pairs={{0,64},{32,96},{64,0},{96,32},{1,65},{33,97},{65,1},{97,33},{2,66}... | collective-permute-start | bytes 1572872 | tf_op jit(solution)/shard_map/ppermute | solution.py:279
  120.0 33.9 %collective-permute-start.13 = (bf16[4,2,16,16,128]{4,3,2,1,0:T(8,128)(2,1)S(1)}, bf16[4,2,16,16,128]{4,3,2,1,0:T(8,128)(2,1)S(1)}, u32[]{:S(2)}, u32[]{:S(2)}) collective-permute-start(bf16[4,2,16,16,128]{4,3,2,1,0:T(8,128)(2,1)S(1)} %form_beams.5), channel_id=1, source_target_pairs={{0,32},{32,64},{64,96},{96,0},{1,33},{33,65},{65,97},{97,1},{2,34}... | collective-permute-start | bytes 1572872 | tf_op jit(solution)/shard_map/ppermute | solution.py:279
  123.1 45.2 %collective-permute-start.14 = (bf16[4,2,16,16,128]{4,3,2,1,0:T(8,128)(2,1)S(1)}, bf16[4,2,16,16,128]{4,3,2,1,0:T(8,128)(2,1)S(1)}, u32[]{:S(2)}, u32[]{:S(2)}) collective-permute-start(bf16[4,2,16,16,128]{4,3,2,1,0:T(8,128)(2,1)S(1)} %form_beams.6), channel_id=1, source_target_pairs={{0,96},{32,0},{64,32},{96,64},{1,97},{33,1},{65,33},{97,65},{2,98}... | collective-permute-start | bytes 1572872 | tf_op jit(solution)/shard_map/ppermute | solution.py:279
  168.3 3.1 %collective-permute-start.15 = (bf16[2,16,16,128]{3,2,1,0:T(8,128)(2,1)S(1)}, bf16[2,16,16,128]{3,2,1,0:T(8,128)(2,1)S(1)}, u32[]{:S(2)}, u32[]{:S(2)}) collective-permute-start(bf16[2,16,16,128]{3,2,1,0:T(8,128)(2,1)S(1)} %add_group.5), channel_id=1, source_target_pairs={{0,1},{1,0},{2,3},{3,2},{4,5},{5,4},{6,7},{7,6},{8,9},{9,8},{10,11... | collective-permute-start | bytes 393224 | tf_op jit(solution)/shard_map/ppermute | solution.py:283
  169.0 6.1 %collective-permute-start.16 = (bf16[2,16,16,128]{3,2,1,0:T(8,128)(2,1)S(1)}, bf16[2,16,16,128]{3,2,1,0:T(8,128)(2,1)S(1)}, u32[]{:S(2)}, u32[]{:S(2)}) collective-permute-start(bf16[2,16,16,128]{3,2,1,0:T(8,128)(2,1)S(1)} %add_group.6), channel_id=1, source_target_pairs={{0,2},{1,3},{2,0},{3,1},{4,6},{5,7},{6,4},{7,5},{8,10},{9,11},{10,... | collective-permute-start | bytes 393224 | tf_op jit(solution)/shard_map/ppermute | solution.py:283
  171.2 6.6 %collective-permute-start.17 = (bf16[2,16,16,128]{3,2,1,0:T(8,128)(2,1)S(1)}, bf16[2,16,16,128]{3,2,1,0:T(8,128)(2,1)S(1)}, u32[]{:S(2)}, u32[]{:S(2)}) collective-permute-start(bf16[2,16,16,128]{3,2,1,0:T(8,128)(2,1)S(1)} %add_group.7), channel_id=1, source_target_pairs={{0,3},{1,2},{2,1},{3,0},{4,7},{5,6},{6,5},{7,4},{8,11},{9,10},{10,... | collective-permute-start | bytes 393224 | tf_op jit(solution)/shard_map/ppermute | solution.py:283

commit v6 on v4

--- a/solution.py
+++ b/solution.py
@@ -60,10 +60,10 @@
     volts, taps, one, twist, two, out, coeff_rows, folded, turned_re, turned_im, stage
 ):
     block = pl.program_id(1)
-    for pol in range(2):
-        for m in range(TAPS):
-            coeff_rows[m, pl.ds(pol, 8, stride=2), :] = taps[m]
-    coeff = [coeff_rows[m] for m in range(TAPS)]
+    for row in range(16):
+        lane = row // 2 * Q
+        coeff_rows[pl.ds(row, TAPS, stride=16), :] = taps[:, lane : lane + Q]
+    coeff = [coeff_rows[m * 16 : (m + 1) * 16, :] for m in range(TAPS)]
     row0 = pl.multiple_of(block * 16, 16)
     for chunk in range(FRAMES // FRAME_CHUNK):
         first = chunk * FRAME_CHUNK
@@ -135,7 +135,7 @@
         grid=(2, 8),
         in_specs=[
             pl.BlockSpec((1, 75, 16, Q), lambda s, r: (s, 0, r, 0)),
-            pl.BlockSpec((TAPS, 8, Q), lambda s, r: (0, r, 0)),
+            pl.BlockSpec((TAPS, 8 * Q), lambda s, r: (0, r)),
             whole(256, 128),
             whole(2, 64, Q),
             whole(128, 256),
@@ -143,7 +143,7 @@
         out_specs=pl.BlockSpec((2, 2, 4, 4, 4, 1, 32, 128), lambda s, r: (0, 0, 0, 0, 0, s, 0, 0)),
         out_shape=jax.ShapeDtypeStruct((2, 2, 4, 4, 4, 2, 32, 128), BF16),
         scratch_shapes=[
-            pltpu.VMEM((TAPS, 16, Q), F32),
+            pltpu.VMEM((TAPS * 16, Q), F32),
             pltpu.VMEM((FRAMES // 2, 128, 256), BF16),
             pltpu.VMEM((64 * TURN_ROWS, Q), F32),
             pltpu.VMEM((64 * TURN_ROWS, Q), F32),
@@ -154,7 +154,7 @@
     )(volts, taps, jnp.asarray(one), jnp.asarray(twist), jnp.asarray(two))
 
 
-def beam_kernel(where, spectra, base, step, out, wide):
+def beam_kernel(where, spectra, base, step, out_re, out_im, wide):
     del where
     for src in range(64):
         wide[src * WIDE_ROWS : src * WIDE_ROWS + 64, :] = spectra[src, 0].astype(F32)
@@ -178,10 +178,10 @@
             axis=0,
         )
         part = jnp.dot(left, right, preferred_element_type=F32)
-        for ri in range(2):
+        for ri, out in enumerate((out_re, out_im)):
             for group in range(4):
                 row = ri * 64 + group * 16
-                out[group, ri, i] = part[row : row + 16].astype(BF16)
+                out[group, i] = part[row : row + 16].astype(BF16)
         if i < 15:
             cos_w, sin_w = (
                 cos_w * cos_step - sin_w * sin_step,
@@ -200,32 +200,51 @@
                 CHIP,
                 CHIP,
             ],
-            out_specs=CHIP,
+            out_specs=[CHIP, CHIP],
             scratch_shapes=[pltpu.VMEM((64 * WIDE_ROWS, 128), F32)],
         ),
-        out_shape=pltpu.VMEM((4, 2, 16, 16, 128), BF16),
+        out_shape=[pltpu.VMEM((4, 16, 16, 128), BF16)] * 2,
         compiler_params=pltpu.CompilerParams(vmem_limit_bytes=SMALL_LIMIT),
         name="form_beams",
     )(where, spectra, on_chip(base), on_chip(step))
 
 
+def add_pair_kernel(one, other, out):
+    for group in range(4):
+        out[group] = (one[group].astype(F32) + other[group].astype(F32)).astype(BF16)
+
+
+def add_pair(one, other):
+    return pl.pallas_call(
+        add_pair_kernel,
+        in_specs=[CHIP, CHIP],
+        out_specs=CHIP,
+        out_shape=pltpu.VMEM((4, 16, 16, 128), BF16),
+        compiler_params=pltpu.CompilerParams(vmem_limit_bytes=SMALL_LIMIT),
+        name="add_pair",
+    )(on_chip(one), on_chip(other))
+
+
 def add_kernel(offset, beam_pos, *refs):
     group = beam_pos[0] ^ offset
-    total = refs[0][group].astype(F32)
-    for part in refs[1:-1]:
-        total = total + part[group].astype(F32)
-    refs[-1][...] = total.astype(BF16)
+    parts, out = refs[:-1], refs[-1]
+    for ri in range(2):
+        total = parts[ri][group].astype(F32)
+        for part in parts[2 + ri :: 2]:
+            total = total + part[group].astype(F32)
+        out[ri] = total.astype(BF16)
 
 
 def add_group(offset, beam_pos, parts):
+    flat = [on_chip(value) for pair in parts for value in pair]
     return pl.pallas_call(
         functools.partial(add_kernel, offset),
-        in_specs=[SCALAR] + [CHIP] * len(parts),
+        in_specs=[SCALAR] + [CHIP] * len(flat),
         out_specs=CHIP,
         out_shape=pltpu.VMEM((2, 16, 16, 128), BF16),
         compiler_params=pltpu.CompilerParams(vmem_limit_bytes=SMALL_LIMIT),
         name="add_group",
-    )(beam_pos, *[on_chip(part) for part in parts])
+    )(beam_pos, *flat)
 
 
 def merge_kernel(beam_pos, *refs):
@@ -262,10 +281,6 @@
     )(beam_pos, *[on_chip(part) for part in parts])
 
 
-def swap_beam(value, offset):
-    return lax.ppermute(value, ("yl", "c"), [(b, b ^ offset) for b in range(4)])
-
-
 def station_pick(station_map):
     phys = station_map.reshape(2, 4, 32, 2).transpose(1, 3, 0, 2).reshape(STATIONS)
     return (jnp.arange(STATIONS, dtype=jnp.int32)[:, None] == phys[None, :]).astype(F32)
@@ -275,31 +290,31 @@
     return jnp.dot(values, pick, precision=lax.Precision.HIGHEST)
 
 
+def shift(value, axis, offset):
+    return lax.ppermute(value, axis, [(n, (n + offset) % 4) for n in range(4)])
+
+
+def swap(value, axes, offset):
+    return lax.ppermute(value, axes, [(n, n ^ offset) for n in range(4)])
+
+
 def on_device(voltages, fir_taps, delays, taper, station_map, beam_order, owners):
     yh, zh, zl, x, yl, c = [lax.axis_index(name) for name in AXES]
     volts = voltages.reshape(2, 2, 75 * P_SIZE, Q).transpose(0, 2, 1, 3).reshape(2, 75, 128, Q)
-    taps = fir_taps.reshape(TAPS, P_SIZE, Q)
     slots = delays.shape[1]
-    stn_pos = ((yh * 4 + zh) * 2 + zl) * 4 + x
     beam_pos = yl * 2 + c
-    owner = owners[beam_pos]
 
     pick = station_pick(station_map)
-    kept = jnp.where(owner == stn_pos, delays[0], 0.0)
-    model = pick_columns(kept, pick).reshape(slots, 4, 128).transpose(1, 0, 2)
-    model = lax.psum_scatter(model, "zh", scatter_dimension=0, tiled=False)
-    spectra = channelize(volts, taps)
-    model, spectra = lax.optimization_barrier((model, spectra))
-    models = lax.all_to_all(
-        jnp.broadcast_to(model[None], (16, slots, 128)), ("yh", "zl", "x"), 0, 0, tiled=True
-    )
-    source = (owner // 32 * 2 + owner // 4 % 2) * 4 + owner % 4
-    delay = lax.dynamic_index_in_dim(models, source, 0, keepdims=False)
+    model = pick_columns(delays[0], pick).reshape(slots, 4, 128).transpose(1, 0, 2)
+    model = jnp.broadcast_to(model[None, :, None], (2, 4, 8, slots, 128))
+    models = lax.all_to_all(model.reshape(64, slots, 128), AXES[:4], 0, 0, tiled=True)
+    spectra = channelize(volts, fir_taps)
+    models, spectra = lax.optimization_barrier((models, spectra))
+    delay = lax.dynamic_index_in_dim(models, owners[beam_pos], 0, keepdims=False)
     delay, spectra = lax.optimization_barrier((delay, spectra))
-    delays_by_offset = [delay] + [swap_beam(delay, n) for n in range(1, 4)]
+    models = [delay] + [swap(delay, ("yl", "c"), n) for n in range(1, 4)]
     turned = lax.all_to_all(spectra.reshape(64, 4, 64, 128), TURN, 0, 0, tiled=True)
 
-    models = delays_by_offset
     for bit in (1, 2):
         odd = beam_pos & bit != 0
         models = [jnp.where(odd, models[n ^ bit], models[n]) for n in range(4)]
@@ -309,20 +324,28 @@
     first_chan = yh * 2048 + zl * 256 + x * 64 + beam_pos * 16
     unit = TWO_PI / (P_SIZE * Q)
     step = jnp.stack((jnp.cos(delay * unit), jnp.sin(delay * unit)))
-    parts = []
-    for dz in (2, 1, 3, 0):
-        target = (zh + dz) % 4
+
+    def beams_for(offset):
+        target = (zh + offset) % 4
         phase = delay * (first_chan + 512 * target).astype(F32) * unit
         base = jnp.stack((gain * jnp.cos(phase), gain * jnp.sin(phase)))
-        part = form_beams(target[None], turned, base, step)
-        if dz:
-            part = lax.ppermute(part, "zh", [(z, (z + dz) % 4) for z in range(4)])
-        parts.append(part)
+        return form_beams(target[None], turned, base, step)
+
+    far_re, far_im = beams_for(2)
+    far_re, far_im = shift(far_re, "zh", 1), shift(far_im, "zh", 3)
+    up_re, up_im = beams_for(1)
+    up_im = shift(up_im, "zh", 1)
+    down_re, down_im = beams_for(3)
+    down_re = shift(down_re, "zh", 3)
+    own = beams_for(0)
+    up_re = shift(add_pair(up_re, far_re), "zh", 1)
+    down_im = shift(add_pair(down_im, far_im), "zh", 3)
+    parts = [own, (up_re, up_im), (down_re, down_im)]
     pos = beam_pos.astype(jnp.int32)[None]
     quarters = {}
     for n in (2, 3, 1, 0):
         quarter = add_group(n, pos, parts)
-        quarters[n] = swap_beam(quarter, n) if n else quarter
+        quarters[n] = swap(quarter, ("yl", "c"), n) if n else quarter
     out_re, out_im = merge(pos, [quarters[n] for n in range(4)])
     return (out_re, out_im)
 

time: 190 us -> 161 us (0.85)
  waiting for transfers between devices: 104 us -> 70.8 us
  starting transfers between devices: 27.8 us -> 50.5 us
  between operations: 17.5 us -> 2.87 us
  local copies, waits for them, and re-layouts: 6.23 us -> 3.83 us
    ppermute x9 -> x12, waiting for transfers between devices: 92.3 us -> 69.4 us  [the longest x6 51.5 us: swap(): return lax.ppermute(value, axes, [(n, n ^ offset) for n in range(4)])]
    ppermute x9 -> x12, starting transfers between devices: 11.7 us -> 25.8 us  [the longest x6 14.6 us: swap(): return lax.ppermute(value, axes, [(n, n ^ offset) for n in range(4)])]
    all_to_all x1, starting transfers between devices: 6.64 us -> 15.1 us  [on_device(): lax.all_to_all(model.reshape(64, slots, 128), AXES[:4], 0, 0, tiled=True)]
    all_to_all x1, waiting for transfers between devices: 5.48 us -> 0.01 us  [on_device(): lax.all_to_all(model.reshape(64, slots, 128), AXES[:4], 0, 0, tiled=True)]
    reduce_scatter x1 -> x0, waiting for transfers between devices: 4.88 us -> none  [on_device(): model = lax.psum_scatter(model, 'zh', scatter_dimension=0, tiled=False)]
  transfers between devices with their start and end apart: 12 -> 14, of which waited for: 9 -> 6; matrix products, arithmetic and copies ran while one was open for 2% -> 2% of each run, Pallas kernels for 14% -> 16%
where the time goes in v6:
time: 161 us
  waiting for transfers between devices  70.8 us (44%)
  starting transfers between devices  50.5 us (31%)
  Pallas kernels  29.8 us (19%)
  local copies, waits for them, and re-layouts  3.83 us (2%)
  between operations  2.87 us (2%)
  matrix products  1.66 us (1%)
    ppermute x6, waiting for transfers between devices, swap(): return lax.ppermute(value, axes, [(n, n ^ offset) for n in range(4)])  51.5 us
    pallas_call x1, Pallas kernels, channelize(): pl.pallas_call(channel_kernel, grid=(2, 8), in_specs=[pl.BlockSpec((1, 75...  20.4 us
    ppermute x6, waiting for transfers between devices, shift(): return lax.ppermute(value, axis, [(n, (n + offset) % 4) for n in range(4)])  17.9 us
    all_to_all x1, starting transfers between devices, on_device(): lax.all_to_all(model.reshape(64, slots, 128), AXES[:4], 0, 0, tiled=True)  15.1 us
    ppermute x6, starting transfers between devices, swap(): return lax.ppermute(value, axes, [(n, n ^ offset) for n in range(4)])  14.6 us
    ppermute x6, starting transfers between devices, shift(): return lax.ppermute(value, axis, [(n, (n + offset) % 4) for n in range(4)])  11.3 us
    all_to_all x1, starting transfers between devices, on_device(): lax.all_to_all(spectra.reshape(64, 4, 64, 128), TURN, 0, 0, tiled=True)  9.5 us
    pallas_call x4, Pallas kernels, form_beams(): pl.pallas_call(beam_kernel, grid_spec=pltpu.PrefetchScalarGridSpec(num_sc...  7.44 us
  transfers between devices with their start and end apart: 14, of which 6 were waited for; matrix products, arithmetic and copies ran while one was open for 2% of the time, Pallas kernels for 16%

profile of v6, /device:TPU:1, one launch (start us, length us, event | category | flops | bytes accessed | tf_op | source)
XLA Modules:
  0.0 160.5 jit_solution(16946078261351927341)
XLA Ops:
  0.6 0.9 reshape.101
  1.7 1.2 convolution_bitcast_fusion
  2.9 0.8 broadcast_in_dim.27
  3.8 15.1 %all-to-all-start = ((f32[64,16,128]{2,1,0:T(8,128)}), f32[64,16,128]{2,1,0:T(8,128)S(1)}, u32[]{:S(2)}, u32[]{:S(2)}) async-start(f32[64,16,128]{2,1,0:T(8,128)} %bitcast.6), calls=%async_computation | async-start | bytes 1048576 | tf_op jit(solution)/shard_map/all_to_all | solution.py:310
  18.9 1.2 dynamic_slice.10
  22.1 20.4 %channelize.1 = bf16[2,2,4,4,4,2,32,128]{7,6,5,4,3,2,1,0:T(8,128)(2,1)} custom-call(bf16[2,75,128,128]{3,2,1,0:T(8,128)(2,1)} %bitcast.44, f32[12,8192]{1,0:T(8,128)} %taps.1, bf16[256,128]{1,0:T(8,128)(2,1)} %constant.80.clone.one, f32[2,64,128]{2,1,0:T(8,128)} %constant.81.clone.twist, bf16[128,256]{1,0:T(8,128)(2,1)} %constant.82.clone.two), custom_call_target="tpu_custom_call" | custom-call | tf_op jit(solution)/shard_map/channelize/pallas_call | solution.py:133
  42.5 9.5 %all-to-all-start.1 = ((bf16[64,4,64,128]{3,2,1,0:T(8,128)(2,1)}), bf16[64,4,64,128]{3,2,1,0:T(8,128)(2,1)}, u32[]{:S(2)}, u32[]{:S(2)}) async-start(bf16[64,4,64,128]{3,2,1,0:T(8,128)(2,1)} %bitcast.43), calls=%async_computation.1 | async-start | bytes 8388608 | tf_op jit(solution)/shard_map/all_to_all | solution.py:316
  52.0 0.7 gather_fusion
  52.7 1.7 %collective-permute-start = (f32[16,128]{1,0:T(8,128)S(1)}, f32[16,128]{1,0:T(8,128)S(1)}, u32[]{:S(2)}, u32[]{:S(2)}) collective-permute-start(f32[16,128]{1,0:T(8,128)S(1)} %dynamic-slice_bitcast_fusion), channel_id=1, source_target_pairs={{0,3},{1,2},{2,1},{3,0},{4,7},{5,6},{6,5},{7,4},{8,11},{9,10},{10,... | collective-permute-start | bytes 24584 | tf_op jit(solution)/shard_map/ppermute | solution.py:298
  54.6 0.3 collective-permute-start.2
  54.9 0.5 fusion
  55.5 45.1 %collective-permute-done = f32[16,128]{1,0:T(8,128)S(1)} collective-permute-done((f32[16,128]{1,0:T(8,128)S(1)}, f32[16,128]{1,0:T(8,128)S(1)}, u32[]{:S(2)}, u32[]{:S(2)}) %collective-permute-start) | collective-permute-done | bytes 8224 | tf_op jit(solution)/shard_map/ppermute | solution.py:298
  100.9 0.3 multiply_bitcast_fusion.1
  101.3 0.3 multiply_bitcast_fusion
  101.6 1.5 all-to-all-done.1.spectra
  103.1 1.9 %form_beams.6 = (bf16[4,16,16,128]{3,2,1,0:T(8,128)(2,1)S(1)}, bf16[4,16,16,128]{3,2,1,0:T(8,128)(2,1)S(1)}) custom-call(s32[1]{0:T(128)} %bitcast.22.where, bf16[64,4,64,128]{3,2,1,0:T(8,128)(2,1)} %all-to-all-done.1.spectra, f32[2,64,128]{2,1,0:T(8,128)S(1)} %get-tuple-element.42.base, f32[2,64,128]{2,1,0:T(8,128)S(1)} %pad_maximum_fusion.1.step), custom_call_target="tpu_custom_call" | custom-call | tf_op jit(solution)/shard_map/form_beams/pallas_call | solution.py:193
  105.0 2.2 %collective-permute-start.3 = (bf16[4,16,16,128]{3,2,1,0:T(8,128)(2,1)S(1)}, bf16[4,16,16,128]{3,2,1,0:T(8,128)(2,1)S(1)}, u32[]{:S(2)}, u32[]{:S(2)}) collective-permute-start(bf16[4,16,16,128]{3,2,1,0:T(8,128)(2,1)S(1)} %get-tuple-element.21), channel_id=1, source_target_pairs={{0,32},{32,64},{64,96},{96,0},{1,33},{33,65},{65,97},{97,1},{2,34}... | collective-permute-start | bytes 786440 | tf_op jit(solution)/shard_map/ppermute | solution.py:294
  107.2 1.4 collective-permute-start.7
  108.6 1.9 %form_beams.5 = (bf16[4,16,16,128]{3,2,1,0:T(8,128)(2,1)S(1)}, bf16[4,16,16,128]{3,2,1,0:T(8,128)(2,1)S(1)}) custom-call(s32[1]{0:T(128)} %bitcast.19.where, bf16[64,4,64,128]{3,2,1,0:T(8,128)(2,1)} %all-to-all-done.1.spectra, f32[2,64,128]{2,1,0:T(8,128)S(1)} %get-tuple-element.41.base, f32[2,64,128]{2,1,0:T(8,128)S(1)} %pad_maximum_fusion.1.step), custom_call_target="tpu_custom_call" | custom-call | tf_op jit(solution)/shard_map/form_beams/pallas_call | solution.py:193
  110.5 1.3 collective-permute-start.5
  111.8 1.9 %form_beams.7 = (bf16[4,16,16,128]{3,2,1,0:T(8,128)(2,1)S(1)}, bf16[4,16,16,128]{3,2,1,0:T(8,128)(2,1)S(1)}) custom-call(s32[1]{0:T(128)} %bitcast.25.where, bf16[64,4,64,128]{3,2,1,0:T(8,128)(2,1)} %all-to-all-done.1.spectra, f32[2,64,128]{2,1,0:T(8,128)S(1)} %get-tuple-element.43.base, f32[2,64,128]{2,1,0:T(8,128)S(1)} %pad_maximum_fusion.1.step), custom_call_target="tpu_custom_call" | custom-call | tf_op jit(solution)/shard_map/form_beams/pallas_call | solution.py:193
  113.7 2.6 %collective-permute-start.6 = (bf16[4,16,16,128]{3,2,1,0:T(8,128)(2,1)S(1)}, bf16[4,16,16,128]{3,2,1,0:T(8,128)(2,1)S(1)}, u32[]{:S(2)}, u32[]{:S(2)}) collective-permute-start(bf16[4,16,16,128]{3,2,1,0:T(8,128)(2,1)S(1)} %get-tuple-element.23), channel_id=1, source_target_pairs={{0,96},{32,0},{64,32},{96,64},{1,97},{33,1},{65,33},{97,65},{2,98}... | collective-permute-start | bytes 786440 | tf_op jit(solution)/shard_map/ppermute | solution.py:294
  116.4 1.1 collective-permute-start.4
  117.6 2.6 %collective-permute-start.8 = (bf16[4,16,16,128]{3,2,1,0:T(8,128)(2,1)S(1)}, bf16[4,16,16,128]{3,2,1,0:T(8,128)(2,1)S(1)}, u32[]{:S(2)}, u32[]{:S(2)}) collective-permute-start(bf16[4,16,16,128]{3,2,1,0:T(8,128)(2,1)S(1)} %add_pair.3), channel_id=1, source_target_pairs={{0,96},{32,0},{64,32},{96,64},{1,97},{33,1},{65,33},{97,65},{2,98}... | collective-permute-start | bytes 786440 | tf_op jit(solution)/shard_map/ppermute | solution.py:294
  120.2 1.9 %form_beams.4 = (bf16[4,16,16,128]{3,2,1,0:T(8,128)(2,1)S(1)}, bf16[4,16,16,128]{3,2,1,0:T(8,128)(2,1)S(1)}) custom-call(s32[1]{0:T(128)} %bitcast.1.where, bf16[64,4,64,128]{3,2,1,0:T(8,128)(2,1)} %all-to-all-done.1.spectra, f32[2,64,128]{2,1,0:T(8,128)S(1)} %get-tuple-element.40.base, f32[2,64,128]{2,1,0:T(8,128)S(1)} %pad_maximum_fusion.1.step), custom_call_target="tpu_custom_call" | custom-call | tf_op jit(solution)/shard_map/form_beams/pallas_call | solution.py:193
  122.0 12.2 %collective-permute-done.6.refs_4_ = bf16[4,16,16,128]{3,2,1,0:T(8,128)(2,1)S(1)} collective-permute-done((bf16[4,16,16,128]{3,2,1,0:T(8,128)(2,1)S(1)}, bf16[4,16,16,128]{3,2,1,0:T(8,128)(2,1)S(1)}, u32[]{:S(2)}, u32[]{:S(2)}) %collective-permute-start.6) | collective-permute-done | bytes 262176 | tf_op jit(solution)/shard_map/ppermute | solution.py:294
  134.2 5.7 %collective-permute-done.8.refs_5_ = bf16[4,16,16,128]{3,2,1,0:T(8,128)(2,1)S(1)} collective-permute-done((bf16[4,16,16,128]{3,2,1,0:T(8,128)(2,1)S(1)}, bf16[4,16,16,128]{3,2,1,0:T(8,128)(2,1)S(1)}, u32[]{:S(2)}, u32[]{:S(2)}) %collective-permute-start.8) | collective-permute-done | bytes 262176 | tf_op jit(solution)/shard_map/ppermute | solution.py:294
  139.9 1.2 collective-permute-start.9
  141.2 11.0 %collective-permute-start.10 = (bf16[2,16,16,128]{3,2,1,0:T(8,128)(2,1)S(1)}, bf16[2,16,16,128]{3,2,1,0:T(8,128)(2,1)S(1)}, u32[]{:S(2)}, u32[]{:S(2)}) collective-permute-start(bf16[2,16,16,128]{3,2,1,0:T(8,128)(2,1)S(1)} %add_group.6), channel_id=1, source_target_pairs={{0,2},{1,3},{2,0},{3,1},{4,6},{5,7},{6,4},{7,5},{8,10},{9,11},{10,... | collective-permute-start | bytes 393224 | tf_op jit(solution)/shard_map/ppermute | solution.py:298
  152.5 3.6 %collective-permute-done.10.refs_2_ = bf16[2,16,16,128]{3,2,1,0:T(8,128)(2,1)S(1)} collective-permute-done((bf16[2,16,16,128]{3,2,1,0:T(8,128)(2,1)S(1)}, bf16[2,16,16,128]{3,2,1,0:T(8,128)(2,1)S(1)}, u32[]{:S(2)}, u32[]{:S(2)}) %collective-permute-start.10) | collective-permute-done | bytes 131104 | tf_op jit(solution)/shard_map/ppermute | solution.py:298
  156.1 2.8 %collective-permute-done.11.refs_3_ = bf16[2,16,16,128]{3,2,1,0:T(8,128)(2,1)S(1)} collective-permute-done((bf16[2,16,16,128]{3,2,1,0:T(8,128)(2,1)S(1)}, bf16[2,16,16,128]{3,2,1,0:T(8,128)(2,1)S(1)}, u32[]{:S(2)}, u32[]{:S(2)}) %collective-permute-start.11) | collective-permute-done | bytes 131104 | tf_op jit(solution)/shard_map/ppermute | solution.py:298
  158.9 1.6 %merge.1 = (f32[16,64,128]{2,1,0:T(8,128)}, f32[16,64,128]{2,1,0:T(8,128)}) custom-call(s32[1]{0:T(128)} %bitcast.beam_pos, bf16[2,16,16,128]{3,2,1,0:T(8,128)(2,1)S(1)} %add_group.4.refs_0_, bf16[2,16,16,128]{3,2,1,0:T(8,128)(2,1)S(1)} %collective-permute-done.9.refs_1_, bf16[2,16,16,128]{3,2,1,0:T(8,128)(2,1)S(1)} %collective-permute-done.10.refs_2_, ...), custom_call_target="tpu_custom_call" | custom-call | tf_op jit(solution)/shard_map/merge/pallas_call | solution.py:269
  (33 shorter events, 1.4 us)
Async XLA Ops:
  0.6 51.4 %copy-start = (f32[64,512]{1,0:T(8,128)S(1)}, f32[64,512]{1,0:T(8,128)}, u32[]{:S(2)}) copy-start(f32[64,512]{1,0:T(8,128)} %param.13) | copy-start | bytes 393220
  3.8 38.7 %all-to-all-start = ((f32[64,16,128]{2,1,0:T(8,128)}), f32[64,16,128]{2,1,0:T(8,128)S(1)}, u32[]{:S(2)}, u32[]{:S(2)}) async-start(f32[64,16,128]{2,1,0:T(8,128)} %bitcast.6), calls=%async_computation | async-start | bytes 1048576 | tf_op jit(solution)/shard_map/all_to_all | solution.py:310
  42.5 9.5 %copy-start.1 = (s32[64]{0:T(128)S(1)}, s32[64]{0:T(128)}, u32[]{:S(2)}) copy-start(s32[64]{0:T(128)} %param.15) | copy-start | bytes 772
  42.5 60.6 %all-to-all-start.1 = ((bf16[64,4,64,128]{3,2,1,0:T(8,128)(2,1)}), bf16[64,4,64,128]{3,2,1,0:T(8,128)(2,1)}, u32[]{:S(2)}, u32[]{:S(2)}) async-start(bf16[64,4,64,128]{3,2,1,0:T(8,128)(2,1)} %bitcast.43), calls=%async_computation.1 | async-start | bytes 8388608 | tf_op jit(solution)/shard_map/all_to_all | solution.py:316
  52.7 47.8 %collective-permute-start = (f32[16,128]{1,0:T(8,128)S(1)}, f32[16,128]{1,0:T(8,128)S(1)}, u32[]{:S(2)}, u32[]{:S(2)}) collective-permute-start(f32[16,128]{1,0:T(8,128)S(1)} %dynamic-slice_bitcast_fusion), channel_id=1, source_target_pairs={{0,3},{1,2},{2,1},{3,0},{4,7},{5,6},{6,5},{7,4},{8,11},{9,10},{10,... | collective-permute-start | bytes 24584 | tf_op jit(solution)/shard_map/ppermute | solution.py:298
  54.4 46.1 %collective-permute-start.1 = (f32[16,128]{1,0:T(8,128)S(1)}, f32[16,128]{1,0:T(8,128)S(1)}, u32[]{:S(2)}, u32[]{:S(2)}) collective-permute-start(f32[16,128]{1,0:T(8,128)S(1)} %dynamic-slice_bitcast_fusion), channel_id=1, source_target_pairs={{0,2},{1,3},{2,0},{3,1},{4,6},{5,7},{6,4},{7,5},{8,10},{9,11},{10,... | collective-permute-start | bytes 24584 | tf_op jit(solution)/shard_map/ppermute | solution.py:298
  54.6 45.9 %collective-permute-start.2 = (f32[16,128]{1,0:T(8,128)S(1)}, f32[16,128]{1,0:T(8,128)S(1)}, u32[]{:S(2)}, u32[]{:S(2)}) collective-permute-start(f32[16,128]{1,0:T(8,128)S(1)} %dynamic-slice_bitcast_fusion), channel_id=1, source_target_pairs={{0,1},{1,0},{2,3},{3,2},{4,5},{5,4},{6,7},{7,6},{8,9},{9,8},{10,11... | collective-permute-start | bytes 24584 | tf_op jit(solution)/shard_map/ppermute | solution.py:298
  105.0 11.3 %collective-permute-start.3 = (bf16[4,16,16,128]{3,2,1,0:T(8,128)(2,1)S(1)}, bf16[4,16,16,128]{3,2,1,0:T(8,128)(2,1)S(1)}, u32[]{:S(2)}, u32[]{:S(2)}) collective-permute-start(bf16[4,16,16,128]{3,2,1,0:T(8,128)(2,1)S(1)} %get-tuple-element.21), channel_id=1, source_target_pairs={{0,32},{32,64},{64,96},{96,0},{1,33},{33,65},{65,97},{97,1},{2,34}... | collective-permute-start | bytes 786440 | tf_op jit(solution)/shard_map/ppermute | solution.py:294
  107.2 10.3 %collective-permute-start.7 = (bf16[4,16,16,128]{3,2,1,0:T(8,128)(2,1)S(1)}, bf16[4,16,16,128]{3,2,1,0:T(8,128)(2,1)S(1)}, u32[]{:S(2)}, u32[]{:S(2)}) collective-permute-start(bf16[4,16,16,128]{3,2,1,0:T(8,128)(2,1)S(1)} %get-tuple-element.25), channel_id=1, source_target_pairs={{0,96},{32,0},{64,32},{96,64},{1,97},{33,1},{65,33},{97,65},{2,98}... | collective-permute-start | bytes 786440 | tf_op jit(solution)/shard_map/ppermute | solution.py:294
  110.5 11.5 %collective-permute-start.5 = (bf16[4,16,16,128]{3,2,1,0:T(8,128)(2,1)S(1)}, bf16[4,16,16,128]{3,2,1,0:T(8,128)(2,1)S(1)}, u32[]{:S(2)}, u32[]{:S(2)}) collective-permute-start(bf16[4,16,16,128]{3,2,1,0:T(8,128)(2,1)S(1)} %get-tuple-element.22), channel_id=1, source_target_pairs={{0,32},{32,64},{64,96},{96,0},{1,33},{33,65},{65,97},{97,1},{2,34}... | collective-permute-start | bytes 786440 | tf_op jit(solution)/shard_map/ppermute | solution.py:294
  113.7 20.5 %collective-permute-start.6 = (bf16[4,16,16,128]{3,2,1,0:T(8,128)(2,1)S(1)}, bf16[4,16,16,128]{3,2,1,0:T(8,128)(2,1)S(1)}, u32[]{:S(2)}, u32[]{:S(2)}) collective-permute-start(bf16[4,16,16,128]{3,2,1,0:T(8,128)(2,1)S(1)} %get-tuple-element.23), channel_id=1, source_target_pairs={{0,96},{32,0},{64,32},{96,64},{1,97},{33,1},{65,33},{97,65},{2,98}... | collective-permute-start | bytes 786440 | tf_op jit(solution)/shard_map/ppermute | solution.py:294
  116.4 17.9 %collective-permute-start.4 = (bf16[4,16,16,128]{3,2,1,0:T(8,128)(2,1)S(1)}, bf16[4,16,16,128]{3,2,1,0:T(8,128)(2,1)S(1)}, u32[]{:S(2)}, u32[]{:S(2)}) collective-permute-start(bf16[4,16,16,128]{3,2,1,0:T(8,128)(2,1)S(1)} %add_pair.2), channel_id=1, source_target_pairs={{0,32},{32,64},{64,96},{96,0},{1,33},{33,65},{65,97},{97,1},{2,34}... | collective-permute-start | bytes 786440 | tf_op jit(solution)/shard_map/ppermute | solution.py:294
  117.6 22.3 %collective-permute-start.8 = (bf16[4,16,16,128]{3,2,1,0:T(8,128)(2,1)S(1)}, bf16[4,16,16,128]{3,2,1,0:T(8,128)(2,1)S(1)}, u32[]{:S(2)}, u32[]{:S(2)}) collective-permute-start(bf16[4,16,16,128]{3,2,1,0:T(8,128)(2,1)S(1)} %add_pair.3), channel_id=1, source_target_pairs={{0,96},{32,0},{64,32},{96,64},{1,97},{33,1},{65,33},{97,65},{2,98}... | collective-permute-start | bytes 786440 | tf_op jit(solution)/shard_map/ppermute | solution.py:294
  139.9 12.5 %collective-permute-start.9 = (bf16[2,16,16,128]{3,2,1,0:T(8,128)(2,1)S(1)}, bf16[2,16,16,128]{3,2,1,0:T(8,128)(2,1)S(1)}, u32[]{:S(2)}, u32[]{:S(2)}) collective-permute-start(bf16[2,16,16,128]{3,2,1,0:T(8,128)(2,1)S(1)} %add_group.5), channel_id=1, source_target_pairs={{0,1},{1,0},{2,3},{3,2},{4,5},{5,4},{6,7},{7,6},{8,9},{9,8},{10,11... | collective-permute-start | bytes 393224 | tf_op jit(solution)/shard_map/ppermute | solution.py:298
  141.2 14.9 %collective-permute-start.10 = (bf16[2,16,16,128]{3,2,1,0:T(8,128)(2,1)S(1)}, bf16[2,16,16,128]{3,2,1,0:T(8,128)(2,1)S(1)}, u32[]{:S(2)}, u32[]{:S(2)}) collective-permute-start(bf16[2,16,16,128]{3,2,1,0:T(8,128)(2,1)S(1)} %add_group.6), channel_id=1, source_target_pairs={{0,2},{1,3},{2,0},{3,1},{4,6},{5,7},{6,4},{7,5},{8,10},{9,11},{10,... | collective-permute-start | bytes 393224 | tf_op jit(solution)/shard_map/ppermute | solution.py:298
  152.3 6.6 %collective-permute-start.11 = (bf16[2,16,16,128]{3,2,1,0:T(8,128)(2,1)S(1)}, bf16[2,16,16,128]{3,2,1,0:T(8,128)(2,1)S(1)}, u32[]{:S(2)}, u32[]{:S(2)}) collective-permute-start(bf16[2,16,16,128]{3,2,1,0:T(8,128)(2,1)S(1)} %add_group.7), channel_id=1, source_target_pairs={{0,3},{1,2},{2,1},{3,0},{4,7},{5,6},{6,5},{7,4},{8,11},{9,10},{10,... | collective-permute-start | bytes 393224 | tf_op jit(solution)/shard_map/ppermute | solution.py:298

commit v7 on v6

--- a/solution.py
+++ b/solution.py
@@ -112,7 +112,7 @@
 
     @pl.when(block == 7)
     def _():
-        lax.fori_loop(0, FRAMES // 2, first_section, 0, unroll=16)
+        lax.fori_loop(0, FRAMES // 2, first_section, 0, unroll=32)
         lax.fori_loop(0, 4, second_section, 0, unroll=4)
 
 
@@ -281,6 +281,21 @@
     )(beam_pos, *[on_chip(part) for part in parts])
 
 
+def keep_kernel(beam_pos, owners, models, out):
+    out[...] = models[owners[beam_pos[0]]]
+
+
+def keep_owner(beam_pos, owners, models):
+    return pl.pallas_call(
+        keep_kernel,
+        in_specs=[SCALAR, SCALAR, CHIP],
+        out_specs=CHIP,
+        out_shape=pltpu.VMEM(models.shape[1:], F32),
+        compiler_params=pltpu.CompilerParams(vmem_limit_bytes=SMALL_LIMIT),
+        name="keep_owner",
+    )(beam_pos, owners, on_chip(models))
+
+
 def station_pick(station_map):
     phys = station_map.reshape(2, 4, 32, 2).transpose(1, 3, 0, 2).reshape(STATIONS)
     return (jnp.arange(STATIONS, dtype=jnp.int32)[:, None] == phys[None, :]).astype(F32)
@@ -310,7 +325,8 @@
     models = lax.all_to_all(model.reshape(64, slots, 128), AXES[:4], 0, 0, tiled=True)
     spectra = channelize(volts, fir_taps)
     models, spectra = lax.optimization_barrier((models, spectra))
-    delay = lax.dynamic_index_in_dim(models, owners[beam_pos], 0, keepdims=False)
+    pos = beam_pos.astype(jnp.int32)[None]
+    delay = keep_owner(pos, owners, models)
     delay, spectra = lax.optimization_barrier((delay, spectra))
     models = [delay] + [swap(delay, ("yl", "c"), n) for n in range(1, 4)]
     turned = lax.all_to_all(spectra.reshape(64, 4, 64, 128), TURN, 0, 0, tiled=True)
@@ -341,7 +357,6 @@
     up_re = shift(add_pair(up_re, far_re), "zh", 1)
     down_im = shift(add_pair(down_im, far_im), "zh", 3)
     parts = [own, (up_re, up_im), (down_re, down_im)]
-    pos = beam_pos.astype(jnp.int32)[None]
     quarters = {}
     for n in (2, 3, 1, 0):
         quarter = add_group(n, pos, parts)

time: 161 us -> 158 us (0.981)
  between operations: 2.87 us -> 0.93 us
  transfers between devices with their start and end apart: 14 -> 14, of which waited for: 6 -> 6; matrix products, arithmetic and copies ran while one was open for 2% -> 1% of each run, Pallas kernels for 16% -> 16%
where the time goes in v7:
time: 158 us
  waiting for transfers between devices  70.8 us (45%)
  starting transfers between devices  50.5 us (32%)
  Pallas kernels  30 us (19%)
  local copies, waits for them, and re-layouts  2.6 us (2%)
  matrix products  1.67 us (1%)
    ppermute x6, waiting for transfers between devices, swap(): return lax.ppermute(value, axes, [(n, n ^ offset) for n in range(4)])  51.5 us
    pallas_call x1, Pallas kernels, channelize(): pl.pallas_call(channel_kernel, grid=(2, 8), in_specs=[pl.BlockSpec((1, 75...  20 us
    ppermute x6, waiting for transfers between devices, shift(): return lax.ppermute(value, axis, [(n, (n + offset) % 4) for n in range(4)])  17.9 us
    all_to_all x1, starting transfers between devices, on_device(): lax.all_to_all(model.reshape(64, slots, 128), AXES[:4], 0, 0, tiled=True)  15.1 us
    ppermute x6, starting transfers between devices, swap(): return lax.ppermute(value, axes, [(n, n ^ offset) for n in range(4)])  14.6 us
    ppermute x6, starting transfers between devices, shift(): return lax.ppermute(value, axis, [(n, (n + offset) % 4) for n in range(4)])  11.3 us
    all_to_all x1, starting transfers between devices, on_device(): lax.all_to_all(spectra.reshape(64, 4, 64, 128), TURN, 0, 0, tiled=True)  9.51 us
    pallas_call x4, Pallas kernels, form_beams(): pl.pallas_call(beam_kernel, grid_spec=pltpu.PrefetchScalarGridSpec(num_sc...  7.45 us
  transfers between devices with their start and end apart: 14, of which 6 were waited for; matrix products, arithmetic and copies ran while one was open for 1% of the time, Pallas kernels for 16%

profile of v7, /device:TPU:1, one launch (start us, length us, event | category | flops | bytes accessed | tf_op | source)
XLA Modules:
  0.0 157.5 jit_solution(10230257623115283232)
XLA Ops:
  0.6 0.9 reshape.101
  1.7 1.2 convolution_bitcast_fusion
  2.9 0.8 broadcast_in_dim.27
  3.8 15.1 %all-to-all-start = ((f32[64,16,128]{2,1,0:T(8,128)}), f32[64,16,128]{2,1,0:T(8,128)S(1)}, u32[]{:S(2)}, u32[]{:S(2)}) async-start(f32[64,16,128]{2,1,0:T(8,128)} %bitcast.6), calls=%async_computation | async-start | bytes 1048576 | tf_op jit(solution)/shard_map/all_to_all | solution.py:325
  18.9 20.0 %channelize.1 = bf16[2,2,4,4,4,2,32,128]{7,6,5,4,3,2,1,0:T(8,128)(2,1)} custom-call(bf16[2,75,128,128]{3,2,1,0:T(8,128)(2,1)} %bitcast.41, f32[12,8192]{1,0:T(8,128)} %taps.1, bf16[256,128]{1,0:T(8,128)(2,1)} %constant.76.clone.one, f32[2,64,128]{2,1,0:T(8,128)} %constant.77.clone.twist, bf16[128,256]{1,0:T(8,128)(2,1)} %constant.78.clone.two), custom_call_target="tpu_custom_call" | custom-call | tf_op jit(solution)/shard_map/channelize/pallas_call | solution.py:133
  38.9 0.5 keep_owner.1
  39.5 9.5 %all-to-all-start.1 = ((bf16[64,4,64,128]{3,2,1,0:T(8,128)(2,1)}), bf16[64,4,64,128]{3,2,1,0:T(8,128)(2,1)}, u32[]{:S(2)}, u32[]{:S(2)}) async-start(bf16[64,4,64,128]{3,2,1,0:T(8,128)(2,1)} %bitcast.40), calls=%async_computation.1 | async-start | bytes 8388608 | tf_op jit(solution)/shard_map/all_to_all | solution.py:332
  49.0 0.7 gather_fusion
  49.7 1.7 %collective-permute-start = (f32[16,128]{1,0:T(8,128)S(1)}, f32[16,128]{1,0:T(8,128)S(1)}, u32[]{:S(2)}, u32[]{:S(2)}) collective-permute-start(f32[16,128]{1,0:T(8,128)S(1)} %keep_owner.1), channel_id=1, source_target_pairs={{0,3},{1,2},{2,1},{3,0},{4,7},{5,6},{6,5},{7,4},{8,11},{9,10},{10,... | collective-permute-start | bytes 24584 | tf_op jit(solution)/shard_map/ppermute | solution.py:313
  51.7 0.3 collective-permute-start.2
  51.9 0.5 fusion
  52.5 45.0 %collective-permute-done = f32[16,128]{1,0:T(8,128)S(1)} collective-permute-done((f32[16,128]{1,0:T(8,128)S(1)}, f32[16,128]{1,0:T(8,128)S(1)}, u32[]{:S(2)}, u32[]{:S(2)}) %collective-permute-start) | collective-permute-done | bytes 8224 | tf_op jit(solution)/shard_map/ppermute | solution.py:313
  97.9 0.3 multiply_bitcast_fusion.1
  98.3 0.3 multiply_bitcast_fusion
  98.6 1.5 all-to-all-done.1.spectra
  100.1 1.9 %form_beams.6 = (bf16[4,16,16,128]{3,2,1,0:T(8,128)(2,1)S(1)}, bf16[4,16,16,128]{3,2,1,0:T(8,128)(2,1)S(1)}) custom-call(s32[1]{0:T(128)} %bitcast.20.where, bf16[64,4,64,128]{3,2,1,0:T(8,128)(2,1)} %all-to-all-done.1.spectra, f32[2,64,128]{2,1,0:T(8,128)S(1)} %get-tuple-element.42.base, f32[2,64,128]{2,1,0:T(8,128)S(1)} %pad_maximum_fusion.1.step), custom_call_target="tpu_custom_call" | custom-call | tf_op jit(solution)/shard_map/form_beams/pallas_call | solution.py:193
  102.0 2.2 %collective-permute-start.3 = (bf16[4,16,16,128]{3,2,1,0:T(8,128)(2,1)S(1)}, bf16[4,16,16,128]{3,2,1,0:T(8,128)(2,1)S(1)}, u32[]{:S(2)}, u32[]{:S(2)}) collective-permute-start(bf16[4,16,16,128]{3,2,1,0:T(8,128)(2,1)S(1)} %get-tuple-element.21), channel_id=1, source_target_pairs={{0,32},{32,64},{64,96},{96,0},{1,33},{33,65},{65,97},{97,1},{2,34}... | collective-permute-start | bytes 786440 | tf_op jit(solution)/shard_map/ppermute | solution.py:309
  104.2 1.4 collective-permute-start.7
  105.6 1.9 %form_beams.5 = (bf16[4,16,16,128]{3,2,1,0:T(8,128)(2,1)S(1)}, bf16[4,16,16,128]{3,2,1,0:T(8,128)(2,1)S(1)}) custom-call(s32[1]{0:T(128)} %bitcast.17.where, bf16[64,4,64,128]{3,2,1,0:T(8,128)(2,1)} %all-to-all-done.1.spectra, f32[2,64,128]{2,1,0:T(8,128)S(1)} %get-tuple-element.41.base, f32[2,64,128]{2,1,0:T(8,128)S(1)} %pad_maximum_fusion.1.step), custom_call_target="tpu_custom_call" | custom-call | tf_op jit(solution)/shard_map/form_beams/pallas_call | solution.py:193
  107.5 1.3 collective-permute-start.5
  108.8 1.9 %form_beams.7 = (bf16[4,16,16,128]{3,2,1,0:T(8,128)(2,1)S(1)}, bf16[4,16,16,128]{3,2,1,0:T(8,128)(2,1)S(1)}) custom-call(s32[1]{0:T(128)} %bitcast.23.where, bf16[64,4,64,128]{3,2,1,0:T(8,128)(2,1)} %all-to-all-done.1.spectra, f32[2,64,128]{2,1,0:T(8,128)S(1)} %get-tuple-element.43.base, f32[2,64,128]{2,1,0:T(8,128)S(1)} %pad_maximum_fusion.1.step), custom_call_target="tpu_custom_call" | custom-call | tf_op jit(solution)/shard_map/form_beams/pallas_call | solution.py:193
  110.7 2.6 %collective-permute-start.6 = (bf16[4,16,16,128]{3,2,1,0:T(8,128)(2,1)S(1)}, bf16[4,16,16,128]{3,2,1,0:T(8,128)(2,1)S(1)}, u32[]{:S(2)}, u32[]{:S(2)}) collective-permute-start(bf16[4,16,16,128]{3,2,1,0:T(8,128)(2,1)S(1)} %get-tuple-element.23), channel_id=1, source_target_pairs={{0,96},{32,0},{64,32},{96,64},{1,97},{33,1},{65,33},{97,65},{2,98}... | collective-permute-start | bytes 786440 | tf_op jit(solution)/shard_map/ppermute | solution.py:309
  113.4 1.1 collective-permute-start.4
  114.6 2.6 %collective-permute-start.8 = (bf16[4,16,16,128]{3,2,1,0:T(8,128)(2,1)S(1)}, bf16[4,16,16,128]{3,2,1,0:T(8,128)(2,1)S(1)}, u32[]{:S(2)}, u32[]{:S(2)}) collective-permute-start(bf16[4,16,16,128]{3,2,1,0:T(8,128)(2,1)S(1)} %add_pair.3), channel_id=1, source_target_pairs={{0,96},{32,0},{64,32},{96,64},{1,97},{33,1},{65,33},{97,65},{2,98}... | collective-permute-start | bytes 786440 | tf_op jit(solution)/shard_map/ppermute | solution.py:309
  117.2 1.9 %form_beams.4 = (bf16[4,16,16,128]{3,2,1,0:T(8,128)(2,1)S(1)}, bf16[4,16,16,128]{3,2,1,0:T(8,128)(2,1)S(1)}) custom-call(s32[1]{0:T(128)} %bitcast.1.where, bf16[64,4,64,128]{3,2,1,0:T(8,128)(2,1)} %all-to-all-done.1.spectra, f32[2,64,128]{2,1,0:T(8,128)S(1)} %get-tuple-element.40.base, f32[2,64,128]{2,1,0:T(8,128)S(1)} %pad_maximum_fusion.1.step), custom_call_target="tpu_custom_call" | custom-call | tf_op jit(solution)/shard_map/form_beams/pallas_call | solution.py:193
  119.0 12.2 %collective-permute-done.6.refs_4_ = bf16[4,16,16,128]{3,2,1,0:T(8,128)(2,1)S(1)} collective-permute-done((bf16[4,16,16,128]{3,2,1,0:T(8,128)(2,1)S(1)}, bf16[4,16,16,128]{3,2,1,0:T(8,128)(2,1)S(1)}, u32[]{:S(2)}, u32[]{:S(2)}) %collective-permute-start.6) | collective-permute-done | bytes 262176 | tf_op jit(solution)/shard_map/ppermute | solution.py:309
  131.2 5.7 %collective-permute-done.8.refs_5_ = bf16[4,16,16,128]{3,2,1,0:T(8,128)(2,1)S(1)} collective-permute-done((bf16[4,16,16,128]{3,2,1,0:T(8,128)(2,1)S(1)}, bf16[4,16,16,128]{3,2,1,0:T(8,128)(2,1)S(1)}, u32[]{:S(2)}, u32[]{:S(2)}) %collective-permute-start.8) | collective-permute-done | bytes 262176 | tf_op jit(solution)/shard_map/ppermute | solution.py:309
  136.9 1.2 collective-permute-start.9
  138.2 11.0 %collective-permute-start.10 = (bf16[2,16,16,128]{3,2,1,0:T(8,128)(2,1)S(1)}, bf16[2,16,16,128]{3,2,1,0:T(8,128)(2,1)S(1)}, u32[]{:S(2)}, u32[]{:S(2)}) collective-permute-start(bf16[2,16,16,128]{3,2,1,0:T(8,128)(2,1)S(1)} %add_group.6), channel_id=1, source_target_pairs={{0,2},{1,3},{2,0},{3,1},{4,6},{5,7},{6,4},{7,5},{8,10},{9,11},{10,... | collective-permute-start | bytes 393224 | tf_op jit(solution)/shard_map/ppermute | solution.py:313
  149.5 3.6 %collective-permute-done.10.refs_2_ = bf16[2,16,16,128]{3,2,1,0:T(8,128)(2,1)S(1)} collective-permute-done((bf16[2,16,16,128]{3,2,1,0:T(8,128)(2,1)S(1)}, bf16[2,16,16,128]{3,2,1,0:T(8,128)(2,1)S(1)}, u32[]{:S(2)}, u32[]{:S(2)}) %collective-permute-start.10) | collective-permute-done | bytes 131104 | tf_op jit(solution)/shard_map/ppermute | solution.py:313
  153.1 2.8 %collective-permute-done.11.refs_3_ = bf16[2,16,16,128]{3,2,1,0:T(8,128)(2,1)S(1)} collective-permute-done((bf16[2,16,16,128]{3,2,1,0:T(8,128)(2,1)S(1)}, bf16[2,16,16,128]{3,2,1,0:T(8,128)(2,1)S(1)}, u32[]{:S(2)}, u32[]{:S(2)}) %collective-permute-start.11) | collective-permute-done | bytes 131104 | tf_op jit(solution)/shard_map/ppermute | solution.py:313
  155.9 1.6 %merge.1 = (f32[16,64,128]{2,1,0:T(8,128)}, f32[16,64,128]{2,1,0:T(8,128)}) custom-call(s32[1]{0:T(128)} %bitcast.beam_pos, bf16[2,16,16,128]{3,2,1,0:T(8,128)(2,1)S(1)} %add_group.4.refs_0_, bf16[2,16,16,128]{3,2,1,0:T(8,128)(2,1)S(1)} %collective-permute-done.9.refs_1_, bf16[2,16,16,128]{3,2,1,0:T(8,128)(2,1)S(1)} %collective-permute-done.10.refs_2_, ...), custom_call_target="tpu_custom_call" | custom-call | tf_op jit(solution)/shard_map/merge/pallas_call | solution.py:269
  (34 shorter events, 1.4 us)
Async XLA Ops:
  0.6 48.4 %copy-start = (f32[64,512]{1,0:T(8,128)S(1)}, f32[64,512]{1,0:T(8,128)}, u32[]{:S(2)}) copy-start(f32[64,512]{1,0:T(8,128)} %param.13) | copy-start | bytes 393220
  3.8 35.1 %all-to-all-start = ((f32[64,16,128]{2,1,0:T(8,128)}), f32[64,16,128]{2,1,0:T(8,128)S(1)}, u32[]{:S(2)}, u32[]{:S(2)}) async-start(f32[64,16,128]{2,1,0:T(8,128)} %bitcast.6), calls=%async_computation | async-start | bytes 1048576 | tf_op jit(solution)/shard_map/all_to_all | solution.py:325
  18.9 20.0 %copy-start.1 = (s32[4]{0:T(128)S(1)}, s32[4]{0:T(128)}, u32[]{:S(2)}) copy-start(s32[4]{0:T(128)} %owners.1) | copy-start | bytes 52
  39.5 9.5 %copy-start.2 = (s32[64]{0:T(128)S(1)}, s32[64]{0:T(128)}, u32[]{:S(2)}) copy-start(s32[64]{0:T(128)} %param.15) | copy-start | bytes 772
  39.5 60.6 %all-to-all-start.1 = ((bf16[64,4,64,128]{3,2,1,0:T(8,128)(2,1)}), bf16[64,4,64,128]{3,2,1,0:T(8,128)(2,1)}, u32[]{:S(2)}, u32[]{:S(2)}) async-start(bf16[64,4,64,128]{3,2,1,0:T(8,128)(2,1)} %bitcast.40), calls=%async_computation.1 | async-start | bytes 8388608 | tf_op jit(solution)/shard_map/all_to_all | solution.py:332
  49.7 47.8 %collective-permute-start = (f32[16,128]{1,0:T(8,128)S(1)}, f32[16,128]{1,0:T(8,128)S(1)}, u32[]{:S(2)}, u32[]{:S(2)}) collective-permute-start(f32[16,128]{1,0:T(8,128)S(1)} %keep_owner.1), channel_id=1, source_target_pairs={{0,3},{1,2},{2,1},{3,0},{4,7},{5,6},{6,5},{7,4},{8,11},{9,10},{10,... | collective-permute-start | bytes 24584 | tf_op jit(solution)/shard_map/ppermute | solution.py:313
  51.4 46.1 %collective-permute-start.1 = (f32[16,128]{1,0:T(8,128)S(1)}, f32[16,128]{1,0:T(8,128)S(1)}, u32[]{:S(2)}, u32[]{:S(2)}) collective-permute-start(f32[16,128]{1,0:T(8,128)S(1)} %keep_owner.1), channel_id=1, source_target_pairs={{0,2},{1,3},{2,0},{3,1},{4,6},{5,7},{6,4},{7,5},{8,10},{9,11},{10,... | collective-permute-start | bytes 24584 | tf_op jit(solution)/shard_map/ppermute | solution.py:313
  51.7 45.9 %collective-permute-start.2 = (f32[16,128]{1,0:T(8,128)S(1)}, f32[16,128]{1,0:T(8,128)S(1)}, u32[]{:S(2)}, u32[]{:S(2)}) collective-permute-start(f32[16,128]{1,0:T(8,128)S(1)} %keep_owner.1), channel_id=1, source_target_pairs={{0,1},{1,0},{2,3},{3,2},{4,5},{5,4},{6,7},{7,6},{8,9},{9,8},{10,11... | collective-permute-start | bytes 24584 | tf_op jit(solution)/shard_map/ppermute | solution.py:313
  102.0 11.3 %collective-permute-start.3 = (bf16[4,16,16,128]{3,2,1,0:T(8,128)(2,1)S(1)}, bf16[4,16,16,128]{3,2,1,0:T(8,128)(2,1)S(1)}, u32[]{:S(2)}, u32[]{:S(2)}) collective-permute-start(bf16[4,16,16,128]{3,2,1,0:T(8,128)(2,1)S(1)} %get-tuple-element.21), channel_id=1, source_target_pairs={{0,32},{32,64},{64,96},{96,0},{1,33},{33,65},{65,97},{97,1},{2,34}... | collective-permute-start | bytes 786440 | tf_op jit(solution)/shard_map/ppermute | solution.py:309
  104.2 10.3 %collective-permute-start.7 = (bf16[4,16,16,128]{3,2,1,0:T(8,128)(2,1)S(1)}, bf16[4,16,16,128]{3,2,1,0:T(8,128)(2,1)S(1)}, u32[]{:S(2)}, u32[]{:S(2)}) collective-permute-start(bf16[4,16,16,128]{3,2,1,0:T(8,128)(2,1)S(1)} %get-tuple-element.25), channel_id=1, source_target_pairs={{0,96},{32,0},{64,32},{96,64},{1,97},{33,1},{65,33},{97,65},{2,98}... | collective-permute-start | bytes 786440 | tf_op jit(solution)/shard_map/ppermute | solution.py:309
  107.5 11.5 %collective-permute-start.5 = (bf16[4,16,16,128]{3,2,1,0:T(8,128)(2,1)S(1)}, bf16[4,16,16,128]{3,2,1,0:T(8,128)(2,1)S(1)}, u32[]{:S(2)}, u32[]{:S(2)}) collective-permute-start(bf16[4,16,16,128]{3,2,1,0:T(8,128)(2,1)S(1)} %get-tuple-element.22), channel_id=1, source_target_pairs={{0,32},{32,64},{64,96},{96,0},{1,33},{33,65},{65,97},{97,1},{2,34}... | collective-permute-start | bytes 786440 | tf_op jit(solution)/shard_map/ppermute | solution.py:309
  110.7 20.5 %collective-permute-start.6 = (bf16[4,16,16,128]{3,2,1,0:T(8,128)(2,1)S(1)}, bf16[4,16,16,128]{3,2,1,0:T(8,128)(2,1)S(1)}, u32[]{:S(2)}, u32[]{:S(2)}) collective-permute-start(bf16[4,16,16,128]{3,2,1,0:T(8,128)(2,1)S(1)} %get-tuple-element.23), channel_id=1, source_target_pairs={{0,96},{32,0},{64,32},{96,64},{1,97},{33,1},{65,33},{97,65},{2,98}... | collective-permute-start | bytes 786440 | tf_op jit(solution)/shard_map/ppermute | solution.py:309
  113.4 17.8 %collective-permute-start.4 = (bf16[4,16,16,128]{3,2,1,0:T(8,128)(2,1)S(1)}, bf16[4,16,16,128]{3,2,1,0:T(8,128)(2,1)S(1)}, u32[]{:S(2)}, u32[]{:S(2)}) collective-permute-start(bf16[4,16,16,128]{3,2,1,0:T(8,128)(2,1)S(1)} %add_pair.2), channel_id=1, source_target_pairs={{0,32},{32,64},{64,96},{96,0},{1,33},{33,65},{65,97},{97,1},{2,34}... | collective-permute-start | bytes 786440 | tf_op jit(solution)/shard_map/ppermute | solution.py:309
  114.6 22.3 %collective-permute-start.8 = (bf16[4,16,16,128]{3,2,1,0:T(8,128)(2,1)S(1)}, bf16[4,16,16,128]{3,2,1,0:T(8,128)(2,1)S(1)}, u32[]{:S(2)}, u32[]{:S(2)}) collective-permute-start(bf16[4,16,16,128]{3,2,1,0:T(8,128)(2,1)S(1)} %add_pair.3), channel_id=1, source_target_pairs={{0,96},{32,0},{64,32},{96,64},{1,97},{33,1},{65,33},{97,65},{2,98}... | collective-permute-start | bytes 786440 | tf_op jit(solution)/shard_map/ppermute | solution.py:309
  136.9 12.5 %collective-permute-start.9 = (bf16[2,16,16,128]{3,2,1,0:T(8,128)(2,1)S(1)}, bf16[2,16,16,128]{3,2,1,0:T(8,128)(2,1)S(1)}, u32[]{:S(2)}, u32[]{:S(2)}) collective-permute-start(bf16[2,16,16,128]{3,2,1,0:T(8,128)(2,1)S(1)} %add_group.5), channel_id=1, source_target_pairs={{0,1},{1,0},{2,3},{3,2},{4,5},{5,4},{6,7},{7,6},{8,9},{9,8},{10,11... | collective-permute-start | bytes 393224 | tf_op jit(solution)/shard_map/ppermute | solution.py:313
  138.2 14.9 %collective-permute-start.10 = (bf16[2,16,16,128]{3,2,1,0:T(8,128)(2,1)S(1)}, bf16[2,16,16,128]{3,2,1,0:T(8,128)(2,1)S(1)}, u32[]{:S(2)}, u32[]{:S(2)}) collective-permute-start(bf16[2,16,16,128]{3,2,1,0:T(8,128)(2,1)S(1)} %add_group.6), channel_id=1, source_target_pairs={{0,2},{1,3},{2,0},{3,1},{4,6},{5,7},{6,4},{7,5},{8,10},{9,11},{10,... | collective-permute-start | bytes 393224 | tf_op jit(solution)/shard_map/ppermute | solution.py:313
  149.3 6.6 %collective-permute-start.11 = (bf16[2,16,16,128]{3,2,1,0:T(8,128)(2,1)S(1)}, bf16[2,16,16,128]{3,2,1,0:T(8,128)(2,1)S(1)}, u32[]{:S(2)}, u32[]{:S(2)}) collective-permute-start(bf16[2,16,16,128]{3,2,1,0:T(8,128)(2,1)S(1)} %add_group.7), channel_id=1, source_target_pairs={{0,3},{1,2},{2,1},{3,0},{4,7},{5,6},{6,5},{7,4},{8,11},{9,10},{10,... | collective-permute-start | bytes 393224 | tf_op jit(solution)/shard_map/ppermute | solution.py:313

commit v8 on v7

--- a/solution.py
+++ b/solution.py
@@ -227,55 +227,49 @@
 
 def add_kernel(offset, beam_pos, *refs):
     group = beam_pos[0] ^ offset
-    parts, out = refs[:-1], refs[-1]
-    for ri in range(2):
-        total = parts[ri][group].astype(F32)
-        for part in parts[2 + ri :: 2]:
-            total = total + part[group].astype(F32)
-        out[ri] = total.astype(BF16)
+    total = refs[0][group].astype(F32)
+    for part in refs[1:-1]:
+        total = total + part[group].astype(F32)
+    refs[-1][...] = total.astype(BF16)
 
 
 def add_group(offset, beam_pos, parts):
-    flat = [on_chip(value) for pair in parts for value in pair]
     return pl.pallas_call(
         functools.partial(add_kernel, offset),
-        in_specs=[SCALAR] + [CHIP] * len(flat),
+        in_specs=[SCALAR] + [CHIP] * len(parts),
         out_specs=CHIP,
-        out_shape=pltpu.VMEM((2, 16, 16, 128), BF16),
+        out_shape=pltpu.VMEM((16, 16, 128), BF16),
         compiler_params=pltpu.CompilerParams(vmem_limit_bytes=SMALL_LIMIT),
         name="add_group",
-    )(beam_pos, *flat)
+    )(beam_pos, *[on_chip(part) for part in parts])
 
 
 def merge_kernel(beam_pos, *refs):
     del beam_pos
-    parts, outs, stage = refs[:4], refs[4:6], refs[6]
+    parts, out, stage = refs[:4], refs[4], refs[5]
     scale = 1.0 / math.sqrt(P_SIZE * Q * STATIONS)
     for n, part in enumerate(parts):
 
         @pl.when(pl.program_id(0) == n)
         def _(part=part):
-            for ri in range(2):
-                for i in range(16):
-                    stage[ri, pl.ds(i, 16, stride=BEAM_ROWS), :] = part[ri, i].astype(F32) * scale
-                for beam in range(16):
-                    row = beam * BEAM_ROWS
-                    outs[ri][beam] = stage[ri, row : row + 16, :]
+            for i in range(16):
+                stage[pl.ds(i, 16, stride=BEAM_ROWS), :] = part[i].astype(F32) * scale
+            for beam in range(16):
+                row = beam * BEAM_ROWS
+                out[beam] = stage[row : row + 16, :]
 
 
 def merge(beam_pos, parts):
-    spec = pl.BlockSpec((16, 16, 128), lambda n, pos: (0, pos[0] ^ n, 0))
-    shape = jax.ShapeDtypeStruct((16, 64, 128), F32)
     return pl.pallas_call(
         merge_kernel,
         grid_spec=pltpu.PrefetchScalarGridSpec(
             num_scalar_prefetch=1,
             grid=(4,),
             in_specs=[CHIP] * 4,
-            out_specs=[spec, spec],
-            scratch_shapes=[pltpu.VMEM((2, 16 * BEAM_ROWS, 128), F32)],
+            out_specs=pl.BlockSpec((16, 16, 128), lambda n, pos: (0, pos[0] ^ n, 0)),
+            scratch_shapes=[pltpu.VMEM((16 * BEAM_ROWS, 128), F32)],
         ),
-        out_shape=[shape, shape],
+        out_shape=jax.ShapeDtypeStruct((16, 64, 128), F32),
         compiler_params=pltpu.CompilerParams(vmem_limit_bytes=SMALL_LIMIT),
         name="merge",
     )(beam_pos, *[on_chip(part) for part in parts])
@@ -356,13 +350,14 @@
     own = beams_for(0)
     up_re = shift(add_pair(up_re, far_re), "zh", 1)
     down_im = shift(add_pair(down_im, far_im), "zh", 3)
-    parts = [own, (up_re, up_im), (down_re, down_im)]
-    quarters = {}
-    for n in (2, 3, 1, 0):
-        quarter = add_group(n, pos, parts)
-        quarters[n] = swap(quarter, ("yl", "c"), n) if n else quarter
-    out_re, out_im = merge(pos, [quarters[n] for n in range(4)])
-    return (out_re, out_im)
+    outs = []
+    for parts in ((own[0], up_re, down_re), (own[1], up_im, down_im)):
+        quarters = {}
+        for n in (2, 3, 1, 0):
+            quarter = add_group(n, pos, parts)
+            quarters[n] = swap(quarter, ("yl", "c"), n) if n else quarter
+        outs.append([quarters[n] for n in range(4)])
+    return tuple(merge(pos, quarters) for quarters in outs)
 
 
 def solution(mesh):

time: 158 us -> 154 us (0.975)
  waiting for transfers between devices: 70.8 us -> 56 us
  starting transfers between devices: 50.5 us -> 59.7 us
    ppermute x6, waiting for transfers between devices: 17.9 us -> 7.04 us  [shift(): return lax.ppermute(value, axis, [(n, (n + offset) % 4) for n in range(4)])]
    ppermute x6 -> x9, starting transfers between devices: 14.6 us -> 25.1 us  [swap(): return lax.ppermute(value, axes, [(n, n ^ offset) for n in range(4)])]
    ppermute x6 -> x9, waiting for transfers between devices: 51.5 us -> 47.5 us  [swap(): return lax.ppermute(value, axes, [(n, n ^ offset) for n in range(4)])]
  transfers between devices with their start and end apart: 14 -> 17, of which waited for: 6 -> 6; matrix products, arithmetic and copies ran while one was open for 1% -> 1% of each run, Pallas kernels for 16% -> 18%
where the time goes in v8:
time: 154 us; the launch traced here: 153 us
  starting transfers between devices  59.7 us (39%)
  waiting for transfers between devices  56 us (36%)
  Pallas kernels  31.3 us (20%)
  local copies, waits for them, and re-layouts  2.6 us (2%)
  matrix products  1.67 us (1%)
    ppermute x9, waiting for transfers between devices, swap(): return lax.ppermute(value, axes, [(n, n ^ offset) for n in range(4)])  47.5 us
    ppermute x9, starting transfers between devices, swap(): return lax.ppermute(value, axes, [(n, n ^ offset) for n in range(4)])  25.1 us
    pallas_call x1, Pallas kernels, channelize(): pl.pallas_call(channel_kernel, grid=(2, 8), in_specs=[pl.BlockSpec((1, 75...  20 us
    all_to_all x1, starting transfers between devices, on_device(): lax.all_to_all(model.reshape(64, slots, 128), AXES[:4], 0, 0, tiled=True)  15.1 us
    ppermute x6, starting transfers between devices, shift(): return lax.ppermute(value, axis, [(n, (n + offset) % 4) for n in range(4)])  10 us
    all_to_all x1, starting transfers between devices, on_device(): lax.all_to_all(spectra.reshape(64, 4, 64, 128), TURN, 0, 0, tiled=True)  9.51 us
    pallas_call x4, Pallas kernels, form_beams(): pl.pallas_call(beam_kernel, grid_spec=pltpu.PrefetchScalarGridSpec(num_sc...  7.44 us
    ppermute x6, waiting for transfers between devices, shift(): return lax.ppermute(value, axis, [(n, (n + offset) % 4) for n in range(4)])  7.04 us
  transfers between devices with their start and end apart: 17, of which 6 were waited for; matrix products, arithmetic and copies ran while one was open for 1% of the time, Pallas kernels for 18%

profile of v8, /device:TPU:1, one launch (start us, length us, event | category | flops | bytes accessed | tf_op | source)
XLA Modules:
  0.0 153.3 jit_solution(4067478820544148433)
XLA Ops:
  0.6 0.9 reshape.101
  1.7 1.2 convolution_bitcast_fusion
  2.9 0.8 broadcast_in_dim.27
  3.8 15.1 %all-to-all-start = ((f32[64,16,128]{2,1,0:T(8,128)}), f32[64,16,128]{2,1,0:T(8,128)S(1)}, u32[]{:S(2)}, u32[]{:S(2)}) async-start(f32[64,16,128]{2,1,0:T(8,128)} %bitcast.6), calls=%async_computation | async-start | bytes 1048576 | tf_op jit(solution)/shard_map/all_to_all | solution.py:319
  18.9 20.0 %channelize.1 = bf16[2,2,4,4,4,2,32,128]{7,6,5,4,3,2,1,0:T(8,128)(2,1)} custom-call(bf16[2,75,128,128]{3,2,1,0:T(8,128)(2,1)} %bitcast.41, f32[12,8192]{1,0:T(8,128)} %taps.1, bf16[256,128]{1,0:T(8,128)(2,1)} %constant.76.clone.one, f32[2,64,128]{2,1,0:T(8,128)} %constant.77.clone.twist, bf16[128,256]{1,0:T(8,128)(2,1)} %constant.78.clone.two), custom_call_target="tpu_custom_call" | custom-call | tf_op jit(solution)/shard_map/channelize/pallas_call | solution.py:133
  38.9 0.5 keep_owner.1
  39.4 9.5 %all-to-all-start.1 = ((bf16[64,4,64,128]{3,2,1,0:T(8,128)(2,1)}), bf16[64,4,64,128]{3,2,1,0:T(8,128)(2,1)}, u32[]{:S(2)}, u32[]{:S(2)}) async-start(bf16[64,4,64,128]{3,2,1,0:T(8,128)(2,1)} %bitcast.40), calls=%async_computation.1 | async-start | bytes 8388608 | tf_op jit(solution)/shard_map/all_to_all | solution.py:326
  49.0 0.7 gather_fusion
  49.7 1.7 %collective-permute-start = (f32[16,128]{1,0:T(8,128)S(1)}, f32[16,128]{1,0:T(8,128)S(1)}, u32[]{:S(2)}, u32[]{:S(2)}) collective-permute-start(f32[16,128]{1,0:T(8,128)S(1)} %keep_owner.1), channel_id=1, source_target_pairs={{0,3},{1,2},{2,1},{3,0},{4,7},{5,6},{6,5},{7,4},{8,11},{9,10},{10,... | collective-permute-start | bytes 24584 | tf_op jit(solution)/shard_map/ppermute | solution.py:307
  51.9 0.5 fusion
  52.4 45.0 %collective-permute-done = f32[16,128]{1,0:T(8,128)S(1)} collective-permute-done((f32[16,128]{1,0:T(8,128)S(1)}, f32[16,128]{1,0:T(8,128)S(1)}, u32[]{:S(2)}, u32[]{:S(2)}) %collective-permute-start) | collective-permute-done | bytes 8224 | tf_op jit(solution)/shard_map/ppermute | solution.py:307
  97.9 0.3 multiply_bitcast_fusion.1
  98.3 0.3 multiply_bitcast_fusion
  98.6 1.5 all-to-all-done.1.spectra
  100.1 1.9 %form_beams.6 = (bf16[4,16,16,128]{3,2,1,0:T(8,128)(2,1)S(1)}, bf16[4,16,16,128]{3,2,1,0:T(8,128)(2,1)S(1)}) custom-call(s32[1]{0:T(128)} %bitcast.20.where, bf16[64,4,64,128]{3,2,1,0:T(8,128)(2,1)} %all-to-all-done.1.spectra, f32[2,64,128]{2,1,0:T(8,128)S(1)} %get-tuple-element.42.base, f32[2,64,128]{2,1,0:T(8,128)S(1)} %pad_maximum_fusion.1.step), custom_call_target="tpu_custom_call" | custom-call | tf_op jit(solution)/shard_map/form_beams/pallas_call | solution.py:193
  102.0 2.2 %collective-permute-start.3 = (bf16[4,16,16,128]{3,2,1,0:T(8,128)(2,1)S(1)}, bf16[4,16,16,128]{3,2,1,0:T(8,128)(2,1)S(1)}, u32[]{:S(2)}, u32[]{:S(2)}) collective-permute-start(bf16[4,16,16,128]{3,2,1,0:T(8,128)(2,1)S(1)} %get-tuple-element.20), channel_id=1, source_target_pairs={{0,32},{32,64},{64,96},{96,0},{1,33},{33,65},{65,97},{97,1},{2,34}... | collective-permute-start | bytes 786440 | tf_op jit(solution)/shard_map/ppermute | solution.py:303
  104.2 1.4 collective-permute-start.10
  105.6 1.9 %form_beams.7 = (bf16[4,16,16,128]{3,2,1,0:T(8,128)(2,1)S(1)}, bf16[4,16,16,128]{3,2,1,0:T(8,128)(2,1)S(1)}) custom-call(s32[1]{0:T(128)} %bitcast.23.where, bf16[64,4,64,128]{3,2,1,0:T(8,128)(2,1)} %all-to-all-done.1.spectra, f32[2,64,128]{2,1,0:T(8,128)S(1)} %get-tuple-element.43.base, f32[2,64,128]{2,1,0:T(8,128)S(1)} %pad_maximum_fusion.1.step), custom_call_target="tpu_custom_call" | custom-call | tf_op jit(solution)/shard_map/form_beams/pallas_call | solution.py:193
  107.5 1.6 %collective-permute-start.5 = (bf16[4,16,16,128]{3,2,1,0:T(8,128)(2,1)S(1)}, bf16[4,16,16,128]{3,2,1,0:T(8,128)(2,1)S(1)}, u32[]{:S(2)}, u32[]{:S(2)}) collective-permute-start(bf16[4,16,16,128]{3,2,1,0:T(8,128)(2,1)S(1)} %get-tuple-element.21), channel_id=1, source_target_pairs={{0,96},{32,0},{64,32},{96,64},{1,97},{33,1},{65,33},{97,65},{2,98}... | collective-permute-start | bytes 786440 | tf_op jit(solution)/shard_map/ppermute | solution.py:303
  109.1 1.9 %form_beams.5 = (bf16[4,16,16,128]{3,2,1,0:T(8,128)(2,1)S(1)}, bf16[4,16,16,128]{3,2,1,0:T(8,128)(2,1)S(1)}) custom-call(s32[1]{0:T(128)} %bitcast.17.where, bf16[64,4,64,128]{3,2,1,0:T(8,128)(2,1)} %all-to-all-done.1.spectra, f32[2,64,128]{2,1,0:T(8,128)S(1)} %get-tuple-element.41.base, f32[2,64,128]{2,1,0:T(8,128)S(1)} %pad_maximum_fusion.1.step), custom_call_target="tpu_custom_call" | custom-call | tf_op jit(solution)/shard_map/form_beams/pallas_call | solution.py:193
  111.0 1.1 collective-permute-start.4
  112.1 3.3 %collective-permute-start.9 = (bf16[4,16,16,128]{3,2,1,0:T(8,128)(2,1)S(1)}, bf16[4,16,16,128]{3,2,1,0:T(8,128)(2,1)S(1)}, u32[]{:S(2)}, u32[]{:S(2)}) collective-permute-start(bf16[4,16,16,128]{3,2,1,0:T(8,128)(2,1)S(1)} %get-tuple-element.23), channel_id=1, source_target_pairs={{0,32},{32,64},{64,96},{96,0},{1,33},{33,65},{65,97},{97,1},{2,34}... | collective-permute-start | bytes 786440 | tf_op jit(solution)/shard_map/ppermute | solution.py:303
  115.9 1.9 %form_beams.4 = (bf16[4,16,16,128]{3,2,1,0:T(8,128)(2,1)S(1)}, bf16[4,16,16,128]{3,2,1,0:T(8,128)(2,1)S(1)}) custom-call(s32[1]{0:T(128)} %bitcast.1.where, bf16[64,4,64,128]{3,2,1,0:T(8,128)(2,1)} %all-to-all-done.1.spectra, f32[2,64,128]{2,1,0:T(8,128)S(1)} %get-tuple-element.40.base, f32[2,64,128]{2,1,0:T(8,128)S(1)} %pad_maximum_fusion.1.step), custom_call_target="tpu_custom_call" | custom-call | tf_op jit(solution)/shard_map/form_beams/pallas_call | solution.py:193
  117.8 6.9 %collective-permute-done.4.refs_1_ = bf16[4,16,16,128]{3,2,1,0:T(8,128)(2,1)S(1)} collective-permute-done((bf16[4,16,16,128]{3,2,1,0:T(8,128)(2,1)S(1)}, bf16[4,16,16,128]{3,2,1,0:T(8,128)(2,1)S(1)}, u32[]{:S(2)}, u32[]{:S(2)}) %collective-permute-start.4) | collective-permute-done | bytes 262176 | tf_op jit(solution)/shard_map/ppermute | solution.py:303
  124.8 1.4 collective-permute-start.6
  126.2 16.0 %collective-permute-start.7 = (bf16[16,16,128]{2,1,0:T(8,128)(2,1)S(1)}, bf16[16,16,128]{2,1,0:T(8,128)(2,1)S(1)}, u32[]{:S(2)}, u32[]{:S(2)}) collective-permute-start(bf16[16,16,128]{2,1,0:T(8,128)(2,1)S(1)} %add_group.10), channel_id=1, source_target_pairs={{0,2},{1,3},{2,0},{3,1},{4,6},{5,7},{6,4},{7,5},{8,10},{9,11},{10,... | collective-permute-start | bytes 196616 | tf_op jit(solution)/shard_map/ppermute | solution.py:307
  142.4 1.7 %collective-permute-start.12 = (bf16[16,16,128]{2,1,0:T(8,128)(2,1)S(1)}, bf16[16,16,128]{2,1,0:T(8,128)(2,1)S(1)}, u32[]{:S(2)}, u32[]{:S(2)}) collective-permute-start(bf16[16,16,128]{2,1,0:T(8,128)(2,1)S(1)} %add_group.13), channel_id=1, source_target_pairs={{0,1},{1,0},{2,3},{3,2},{4,5},{5,4},{6,7},{7,6},{8,9},{9,8},{10,11... | collective-permute-start | bytes 196616 | tf_op jit(solution)/shard_map/ppermute | solution.py:307
  144.1 3.6 %collective-permute-start.13 = (bf16[16,16,128]{2,1,0:T(8,128)(2,1)S(1)}, bf16[16,16,128]{2,1,0:T(8,128)(2,1)S(1)}, u32[]{:S(2)}, u32[]{:S(2)}) collective-permute-start(bf16[16,16,128]{2,1,0:T(8,128)(2,1)S(1)} %add_group.14), channel_id=1, source_target_pairs={{0,2},{1,3},{2,0},{3,1},{4,6},{5,7},{6,4},{7,5},{8,10},{9,11},{10,... | collective-permute-start | bytes 196616 | tf_op jit(solution)/shard_map/ppermute | solution.py:307
  148.0 1.5 merge.2
  149.4 0.7 collective-permute-done.13.refs_2_
  150.2 1.7 %collective-permute-done.14.refs_3_ = bf16[16,16,128]{2,1,0:T(8,128)(2,1)S(1)} collective-permute-done((bf16[16,16,128]{2,1,0:T(8,128)(2,1)S(1)}, bf16[16,16,128]{2,1,0:T(8,128)(2,1)S(1)}, u32[]{:S(2)}, u32[]{:S(2)}) %collective-permute-start.14) | collective-permute-done | bytes 65568 | tf_op jit(solution)/shard_map/ppermute | solution.py:307
  151.8 1.5 merge.3
  (45 shorter events, 2.1 us)
Async XLA Ops:
  0.6 48.4 %copy-start = (f32[64,512]{1,0:T(8,128)S(1)}, f32[64,512]{1,0:T(8,128)}, u32[]{:S(2)}) copy-start(f32[64,512]{1,0:T(8,128)} %param.13) | copy-start | bytes 393220
  3.8 35.1 %all-to-all-start = ((f32[64,16,128]{2,1,0:T(8,128)}), f32[64,16,128]{2,1,0:T(8,128)S(1)}, u32[]{:S(2)}, u32[]{:S(2)}) async-start(f32[64,16,128]{2,1,0:T(8,128)} %bitcast.6), calls=%async_computation | async-start | bytes 1048576 | tf_op jit(solution)/shard_map/all_to_all | solution.py:319
  18.9 20.0 %copy-start.1 = (s32[4]{0:T(128)S(1)}, s32[4]{0:T(128)}, u32[]{:S(2)}) copy-start(s32[4]{0:T(128)} %owners.1) | copy-start | bytes 52
  39.4 9.5 %copy-start.2 = (s32[64]{0:T(128)S(1)}, s32[64]{0:T(128)}, u32[]{:S(2)}) copy-start(s32[64]{0:T(128)} %param.15) | copy-start | bytes 772
  39.4 60.6 %all-to-all-start.1 = ((bf16[64,4,64,128]{3,2,1,0:T(8,128)(2,1)}), bf16[64,4,64,128]{3,2,1,0:T(8,128)(2,1)}, u32[]{:S(2)}, u32[]{:S(2)}) async-start(bf16[64,4,64,128]{3,2,1,0:T(8,128)(2,1)} %bitcast.40), calls=%async_computation.1 | async-start | bytes 8388608 | tf_op jit(solution)/shard_map/all_to_all | solution.py:326
  49.7 47.8 %collective-permute-start = (f32[16,128]{1,0:T(8,128)S(1)}, f32[16,128]{1,0:T(8,128)S(1)}, u32[]{:S(2)}, u32[]{:S(2)}) collective-permute-start(f32[16,128]{1,0:T(8,128)S(1)} %keep_owner.1), channel_id=1, source_target_pairs={{0,3},{1,2},{2,1},{3,0},{4,7},{5,6},{6,5},{7,4},{8,11},{9,10},{10,... | collective-permute-start | bytes 24584 | tf_op jit(solution)/shard_map/ppermute | solution.py:307
  51.4 46.1 %collective-permute-start.1 = (f32[16,128]{1,0:T(8,128)S(1)}, f32[16,128]{1,0:T(8,128)S(1)}, u32[]{:S(2)}, u32[]{:S(2)}) collective-permute-start(f32[16,128]{1,0:T(8,128)S(1)} %keep_owner.1), channel_id=1, source_target_pairs={{0,2},{1,3},{2,0},{3,1},{4,6},{5,7},{6,4},{7,5},{8,10},{9,11},{10,... | collective-permute-start | bytes 24584 | tf_op jit(solution)/shard_map/ppermute | solution.py:307
  51.6 45.9 %collective-permute-start.2 = (f32[16,128]{1,0:T(8,128)S(1)}, f32[16,128]{1,0:T(8,128)S(1)}, u32[]{:S(2)}, u32[]{:S(2)}) collective-permute-start(f32[16,128]{1,0:T(8,128)S(1)} %keep_owner.1), channel_id=1, source_target_pairs={{0,1},{1,0},{2,3},{3,2},{4,5},{5,4},{6,7},{7,6},{8,9},{9,8},{10,11... | collective-permute-start | bytes 24584 | tf_op jit(solution)/shard_map/ppermute | solution.py:307
  102.0 9.0 %collective-permute-start.3 = (bf16[4,16,16,128]{3,2,1,0:T(8,128)(2,1)S(1)}, bf16[4,16,16,128]{3,2,1,0:T(8,128)(2,1)S(1)}, u32[]{:S(2)}, u32[]{:S(2)}) collective-permute-start(bf16[4,16,16,128]{3,2,1,0:T(8,128)(2,1)S(1)} %get-tuple-element.20), channel_id=1, source_target_pairs={{0,32},{32,64},{64,96},{96,0},{1,33},{33,65},{65,97},{97,1},{2,34}... | collective-permute-start | bytes 786440 | tf_op jit(solution)/shard_map/ppermute | solution.py:303
  104.2 11.3 %collective-permute-start.10 = (bf16[4,16,16,128]{3,2,1,0:T(8,128)(2,1)S(1)}, bf16[4,16,16,128]{3,2,1,0:T(8,128)(2,1)S(1)}, u32[]{:S(2)}, u32[]{:S(2)}) collective-permute-start(bf16[4,16,16,128]{3,2,1,0:T(8,128)(2,1)S(1)} %get-tuple-element.25), channel_id=1, source_target_pairs={{0,96},{32,0},{64,32},{96,64},{1,97},{33,1},{65,33},{97,65},{2,98}... | collective-permute-start | bytes 786440 | tf_op jit(solution)/shard_map/ppermute | solution.py:303
  107.5 10.3 %collective-permute-start.5 = (bf16[4,16,16,128]{3,2,1,0:T(8,128)(2,1)S(1)}, bf16[4,16,16,128]{3,2,1,0:T(8,128)(2,1)S(1)}, u32[]{:S(2)}, u32[]{:S(2)}) collective-permute-start(bf16[4,16,16,128]{3,2,1,0:T(8,128)(2,1)S(1)} %get-tuple-element.21), channel_id=1, source_target_pairs={{0,96},{32,0},{64,32},{96,64},{1,97},{33,1},{65,33},{97,65},{2,98}... | collective-permute-start | bytes 786440 | tf_op jit(solution)/shard_map/ppermute | solution.py:303
  111.0 13.7 %collective-permute-start.4 = (bf16[4,16,16,128]{3,2,1,0:T(8,128)(2,1)S(1)}, bf16[4,16,16,128]{3,2,1,0:T(8,128)(2,1)S(1)}, u32[]{:S(2)}, u32[]{:S(2)}) collective-permute-start(bf16[4,16,16,128]{3,2,1,0:T(8,128)(2,1)S(1)} %add_pair.2), channel_id=1, source_target_pairs={{0,32},{32,64},{64,96},{96,0},{1,33},{33,65},{65,97},{97,1},{2,34}... | collective-permute-start | bytes 786440 | tf_op jit(solution)/shard_map/ppermute | solution.py:303
  112.1 30.2 %collective-permute-start.9 = (bf16[4,16,16,128]{3,2,1,0:T(8,128)(2,1)S(1)}, bf16[4,16,16,128]{3,2,1,0:T(8,128)(2,1)S(1)}, u32[]{:S(2)}, u32[]{:S(2)}) collective-permute-start(bf16[4,16,16,128]{3,2,1,0:T(8,128)(2,1)S(1)} %get-tuple-element.23), channel_id=1, source_target_pairs={{0,32},{32,64},{64,96},{96,0},{1,33},{33,65},{65,97},{97,1},{2,34}... | collective-permute-start | bytes 786440 | tf_op jit(solution)/shard_map/ppermute | solution.py:303
  115.5 26.8 %collective-permute-start.11 = (bf16[4,16,16,128]{3,2,1,0:T(8,128)(2,1)S(1)}, bf16[4,16,16,128]{3,2,1,0:T(8,128)(2,1)S(1)}, u32[]{:S(2)}, u32[]{:S(2)}) collective-permute-start(bf16[4,16,16,128]{3,2,1,0:T(8,128)(2,1)S(1)} %add_pair.3), channel_id=1, source_target_pairs={{0,96},{32,0},{64,32},{96,64},{1,97},{33,1},{65,33},{97,65},{2,98}... | collective-permute-start | bytes 786440 | tf_op jit(solution)/shard_map/ppermute | solution.py:303
  124.8 23.0 %collective-permute-start.6 = (bf16[16,16,128]{2,1,0:T(8,128)(2,1)S(1)}, bf16[16,16,128]{2,1,0:T(8,128)(2,1)S(1)}, u32[]{:S(2)}, u32[]{:S(2)}) collective-permute-start(bf16[16,16,128]{2,1,0:T(8,128)(2,1)S(1)} %add_group.9), channel_id=1, source_target_pairs={{0,1},{1,0},{2,3},{3,2},{4,5},{5,4},{6,7},{7,6},{8,9},{9,8},{10,11... | collective-permute-start | bytes 196616 | tf_op jit(solution)/shard_map/ppermute | solution.py:307
  126.2 21.8 %collective-permute-start.7 = (bf16[16,16,128]{2,1,0:T(8,128)(2,1)S(1)}, bf16[16,16,128]{2,1,0:T(8,128)(2,1)S(1)}, u32[]{:S(2)}, u32[]{:S(2)}) collective-permute-start(bf16[16,16,128]{2,1,0:T(8,128)(2,1)S(1)} %add_group.10), channel_id=1, source_target_pairs={{0,2},{1,3},{2,0},{3,1},{4,6},{5,7},{6,4},{7,5},{8,10},{9,11},{10,... | collective-permute-start | bytes 196616 | tf_op jit(solution)/shard_map/ppermute | solution.py:307
  142.2 5.7 %collective-permute-start.8 = (bf16[16,16,128]{2,1,0:T(8,128)(2,1)S(1)}, bf16[16,16,128]{2,1,0:T(8,128)(2,1)S(1)}, u32[]{:S(2)}, u32[]{:S(2)}) collective-permute-start(bf16[16,16,128]{2,1,0:T(8,128)(2,1)S(1)} %add_group.11), channel_id=1, source_target_pairs={{0,3},{1,2},{2,1},{3,0},{4,7},{5,6},{6,5},{7,4},{8,11},{9,10},{10,... | collective-permute-start | bytes 196616 | tf_op jit(solution)/shard_map/ppermute | solution.py:307
  142.4 7.1 %collective-permute-start.12 = (bf16[16,16,128]{2,1,0:T(8,128)(2,1)S(1)}, bf16[16,16,128]{2,1,0:T(8,128)(2,1)S(1)}, u32[]{:S(2)}, u32[]{:S(2)}) collective-permute-start(bf16[16,16,128]{2,1,0:T(8,128)(2,1)S(1)} %add_group.13), channel_id=1, source_target_pairs={{0,1},{1,0},{2,3},{3,2},{4,5},{5,4},{6,7},{7,6},{8,9},{9,8},{10,11... | collective-permute-start | bytes 196616 | tf_op jit(solution)/shard_map/ppermute | solution.py:307
  144.1 6.0 %collective-permute-start.13 = (bf16[16,16,128]{2,1,0:T(8,128)(2,1)S(1)}, bf16[16,16,128]{2,1,0:T(8,128)(2,1)S(1)}, u32[]{:S(2)}, u32[]{:S(2)}) collective-permute-start(bf16[16,16,128]{2,1,0:T(8,128)(2,1)S(1)} %add_group.14), channel_id=1, source_target_pairs={{0,2},{1,3},{2,0},{3,1},{4,6},{5,7},{6,4},{7,5},{8,10},{9,11},{10,... | collective-permute-start | bytes 196616 | tf_op jit(solution)/shard_map/ppermute | solution.py:307
  147.8 4.1 %collective-permute-start.14 = (bf16[16,16,128]{2,1,0:T(8,128)(2,1)S(1)}, bf16[16,16,128]{2,1,0:T(8,128)(2,1)S(1)}, u32[]{:S(2)}, u32[]{:S(2)}) collective-permute-start(bf16[16,16,128]{2,1,0:T(8,128)(2,1)S(1)} %add_group.15), channel_id=1, source_target_pairs={{0,3},{1,2},{2,1},{3,0},{4,7},{5,6},{6,5},{7,4},{8,11},{9,10},{10,... | collective-permute-start | bytes 196616 | tf_op jit(solution)/shard_map/ppermute | solution.py:307

commit v9 on v8

--- a/solution.py
+++ b/solution.py
@@ -29,7 +29,7 @@
 FRAME_CHUNK = 16
 TURN_ROWS = 132
 STAGE_ROWS = 36
-WIDE_ROWS = 68
+WIDE_ROWS = 34
 BEAM_ROWS = 24
 
 
@@ -157,15 +157,16 @@
 def beam_kernel(where, spectra, base, step, out_re, out_im, wide):
     del where
     for src in range(64):
-        wide[src * WIDE_ROWS : src * WIDE_ROWS + 64, :] = spectra[src, 0].astype(F32)
+        for s in range(2):
+            row = (src * 2 + s) * WIDE_ROWS
+            wide[row : row + 32, :] = spectra[src, 0, s * 32 : s * 32 + 32, :].astype(F32)
     cos_w, sin_w = base[0], base[1]
     cos_step, sin_step = step[0], step[1]
     for i in range(16):
         right = jnp.concatenate(
             [
-                wide[pl.ds(s * 32 + ri * 16 + i, 64, stride=WIDE_ROWS), :].astype(BF16)
+                wide[pl.ds(ri * 16 + i, 128, stride=WIDE_ROWS), :].astype(BF16)
                 for ri in range(2)
-                for s in range(2)
             ],
             axis=0,
         )
@@ -201,7 +202,7 @@
                 CHIP,
             ],
             out_specs=[CHIP, CHIP],
-            scratch_shapes=[pltpu.VMEM((64 * WIDE_ROWS, 128), F32)],
+            scratch_shapes=[pltpu.VMEM((128 * WIDE_ROWS, 128), F32)],
         ),
         out_shape=[pltpu.VMEM((4, 16, 16, 128), BF16)] * 2,
         compiler_params=pltpu.CompilerParams(vmem_limit_bytes=SMALL_LIMIT),
@@ -291,7 +292,8 @@
 
 
 def station_pick(station_map):
-    phys = station_map.reshape(2, 4, 32, 2).transpose(1, 3, 0, 2).reshape(STATIONS)
+    starts = [(yh * 4 + zh) * 64 for zh in range(4) for yh in range(2)]
+    phys = jnp.concatenate([station_map[n : n + 64] for n in starts])
     return (jnp.arange(STATIONS, dtype=jnp.int32)[:, None] == phys[None, :]).astype(F32)
 
 

time: 154 us -> 154 us (level)
  no operation moved by 1% of the time
where the time goes in v9:
time: 154 us; the launch traced here: 153 us
  starting transfers between devices  59.7 us (39%)
  waiting for transfers between devices  56.1 us (36%)
  Pallas kernels  31.1 us (20%)
  local copies, waits for them, and re-layouts  2.67 us (2%)
  matrix products  1.65 us (1%)
    ppermute x9, waiting for transfers between devices, swap(): return lax.ppermute(value, axes, [(n, n ^ offset) for n in range(4)])  47.5 us
    ppermute x9, starting transfers between devices, swap(): return lax.ppermute(value, axes, [(n, n ^ offset) for n in range(4)])  25.1 us
    pallas_call x1, Pallas kernels, channelize(): pl.pallas_call(channel_kernel, grid=(2, 8), in_specs=[pl.BlockSpec((1, 75...  20 us
    all_to_all x1, starting transfers between devices, on_device(): lax.all_to_all(model.reshape(64, slots, 128), AXES[:4], 0, 0, tiled=True)  15.1 us
    ppermute x6, starting transfers between devices, shift(): return lax.ppermute(value, axis, [(n, (n + offset) % 4) for n in range(4)])  10 us
    all_to_all x1, starting transfers between devices, on_device(): lax.all_to_all(spectra.reshape(64, 4, 64, 128), TURN, 0, 0, tiled=True)  9.51 us
    pallas_call x4, Pallas kernels, form_beams(): pl.pallas_call(beam_kernel, grid_spec=pltpu.PrefetchScalarGridSpec(num_sc...  7.31 us
    ppermute x6, waiting for transfers between devices, shift(): return lax.ppermute(value, axis, [(n, (n + offset) % 4) for n in range(4)])  7.13 us
  transfers between devices with their start and end apart: 17, of which 6 were waited for; matrix products, arithmetic and copies ran while one was open for 1% of the time, Pallas kernels for 18%

profile of v9, /device:TPU:1, one launch (start us, length us, event | category | flops | bytes accessed | tf_op | source)
XLA Modules:
  0.0 153.3 jit_solution(8596624349928128091)
XLA Ops:
  0.6 1.1 fusion.6
  1.8 1.2 convolution_bitcast_fusion
  3.0 0.8 broadcast_in_dim.28
  3.8 15.1 %all-to-all-start = ((f32[64,16,128]{2,1,0:T(8,128)}), f32[64,16,128]{2,1,0:T(8,128)S(1)}, u32[]{:S(2)}, u32[]{:S(2)}) async-start(f32[64,16,128]{2,1,0:T(8,128)} %bitcast.5), calls=%async_computation | async-start | bytes 1048576 | tf_op jit(solution)/shard_map/all_to_all | solution.py:321
  19.0 20.0 %channelize.1 = bf16[2,2,4,4,4,2,32,128]{7,6,5,4,3,2,1,0:T(8,128)(2,1)} custom-call(bf16[2,75,128,128]{3,2,1,0:T(8,128)(2,1)} %bitcast.40, f32[12,8192]{1,0:T(8,128)} %taps.1, bf16[256,128]{1,0:T(8,128)(2,1)} %constant.76.clone.one, f32[2,64,128]{2,1,0:T(8,128)} %constant.77.clone.twist, bf16[128,256]{1,0:T(8,128)(2,1)} %constant.78.clone.two), custom_call_target="tpu_custom_call" | custom-call | tf_op jit(solution)/shard_map/channelize/pallas_call | solution.py:133
  39.0 0.5 keep_owner.1
  39.5 9.5 %all-to-all-start.1 = ((bf16[64,4,64,128]{3,2,1,0:T(8,128)(2,1)}), bf16[64,4,64,128]{3,2,1,0:T(8,128)(2,1)}, u32[]{:S(2)}, u32[]{:S(2)}) async-start(bf16[64,4,64,128]{3,2,1,0:T(8,128)(2,1)} %bitcast.39), calls=%async_computation.1 | async-start | bytes 8388608 | tf_op jit(solution)/shard_map/all_to_all | solution.py:328
  49.1 0.7 gather_fusion
  49.7 1.7 %collective-permute-start = (f32[16,128]{1,0:T(8,128)S(1)}, f32[16,128]{1,0:T(8,128)S(1)}, u32[]{:S(2)}, u32[]{:S(2)}) collective-permute-start(f32[16,128]{1,0:T(8,128)S(1)} %keep_owner.1), channel_id=1, source_target_pairs={{0,3},{1,2},{2,1},{3,0},{4,7},{5,6},{6,5},{7,4},{8,11},{9,10},{10,... | collective-permute-start | bytes 24584 | tf_op jit(solution)/shard_map/ppermute | solution.py:309
  52.0 0.5 fusion
  52.5 45.1 %collective-permute-done = f32[16,128]{1,0:T(8,128)S(1)} collective-permute-done((f32[16,128]{1,0:T(8,128)S(1)}, f32[16,128]{1,0:T(8,128)S(1)}, u32[]{:S(2)}, u32[]{:S(2)}) %collective-permute-start) | collective-permute-done | bytes 8224 | tf_op jit(solution)/shard_map/ppermute | solution.py:309
  98.0 0.3 multiply_bitcast_fusion.1
  98.3 0.3 multiply_bitcast_fusion
  98.7 1.5 all-to-all-done.1.spectra
  100.2 1.8 %form_beams.6 = (bf16[4,16,16,128]{3,2,1,0:T(8,128)(2,1)S(1)}, bf16[4,16,16,128]{3,2,1,0:T(8,128)(2,1)S(1)}) custom-call(s32[1]{0:T(128)} %bitcast.19.where, bf16[64,4,64,128]{3,2,1,0:T(8,128)(2,1)} %all-to-all-done.1.spectra, f32[2,64,128]{2,1,0:T(8,128)S(1)} %get-tuple-element.50.base, f32[2,64,128]{2,1,0:T(8,128)S(1)} %pad_maximum_fusion.1.step), custom_call_target="tpu_custom_call" | custom-call | tf_op jit(solution)/shard_map/form_beams/pallas_call | solution.py:194
  102.0 2.2 %collective-permute-start.3 = (bf16[4,16,16,128]{3,2,1,0:T(8,128)(2,1)S(1)}, bf16[4,16,16,128]{3,2,1,0:T(8,128)(2,1)S(1)}, u32[]{:S(2)}, u32[]{:S(2)}) collective-permute-start(bf16[4,16,16,128]{3,2,1,0:T(8,128)(2,1)S(1)} %get-tuple-element.20), channel_id=1, source_target_pairs={{0,32},{32,64},{64,96},{96,0},{1,33},{33,65},{65,97},{97,1},{2,34}... | collective-permute-start | bytes 786440 | tf_op jit(solution)/shard_map/ppermute | solution.py:305
  104.2 1.4 collective-permute-start.10
  105.7 1.8 %form_beams.7 = (bf16[4,16,16,128]{3,2,1,0:T(8,128)(2,1)S(1)}, bf16[4,16,16,128]{3,2,1,0:T(8,128)(2,1)S(1)}) custom-call(s32[1]{0:T(128)} %bitcast.22.where, bf16[64,4,64,128]{3,2,1,0:T(8,128)(2,1)} %all-to-all-done.1.spectra, f32[2,64,128]{2,1,0:T(8,128)S(1)} %get-tuple-element.51.base, f32[2,64,128]{2,1,0:T(8,128)S(1)} %pad_maximum_fusion.1.step), custom_call_target="tpu_custom_call" | custom-call | tf_op jit(solution)/shard_map/form_beams/pallas_call | solution.py:194
  107.5 1.6 %collective-permute-start.5 = (bf16[4,16,16,128]{3,2,1,0:T(8,128)(2,1)S(1)}, bf16[4,16,16,128]{3,2,1,0:T(8,128)(2,1)S(1)}, u32[]{:S(2)}, u32[]{:S(2)}) collective-permute-start(bf16[4,16,16,128]{3,2,1,0:T(8,128)(2,1)S(1)} %get-tuple-element.21), channel_id=1, source_target_pairs={{0,96},{32,0},{64,32},{96,64},{1,97},{33,1},{65,33},{97,65},{2,98}... | collective-permute-start | bytes 786440 | tf_op jit(solution)/shard_map/ppermute | solution.py:305
  109.1 1.8 %form_beams.5 = (bf16[4,16,16,128]{3,2,1,0:T(8,128)(2,1)S(1)}, bf16[4,16,16,128]{3,2,1,0:T(8,128)(2,1)S(1)}) custom-call(s32[1]{0:T(128)} %bitcast.16.where, bf16[64,4,64,128]{3,2,1,0:T(8,128)(2,1)} %all-to-all-done.1.spectra, f32[2,64,128]{2,1,0:T(8,128)S(1)} %get-tuple-element.49.base, f32[2,64,128]{2,1,0:T(8,128)S(1)} %pad_maximum_fusion.1.step), custom_call_target="tpu_custom_call" | custom-call | tf_op jit(solution)/shard_map/form_beams/pallas_call | solution.py:194
  111.0 1.1 collective-permute-start.4
  112.1 3.4 %collective-permute-start.9 = (bf16[4,16,16,128]{3,2,1,0:T(8,128)(2,1)S(1)}, bf16[4,16,16,128]{3,2,1,0:T(8,128)(2,1)S(1)}, u32[]{:S(2)}, u32[]{:S(2)}) collective-permute-start(bf16[4,16,16,128]{3,2,1,0:T(8,128)(2,1)S(1)} %get-tuple-element.23), channel_id=1, source_target_pairs={{0,32},{32,64},{64,96},{96,0},{1,33},{33,65},{65,97},{97,1},{2,34}... | collective-permute-start | bytes 786440 | tf_op jit(solution)/shard_map/ppermute | solution.py:305
  115.8 1.8 %form_beams.4 = (bf16[4,16,16,128]{3,2,1,0:T(8,128)(2,1)S(1)}, bf16[4,16,16,128]{3,2,1,0:T(8,128)(2,1)S(1)}) custom-call(s32[1]{0:T(128)} %bitcast.1.where, bf16[64,4,64,128]{3,2,1,0:T(8,128)(2,1)} %all-to-all-done.1.spectra, f32[2,64,128]{2,1,0:T(8,128)S(1)} %get-tuple-element.48.base, f32[2,64,128]{2,1,0:T(8,128)S(1)} %pad_maximum_fusion.1.step), custom_call_target="tpu_custom_call" | custom-call | tf_op jit(solution)/shard_map/form_beams/pallas_call | solution.py:194
  117.8 6.9 %collective-permute-done.4.refs_1_ = bf16[4,16,16,128]{3,2,1,0:T(8,128)(2,1)S(1)} collective-permute-done((bf16[4,16,16,128]{3,2,1,0:T(8,128)(2,1)S(1)}, bf16[4,16,16,128]{3,2,1,0:T(8,128)(2,1)S(1)}, u32[]{:S(2)}, u32[]{:S(2)}) %collective-permute-start.4) | collective-permute-done | bytes 262176 | tf_op jit(solution)/shard_map/ppermute | solution.py:305
  124.8 1.4 collective-permute-start.6
  126.2 16.0 %collective-permute-start.7 = (bf16[16,16,128]{2,1,0:T(8,128)(2,1)S(1)}, bf16[16,16,128]{2,1,0:T(8,128)(2,1)S(1)}, u32[]{:S(2)}, u32[]{:S(2)}) collective-permute-start(bf16[16,16,128]{2,1,0:T(8,128)(2,1)S(1)} %add_group.10), channel_id=1, source_target_pairs={{0,2},{1,3},{2,0},{3,1},{4,6},{5,7},{6,4},{7,5},{8,10},{9,11},{10,... | collective-permute-start | bytes 196616 | tf_op jit(solution)/shard_map/ppermute | solution.py:309
  142.4 1.7 %collective-permute-start.12 = (bf16[16,16,128]{2,1,0:T(8,128)(2,1)S(1)}, bf16[16,16,128]{2,1,0:T(8,128)(2,1)S(1)}, u32[]{:S(2)}, u32[]{:S(2)}) collective-permute-start(bf16[16,16,128]{2,1,0:T(8,128)(2,1)S(1)} %add_group.13), channel_id=1, source_target_pairs={{0,1},{1,0},{2,3},{3,2},{4,5},{5,4},{6,7},{7,6},{8,9},{9,8},{10,11... | collective-permute-start | bytes 196616 | tf_op jit(solution)/shard_map/ppermute | solution.py:309
  144.1 3.6 %collective-permute-start.13 = (bf16[16,16,128]{2,1,0:T(8,128)(2,1)S(1)}, bf16[16,16,128]{2,1,0:T(8,128)(2,1)S(1)}, u32[]{:S(2)}, u32[]{:S(2)}) collective-permute-start(bf16[16,16,128]{2,1,0:T(8,128)(2,1)S(1)} %add_group.14), channel_id=1, source_target_pairs={{0,2},{1,3},{2,0},{3,1},{4,6},{5,7},{6,4},{7,5},{8,10},{9,11},{10,... | collective-permute-start | bytes 196616 | tf_op jit(solution)/shard_map/ppermute | solution.py:309
  148.0 1.5 merge.2
  149.5 0.7 collective-permute-done.13.refs_2_
  150.2 1.7 %collective-permute-done.14.refs_3_ = bf16[16,16,128]{2,1,0:T(8,128)(2,1)S(1)} collective-permute-done((bf16[16,16,128]{2,1,0:T(8,128)(2,1)S(1)}, bf16[16,16,128]{2,1,0:T(8,128)(2,1)S(1)}, u32[]{:S(2)}, u32[]{:S(2)}) %collective-permute-start.14) | collective-permute-done | bytes 65568 | tf_op jit(solution)/shard_map/ppermute | solution.py:309
  151.9 1.5 merge.3
  (44 shorter events, 2.1 us)
Async XLA Ops:
  0.6 48.4 %copy-start = (f32[64,512]{1,0:T(8,128)S(1)}, f32[64,512]{1,0:T(8,128)}, u32[]{:S(2)}) copy-start(f32[64,512]{1,0:T(8,128)} %param.13) | copy-start | bytes 393220
  3.8 35.1 %all-to-all-start = ((f32[64,16,128]{2,1,0:T(8,128)}), f32[64,16,128]{2,1,0:T(8,128)S(1)}, u32[]{:S(2)}, u32[]{:S(2)}) async-start(f32[64,16,128]{2,1,0:T(8,128)} %bitcast.5), calls=%async_computation | async-start | bytes 1048576 | tf_op jit(solution)/shard_map/all_to_all | solution.py:321
  19.0 20.0 %copy-start.1 = (s32[4]{0:T(128)S(1)}, s32[4]{0:T(128)}, u32[]{:S(2)}) copy-start(s32[4]{0:T(128)} %owners.1) | copy-start | bytes 52
  39.5 9.5 %copy-start.2 = (s32[64]{0:T(128)S(1)}, s32[64]{0:T(128)}, u32[]{:S(2)}) copy-start(s32[64]{0:T(128)} %param.15) | copy-start | bytes 772
  39.5 60.6 %all-to-all-start.1 = ((bf16[64,4,64,128]{3,2,1,0:T(8,128)(2,1)}), bf16[64,4,64,128]{3,2,1,0:T(8,128)(2,1)}, u32[]{:S(2)}, u32[]{:S(2)}) async-start(bf16[64,4,64,128]{3,2,1,0:T(8,128)(2,1)} %bitcast.39), calls=%async_computation.1 | async-start | bytes 8388608 | tf_op jit(solution)/shard_map/all_to_all | solution.py:328
  49.7 47.8 %collective-permute-start = (f32[16,128]{1,0:T(8,128)S(1)}, f32[16,128]{1,0:T(8,128)S(1)}, u32[]{:S(2)}, u32[]{:S(2)}) collective-permute-start(f32[16,128]{1,0:T(8,128)S(1)} %keep_owner.1), channel_id=1, source_target_pairs={{0,3},{1,2},{2,1},{3,0},{4,7},{5,6},{6,5},{7,4},{8,11},{9,10},{10,... | collective-permute-start | bytes 24584 | tf_op jit(solution)/shard_map/ppermute | solution.py:309
  51.5 46.1 %collective-permute-start.1 = (f32[16,128]{1,0:T(8,128)S(1)}, f32[16,128]{1,0:T(8,128)S(1)}, u32[]{:S(2)}, u32[]{:S(2)}) collective-permute-start(f32[16,128]{1,0:T(8,128)S(1)} %keep_owner.1), channel_id=1, source_target_pairs={{0,2},{1,3},{2,0},{3,1},{4,6},{5,7},{6,4},{7,5},{8,10},{9,11},{10,... | collective-permute-start | bytes 24584 | tf_op jit(solution)/shard_map/ppermute | solution.py:309
  51.7 45.9 %collective-permute-start.2 = (f32[16,128]{1,0:T(8,128)S(1)}, f32[16,128]{1,0:T(8,128)S(1)}, u32[]{:S(2)}, u32[]{:S(2)}) collective-permute-start(f32[16,128]{1,0:T(8,128)S(1)} %keep_owner.1), channel_id=1, source_target_pairs={{0,1},{1,0},{2,3},{3,2},{4,5},{5,4},{6,7},{7,6},{8,9},{9,8},{10,11... | collective-permute-start | bytes 24584 | tf_op jit(solution)/shard_map/ppermute | solution.py:309
  102.0 8.9 %collective-permute-start.3 = (bf16[4,16,16,128]{3,2,1,0:T(8,128)(2,1)S(1)}, bf16[4,16,16,128]{3,2,1,0:T(8,128)(2,1)S(1)}, u32[]{:S(2)}, u32[]{:S(2)}) collective-permute-start(bf16[4,16,16,128]{3,2,1,0:T(8,128)(2,1)S(1)} %get-tuple-element.20), channel_id=1, source_target_pairs={{0,32},{32,64},{64,96},{96,0},{1,33},{33,65},{65,97},{97,1},{2,34}... | collective-permute-start | bytes 786440 | tf_op jit(solution)/shard_map/ppermute | solution.py:305
  104.2 11.3 %collective-permute-start.10 = (bf16[4,16,16,128]{3,2,1,0:T(8,128)(2,1)S(1)}, bf16[4,16,16,128]{3,2,1,0:T(8,128)(2,1)S(1)}, u32[]{:S(2)}, u32[]{:S(2)}) collective-permute-start(bf16[4,16,16,128]{3,2,1,0:T(8,128)(2,1)S(1)} %get-tuple-element.25), channel_id=1, source_target_pairs={{0,96},{32,0},{64,32},{96,64},{1,97},{33,1},{65,33},{97,65},{2,98}... | collective-permute-start | bytes 786440 | tf_op jit(solution)/shard_map/ppermute | solution.py:305
  107.5 10.3 %collective-permute-start.5 = (bf16[4,16,16,128]{3,2,1,0:T(8,128)(2,1)S(1)}, bf16[4,16,16,128]{3,2,1,0:T(8,128)(2,1)S(1)}, u32[]{:S(2)}, u32[]{:S(2)}) collective-permute-start(bf16[4,16,16,128]{3,2,1,0:T(8,128)(2,1)S(1)} %get-tuple-element.21), channel_id=1, source_target_pairs={{0,96},{32,0},{64,32},{96,64},{1,97},{33,1},{65,33},{97,65},{2,98}... | collective-permute-start | bytes 786440 | tf_op jit(solution)/shard_map/ppermute | solution.py:305
  111.0 13.8 %collective-permute-start.4 = (bf16[4,16,16,128]{3,2,1,0:T(8,128)(2,1)S(1)}, bf16[4,16,16,128]{3,2,1,0:T(8,128)(2,1)S(1)}, u32[]{:S(2)}, u32[]{:S(2)}) collective-permute-start(bf16[4,16,16,128]{3,2,1,0:T(8,128)(2,1)S(1)} %add_pair.2), channel_id=1, source_target_pairs={{0,32},{32,64},{64,96},{96,0},{1,33},{33,65},{65,97},{97,1},{2,34}... | collective-permute-start | bytes 786440 | tf_op jit(solution)/shard_map/ppermute | solution.py:305
  112.1 30.2 %collective-permute-start.9 = (bf16[4,16,16,128]{3,2,1,0:T(8,128)(2,1)S(1)}, bf16[4,16,16,128]{3,2,1,0:T(8,128)(2,1)S(1)}, u32[]{:S(2)}, u32[]{:S(2)}) collective-permute-start(bf16[4,16,16,128]{3,2,1,0:T(8,128)(2,1)S(1)} %get-tuple-element.23), channel_id=1, source_target_pairs={{0,32},{32,64},{64,96},{96,0},{1,33},{33,65},{65,97},{97,1},{2,34}... | collective-permute-start | bytes 786440 | tf_op jit(solution)/shard_map/ppermute | solution.py:305
  115.6 26.8 %collective-permute-start.11 = (bf16[4,16,16,128]{3,2,1,0:T(8,128)(2,1)S(1)}, bf16[4,16,16,128]{3,2,1,0:T(8,128)(2,1)S(1)}, u32[]{:S(2)}, u32[]{:S(2)}) collective-permute-start(bf16[4,16,16,128]{3,2,1,0:T(8,128)(2,1)S(1)} %add_pair.3), channel_id=1, source_target_pairs={{0,96},{32,0},{64,32},{96,64},{1,97},{33,1},{65,33},{97,65},{2,98}... | collective-permute-start | bytes 786440 | tf_op jit(solution)/shard_map/ppermute | solution.py:305
  124.8 23.0 %collective-permute-start.6 = (bf16[16,16,128]{2,1,0:T(8,128)(2,1)S(1)}, bf16[16,16,128]{2,1,0:T(8,128)(2,1)S(1)}, u32[]{:S(2)}, u32[]{:S(2)}) collective-permute-start(bf16[16,16,128]{2,1,0:T(8,128)(2,1)S(1)} %add_group.9), channel_id=1, source_target_pairs={{0,1},{1,0},{2,3},{3,2},{4,5},{5,4},{6,7},{7,6},{8,9},{9,8},{10,11... | collective-permute-start | bytes 196616 | tf_op jit(solution)/shard_map/ppermute | solution.py:309
  126.2 21.7 %collective-permute-start.7 = (bf16[16,16,128]{2,1,0:T(8,128)(2,1)S(1)}, bf16[16,16,128]{2,1,0:T(8,128)(2,1)S(1)}, u32[]{:S(2)}, u32[]{:S(2)}) collective-permute-start(bf16[16,16,128]{2,1,0:T(8,128)(2,1)S(1)} %add_group.10), channel_id=1, source_target_pairs={{0,2},{1,3},{2,0},{3,1},{4,6},{5,7},{6,4},{7,5},{8,10},{9,11},{10,... | collective-permute-start | bytes 196616 | tf_op jit(solution)/shard_map/ppermute | solution.py:309
  142.2 5.7 %collective-permute-start.8 = (bf16[16,16,128]{2,1,0:T(8,128)(2,1)S(1)}, bf16[16,16,128]{2,1,0:T(8,128)(2,1)S(1)}, u32[]{:S(2)}, u32[]{:S(2)}) collective-permute-start(bf16[16,16,128]{2,1,0:T(8,128)(2,1)S(1)} %add_group.11), channel_id=1, source_target_pairs={{0,3},{1,2},{2,1},{3,0},{4,7},{5,6},{6,5},{7,4},{8,11},{9,10},{10,... | collective-permute-start | bytes 196616 | tf_op jit(solution)/shard_map/ppermute | solution.py:309
  142.4 7.1 %collective-permute-start.12 = (bf16[16,16,128]{2,1,0:T(8,128)(2,1)S(1)}, bf16[16,16,128]{2,1,0:T(8,128)(2,1)S(1)}, u32[]{:S(2)}, u32[]{:S(2)}) collective-permute-start(bf16[16,16,128]{2,1,0:T(8,128)(2,1)S(1)} %add_group.13), channel_id=1, source_target_pairs={{0,1},{1,0},{2,3},{3,2},{4,5},{5,4},{6,7},{7,6},{8,9},{9,8},{10,11... | collective-permute-start | bytes 196616 | tf_op jit(solution)/shard_map/ppermute | solution.py:309
  144.1 6.0 %collective-permute-start.13 = (bf16[16,16,128]{2,1,0:T(8,128)(2,1)S(1)}, bf16[16,16,128]{2,1,0:T(8,128)(2,1)S(1)}, u32[]{:S(2)}, u32[]{:S(2)}) collective-permute-start(bf16[16,16,128]{2,1,0:T(8,128)(2,1)S(1)} %add_group.14), channel_id=1, source_target_pairs={{0,2},{1,3},{2,0},{3,1},{4,6},{5,7},{6,4},{7,5},{8,10},{9,11},{10,... | collective-permute-start | bytes 196616 | tf_op jit(solution)/shard_map/ppermute | solution.py:309
  147.8 4.1 %collective-permute-start.14 = (bf16[16,16,128]{2,1,0:T(8,128)(2,1)S(1)}, bf16[16,16,128]{2,1,0:T(8,128)(2,1)S(1)}, u32[]{:S(2)}, u32[]{:S(2)}) collective-permute-start(bf16[16,16,128]{2,1,0:T(8,128)(2,1)S(1)} %add_group.15), channel_id=1, source_target_pairs={{0,3},{1,2},{2,1},{3,0},{4,7},{5,6},{6,5},{7,4},{8,11},{9,10},{10,... | collective-permute-start | bytes 196616 | tf_op jit(solution)/shard_map/ppermute | solution.py:309

commit v10 on v9

--- a/solution.py
+++ b/solution.py
@@ -136,9 +136,9 @@
         in_specs=[
             pl.BlockSpec((1, 75, 16, Q), lambda s, r: (s, 0, r, 0)),
             pl.BlockSpec((TAPS, 8 * Q), lambda s, r: (0, r)),
-            whole(256, 128),
-            whole(2, 64, Q),
-            whole(128, 256),
+            CHIP,
+            CHIP,
+            CHIP,
         ],
         out_specs=pl.BlockSpec((2, 2, 4, 4, 4, 1, 32, 128), lambda s, r: (0, 0, 0, 0, 0, s, 0, 0)),
         out_shape=jax.ShapeDtypeStruct((2, 2, 4, 4, 4, 2, 32, 128), BF16),
@@ -151,7 +151,7 @@
         ],
         compiler_params=pltpu.CompilerParams(vmem_limit_bytes=VMEM_LIMIT),
         name="channelize",
-    )(volts, taps, jnp.asarray(one), jnp.asarray(twist), jnp.asarray(two))
+    )(volts, taps, *[on_chip(jnp.asarray(table)) for table in (one, twist, two)])
 
 
 def beam_kernel(where, spectra, base, step, out_re, out_im, wide):

time: 154 us -> 157 us (1.019)
  local copies, waits for them, and re-layouts: 2.67 us -> 5.18 us
    unnamed x6 -> x12, local copies, waits for them, and re-layouts: 0.02 us -> 2.53 us
  transfers between devices with their start and end apart: 17 -> 17, of which waited for: 6 -> 6; matrix products, arithmetic and copies ran while one was open for 1% -> 1% of each run, Pallas kernels for 18% -> 17%
where the time goes in v10:
time: 157 us; the launch traced here: 156 us
  starting transfers between devices  59.7 us (38%)
  waiting for transfers between devices  56.1 us (36%)
  Pallas kernels  31 us (20%)
  local copies, waits for them, and re-layouts  5.18 us (3%)
  matrix products  1.66 us (1%)
    ppermute x9, waiting for transfers between devices, swap(): return lax.ppermute(value, axes, [(n, n ^ offset) for n in range(4)])  47.5 us
    ppermute x9, starting transfers between devices, swap(): return lax.ppermute(value, axes, [(n, n ^ offset) for n in range(4)])  25.1 us
    pallas_call x1, Pallas kernels, channelize(): pl.pallas_call(channel_kernel, grid=(2, 8), in_specs=[pl.BlockSpec((1, 75...  19.8 us
    all_to_all x1, starting transfers between devices, on_device(): lax.all_to_all(model.reshape(64, slots, 128), AXES[:4], 0, 0, tiled=True)  15.1 us
    ppermute x6, starting transfers between devices, shift(): return lax.ppermute(value, axis, [(n, (n + offset) % 4) for n in range(4)])  10 us
    all_to_all x1, starting transfers between devices, on_device(): lax.all_to_all(spectra.reshape(64, 4, 64, 128), TURN, 0, 0, tiled=True)  9.51 us
    pallas_call x4, Pallas kernels, form_beams(): pl.pallas_call(beam_kernel, grid_spec=pltpu.PrefetchScalarGridSpec(num_sc...  7.31 us
    ppermute x6, waiting for transfers between devices, shift(): return lax.ppermute(value, axis, [(n, (n + offset) % 4) for n in range(4)])  7.14 us
  transfers between devices with their start and end apart: 17, of which 6 were waited for; matrix products, arithmetic and copies ran while one was open for 1% of the time, Pallas kernels for 17%

profile of v10, /device:TPU:1, one launch (start us, length us, event | category | flops | bytes accessed | tf_op | source)
XLA Modules:
  0.0 155.7 jit_solution(10227209877781145303)
XLA Ops:
  0.6 1.1 fusion.6
  1.8 1.2 convolution_bitcast_fusion
  3.0 0.8 broadcast_in_dim.28
  3.8 15.1 %all-to-all-start = ((f32[64,16,128]{2,1,0:T(8,128)}), f32[64,16,128]{2,1,0:T(8,128)S(1)}, u32[]{:S(2)}, u32[]{:S(2)}) async-start(f32[64,16,128]{2,1,0:T(8,128)} %bitcast.5), calls=%async_computation | async-start | bytes 1048576 | tf_op jit(solution)/shard_map/all_to_all | solution.py:321
  19.0 0.8 copy-done.1
  19.8 0.8 copy-done.2
  20.6 0.8 copy-done.3
  21.5 19.8 %channelize.1 = bf16[2,2,4,4,4,2,32,128]{7,6,5,4,3,2,1,0:T(8,128)(2,1)} custom-call(bf16[2,75,128,128]{3,2,1,0:T(8,128)(2,1)} %bitcast.40, f32[12,8192]{1,0:T(8,128)} %taps.1, bf16[256,128]{1,0:T(8,128)(2,1)S(1)} %copy-done.1, f32[2,64,128]{2,1,0:T(8,128)S(1)} %copy-done.2, bf16[128,256]{1,0:T(8,128)(2,1)S(1)} %copy-done.3), custom_call_target="tpu_custom_call" | custom-call | tf_op jit(solution)/shard_map/channelize/pallas_call | solution.py:133
  41.3 0.5 keep_owner.1
  41.9 9.5 %all-to-all-start.1 = ((bf16[64,4,64,128]{3,2,1,0:T(8,128)(2,1)}), bf16[64,4,64,128]{3,2,1,0:T(8,128)(2,1)}, u32[]{:S(2)}, u32[]{:S(2)}) async-start(bf16[64,4,64,128]{3,2,1,0:T(8,128)(2,1)} %bitcast.39), calls=%async_computation.1 | async-start | bytes 8388608 | tf_op jit(solution)/shard_map/all_to_all | solution.py:328
  51.4 0.7 gather_fusion
  52.1 1.7 %collective-permute-start = (f32[16,128]{1,0:T(8,128)S(1)}, f32[16,128]{1,0:T(8,128)S(1)}, u32[]{:S(2)}, u32[]{:S(2)}) collective-permute-start(f32[16,128]{1,0:T(8,128)S(1)} %keep_owner.1), channel_id=1, source_target_pairs={{0,3},{1,2},{2,1},{3,0},{4,7},{5,6},{6,5},{7,4},{8,11},{9,10},{10,... | collective-permute-start | bytes 24584 | tf_op jit(solution)/shard_map/ppermute | solution.py:309
  54.9 45.0 %collective-permute-done = f32[16,128]{1,0:T(8,128)S(1)} collective-permute-done((f32[16,128]{1,0:T(8,128)S(1)}, f32[16,128]{1,0:T(8,128)S(1)}, u32[]{:S(2)}, u32[]{:S(2)}) %collective-permute-start) | collective-permute-done | bytes 8224 | tf_op jit(solution)/shard_map/ppermute | solution.py:309
  101.1 1.5 all-to-all-done.1.spectra
  102.5 1.8 %form_beams.6 = (bf16[4,16,16,128]{3,2,1,0:T(8,128)(2,1)S(1)}, bf16[4,16,16,128]{3,2,1,0:T(8,128)(2,1)S(1)}) custom-call(s32[1]{0:T(128)} %bitcast.19.where, bf16[64,4,64,128]{3,2,1,0:T(8,128)(2,1)} %all-to-all-done.1.spectra, f32[2,64,128]{2,1,0:T(8,128)S(1)} %get-tuple-element.50.base, f32[2,64,128]{2,1,0:T(8,128)S(1)} %pad_maximum_fusion.1.step), custom_call_target="tpu_custom_call" | custom-call | tf_op jit(solution)/shard_map/form_beams/pallas_call | solution.py:194
  104.4 2.2 %collective-permute-start.3 = (bf16[4,16,16,128]{3,2,1,0:T(8,128)(2,1)S(1)}, bf16[4,16,16,128]{3,2,1,0:T(8,128)(2,1)S(1)}, u32[]{:S(2)}, u32[]{:S(2)}) collective-permute-start(bf16[4,16,16,128]{3,2,1,0:T(8,128)(2,1)S(1)} %get-tuple-element.20), channel_id=1, source_target_pairs={{0,32},{32,64},{64,96},{96,0},{1,33},{33,65},{65,97},{97,1},{2,34}... | collective-permute-start | bytes 786440 | tf_op jit(solution)/shard_map/ppermute | solution.py:305
  106.6 1.4 collective-permute-start.10
  108.0 1.8 %form_beams.7 = (bf16[4,16,16,128]{3,2,1,0:T(8,128)(2,1)S(1)}, bf16[4,16,16,128]{3,2,1,0:T(8,128)(2,1)S(1)}) custom-call(s32[1]{0:T(128)} %bitcast.22.where, bf16[64,4,64,128]{3,2,1,0:T(8,128)(2,1)} %all-to-all-done.1.spectra, f32[2,64,128]{2,1,0:T(8,128)S(1)} %get-tuple-element.51.base, f32[2,64,128]{2,1,0:T(8,128)S(1)} %pad_maximum_fusion.1.step), custom_call_target="tpu_custom_call" | custom-call | tf_op jit(solution)/shard_map/form_beams/pallas_call | solution.py:194
  109.9 1.6 %collective-permute-start.5 = (bf16[4,16,16,128]{3,2,1,0:T(8,128)(2,1)S(1)}, bf16[4,16,16,128]{3,2,1,0:T(8,128)(2,1)S(1)}, u32[]{:S(2)}, u32[]{:S(2)}) collective-permute-start(bf16[4,16,16,128]{3,2,1,0:T(8,128)(2,1)S(1)} %get-tuple-element.21), channel_id=1, source_target_pairs={{0,96},{32,0},{64,32},{96,64},{1,97},{33,1},{65,33},{97,65},{2,98}... | collective-permute-start | bytes 786440 | tf_op jit(solution)/shard_map/ppermute | solution.py:305
  111.5 1.8 %form_beams.5 = (bf16[4,16,16,128]{3,2,1,0:T(8,128)(2,1)S(1)}, bf16[4,16,16,128]{3,2,1,0:T(8,128)(2,1)S(1)}) custom-call(s32[1]{0:T(128)} %bitcast.16.where, bf16[64,4,64,128]{3,2,1,0:T(8,128)(2,1)} %all-to-all-done.1.spectra, f32[2,64,128]{2,1,0:T(8,128)S(1)} %get-tuple-element.49.base, f32[2,64,128]{2,1,0:T(8,128)S(1)} %pad_maximum_fusion.1.step), custom_call_target="tpu_custom_call" | custom-call | tf_op jit(solution)/shard_map/form_beams/pallas_call | solution.py:194
  113.4 1.1 collective-permute-start.4
  114.5 3.4 %collective-permute-start.9 = (bf16[4,16,16,128]{3,2,1,0:T(8,128)(2,1)S(1)}, bf16[4,16,16,128]{3,2,1,0:T(8,128)(2,1)S(1)}, u32[]{:S(2)}, u32[]{:S(2)}) collective-permute-start(bf16[4,16,16,128]{3,2,1,0:T(8,128)(2,1)S(1)} %get-tuple-element.23), channel_id=1, source_target_pairs={{0,32},{32,64},{64,96},{96,0},{1,33},{33,65},{65,97},{97,1},{2,34}... | collective-permute-start | bytes 786440 | tf_op jit(solution)/shard_map/ppermute | solution.py:305
  118.2 1.8 %form_beams.4 = (bf16[4,16,16,128]{3,2,1,0:T(8,128)(2,1)S(1)}, bf16[4,16,16,128]{3,2,1,0:T(8,128)(2,1)S(1)}) custom-call(s32[1]{0:T(128)} %bitcast.1.where, bf16[64,4,64,128]{3,2,1,0:T(8,128)(2,1)} %all-to-all-done.1.spectra, f32[2,64,128]{2,1,0:T(8,128)S(1)} %get-tuple-element.48.base, f32[2,64,128]{2,1,0:T(8,128)S(1)} %pad_maximum_fusion.1.step), custom_call_target="tpu_custom_call" | custom-call | tf_op jit(solution)/shard_map/form_beams/pallas_call | solution.py:194
  120.2 6.9 %collective-permute-done.4.refs_1_ = bf16[4,16,16,128]{3,2,1,0:T(8,128)(2,1)S(1)} collective-permute-done((bf16[4,16,16,128]{3,2,1,0:T(8,128)(2,1)S(1)}, bf16[4,16,16,128]{3,2,1,0:T(8,128)(2,1)S(1)}, u32[]{:S(2)}, u32[]{:S(2)}) %collective-permute-start.4) | collective-permute-done | bytes 262176 | tf_op jit(solution)/shard_map/ppermute | solution.py:305
  127.2 1.4 collective-permute-start.6
  128.6 16.0 %collective-permute-start.7 = (bf16[16,16,128]{2,1,0:T(8,128)(2,1)S(1)}, bf16[16,16,128]{2,1,0:T(8,128)(2,1)S(1)}, u32[]{:S(2)}, u32[]{:S(2)}) collective-permute-start(bf16[16,16,128]{2,1,0:T(8,128)(2,1)S(1)} %add_group.10), channel_id=1, source_target_pairs={{0,2},{1,3},{2,0},{3,1},{4,6},{5,7},{6,4},{7,5},{8,10},{9,11},{10,... | collective-permute-start | bytes 196616 | tf_op jit(solution)/shard_map/ppermute | solution.py:309
  144.8 1.7 %collective-permute-start.12 = (bf16[16,16,128]{2,1,0:T(8,128)(2,1)S(1)}, bf16[16,16,128]{2,1,0:T(8,128)(2,1)S(1)}, u32[]{:S(2)}, u32[]{:S(2)}) collective-permute-start(bf16[16,16,128]{2,1,0:T(8,128)(2,1)S(1)} %add_group.13), channel_id=1, source_target_pairs={{0,1},{1,0},{2,3},{3,2},{4,5},{5,4},{6,7},{7,6},{8,9},{9,8},{10,11... | collective-permute-start | bytes 196616 | tf_op jit(solution)/shard_map/ppermute | solution.py:309
  146.5 3.6 %collective-permute-start.13 = (bf16[16,16,128]{2,1,0:T(8,128)(2,1)S(1)}, bf16[16,16,128]{2,1,0:T(8,128)(2,1)S(1)}, u32[]{:S(2)}, u32[]{:S(2)}) collective-permute-start(bf16[16,16,128]{2,1,0:T(8,128)(2,1)S(1)} %add_group.14), channel_id=1, source_target_pairs={{0,2},{1,3},{2,0},{3,1},{4,6},{5,7},{6,4},{7,5},{8,10},{9,11},{10,... | collective-permute-start | bytes 196616 | tf_op jit(solution)/shard_map/ppermute | solution.py:309
  150.3 1.5 merge.2
  151.8 0.7 collective-permute-done.13.refs_2_
  152.5 1.7 %collective-permute-done.14.refs_3_ = bf16[16,16,128]{2,1,0:T(8,128)(2,1)S(1)} collective-permute-done((bf16[16,16,128]{2,1,0:T(8,128)(2,1)S(1)}, bf16[16,16,128]{2,1,0:T(8,128)(2,1)S(1)}, u32[]{:S(2)}, u32[]{:S(2)}) %collective-permute-start.14) | collective-permute-done | bytes 65568 | tf_op jit(solution)/shard_map/ppermute | solution.py:309
  154.2 1.5 merge.3
  (50 shorter events, 3.3 us)
Async XLA Ops:
  0.6 50.8 %copy-start = (f32[64,512]{1,0:T(8,128)S(1)}, f32[64,512]{1,0:T(8,128)}, u32[]{:S(2)}) copy-start(f32[64,512]{1,0:T(8,128)} %param.13) | copy-start | bytes 393220
  3.8 37.5 %all-to-all-start = ((f32[64,16,128]{2,1,0:T(8,128)}), f32[64,16,128]{2,1,0:T(8,128)S(1)}, u32[]{:S(2)}, u32[]{:S(2)}) async-start(f32[64,16,128]{2,1,0:T(8,128)} %bitcast.5), calls=%async_computation | async-start | bytes 1048576 | tf_op jit(solution)/shard_map/all_to_all | solution.py:321
  19.0 0.8 copy-start.1
  19.8 0.8 copy-start.2
  20.6 0.8 copy-start.3
  21.5 19.8 %copy-start.4 = (s32[4]{0:T(128)S(1)}, s32[4]{0:T(128)}, u32[]{:S(2)}) copy-start(s32[4]{0:T(128)} %owners.1) | copy-start | bytes 52
  41.9 9.5 %copy-start.5 = (s32[64]{0:T(128)S(1)}, s32[64]{0:T(128)}, u32[]{:S(2)}) copy-start(s32[64]{0:T(128)} %param.15) | copy-start | bytes 772
  41.9 60.6 %all-to-all-start.1 = ((bf16[64,4,64,128]{3,2,1,0:T(8,128)(2,1)}), bf16[64,4,64,128]{3,2,1,0:T(8,128)(2,1)}, u32[]{:S(2)}, u32[]{:S(2)}) async-start(bf16[64,4,64,128]{3,2,1,0:T(8,128)(2,1)} %bitcast.39), calls=%async_computation.1 | async-start | bytes 8388608 | tf_op jit(solution)/shard_map/all_to_all | solution.py:328
  52.1 47.8 %collective-permute-start = (f32[16,128]{1,0:T(8,128)S(1)}, f32[16,128]{1,0:T(8,128)S(1)}, u32[]{:S(2)}, u32[]{:S(2)}) collective-permute-start(f32[16,128]{1,0:T(8,128)S(1)} %keep_owner.1), channel_id=1, source_target_pairs={{0,3},{1,2},{2,1},{3,0},{4,7},{5,6},{6,5},{7,4},{8,11},{9,10},{10,... | collective-permute-start | bytes 24584 | tf_op jit(solution)/shard_map/ppermute | solution.py:309
  53.8 46.1 %collective-permute-start.1 = (f32[16,128]{1,0:T(8,128)S(1)}, f32[16,128]{1,0:T(8,128)S(1)}, u32[]{:S(2)}, u32[]{:S(2)}) collective-permute-start(f32[16,128]{1,0:T(8,128)S(1)} %keep_owner.1), channel_id=1, source_target_pairs={{0,2},{1,3},{2,0},{3,1},{4,6},{5,7},{6,4},{7,5},{8,10},{9,11},{10,... | collective-permute-start | bytes 24584 | tf_op jit(solution)/shard_map/ppermute | solution.py:309
  54.1 45.9 %collective-permute-start.2 = (f32[16,128]{1,0:T(8,128)S(1)}, f32[16,128]{1,0:T(8,128)S(1)}, u32[]{:S(2)}, u32[]{:S(2)}) collective-permute-start(f32[16,128]{1,0:T(8,128)S(1)} %keep_owner.1), channel_id=1, source_target_pairs={{0,1},{1,0},{2,3},{3,2},{4,5},{5,4},{6,7},{7,6},{8,9},{9,8},{10,11... | collective-permute-start | bytes 24584 | tf_op jit(solution)/shard_map/ppermute | solution.py:309
  104.4 8.9 %collective-permute-start.3 = (bf16[4,16,16,128]{3,2,1,0:T(8,128)(2,1)S(1)}, bf16[4,16,16,128]{3,2,1,0:T(8,128)(2,1)S(1)}, u32[]{:S(2)}, u32[]{:S(2)}) collective-permute-start(bf16[4,16,16,128]{3,2,1,0:T(8,128)(2,1)S(1)} %get-tuple-element.20), channel_id=1, source_target_pairs={{0,32},{32,64},{64,96},{96,0},{1,33},{33,65},{65,97},{97,1},{2,34}... | collective-permute-start | bytes 786440 | tf_op jit(solution)/shard_map/ppermute | solution.py:305
  106.6 11.3 %collective-permute-start.10 = (bf16[4,16,16,128]{3,2,1,0:T(8,128)(2,1)S(1)}, bf16[4,16,16,128]{3,2,1,0:T(8,128)(2,1)S(1)}, u32[]{:S(2)}, u32[]{:S(2)}) collective-permute-start(bf16[4,16,16,128]{3,2,1,0:T(8,128)(2,1)S(1)} %get-tuple-element.25), channel_id=1, source_target_pairs={{0,96},{32,0},{64,32},{96,64},{1,97},{33,1},{65,33},{97,65},{2,98}... | collective-permute-start | bytes 786440 | tf_op jit(solution)/shard_map/ppermute | solution.py:305
  109.9 10.4 %collective-permute-start.5 = (bf16[4,16,16,128]{3,2,1,0:T(8,128)(2,1)S(1)}, bf16[4,16,16,128]{3,2,1,0:T(8,128)(2,1)S(1)}, u32[]{:S(2)}, u32[]{:S(2)}) collective-permute-start(bf16[4,16,16,128]{3,2,1,0:T(8,128)(2,1)S(1)} %get-tuple-element.21), channel_id=1, source_target_pairs={{0,96},{32,0},{64,32},{96,64},{1,97},{33,1},{65,33},{97,65},{2,98}... | collective-permute-start | bytes 786440 | tf_op jit(solution)/shard_map/ppermute | solution.py:305
  113.4 13.8 %collective-permute-start.4 = (bf16[4,16,16,128]{3,2,1,0:T(8,128)(2,1)S(1)}, bf16[4,16,16,128]{3,2,1,0:T(8,128)(2,1)S(1)}, u32[]{:S(2)}, u32[]{:S(2)}) collective-permute-start(bf16[4,16,16,128]{3,2,1,0:T(8,128)(2,1)S(1)} %add_pair.2), channel_id=1, source_target_pairs={{0,32},{32,64},{64,96},{96,0},{1,33},{33,65},{65,97},{97,1},{2,34}... | collective-permute-start | bytes 786440 | tf_op jit(solution)/shard_map/ppermute | solution.py:305
  114.5 30.2 %collective-permute-start.9 = (bf16[4,16,16,128]{3,2,1,0:T(8,128)(2,1)S(1)}, bf16[4,16,16,128]{3,2,1,0:T(8,128)(2,1)S(1)}, u32[]{:S(2)}, u32[]{:S(2)}) collective-permute-start(bf16[4,16,16,128]{3,2,1,0:T(8,128)(2,1)S(1)} %get-tuple-element.23), channel_id=1, source_target_pairs={{0,32},{32,64},{64,96},{96,0},{1,33},{33,65},{65,97},{97,1},{2,34}... | collective-permute-start | bytes 786440 | tf_op jit(solution)/shard_map/ppermute | solution.py:305
  117.9 26.8 %collective-permute-start.11 = (bf16[4,16,16,128]{3,2,1,0:T(8,128)(2,1)S(1)}, bf16[4,16,16,128]{3,2,1,0:T(8,128)(2,1)S(1)}, u32[]{:S(2)}, u32[]{:S(2)}) collective-permute-start(bf16[4,16,16,128]{3,2,1,0:T(8,128)(2,1)S(1)} %add_pair.3), channel_id=1, source_target_pairs={{0,96},{32,0},{64,32},{96,64},{1,97},{33,1},{65,33},{97,65},{2,98}... | collective-permute-start | bytes 786440 | tf_op jit(solution)/shard_map/ppermute | solution.py:305
  127.2 22.9 %collective-permute-start.6 = (bf16[16,16,128]{2,1,0:T(8,128)(2,1)S(1)}, bf16[16,16,128]{2,1,0:T(8,128)(2,1)S(1)}, u32[]{:S(2)}, u32[]{:S(2)}) collective-permute-start(bf16[16,16,128]{2,1,0:T(8,128)(2,1)S(1)} %add_group.9), channel_id=1, source_target_pairs={{0,1},{1,0},{2,3},{3,2},{4,5},{5,4},{6,7},{7,6},{8,9},{9,8},{10,11... | collective-permute-start | bytes 196616 | tf_op jit(solution)/shard_map/ppermute | solution.py:309
  128.6 21.7 %collective-permute-start.7 = (bf16[16,16,128]{2,1,0:T(8,128)(2,1)S(1)}, bf16[16,16,128]{2,1,0:T(8,128)(2,1)S(1)}, u32[]{:S(2)}, u32[]{:S(2)}) collective-permute-start(bf16[16,16,128]{2,1,0:T(8,128)(2,1)S(1)} %add_group.10), channel_id=1, source_target_pairs={{0,2},{1,3},{2,0},{3,1},{4,6},{5,7},{6,4},{7,5},{8,10},{9,11},{10,... | collective-permute-start | bytes 196616 | tf_op jit(solution)/shard_map/ppermute | solution.py:309
  144.6 5.7 %collective-permute-start.8 = (bf16[16,16,128]{2,1,0:T(8,128)(2,1)S(1)}, bf16[16,16,128]{2,1,0:T(8,128)(2,1)S(1)}, u32[]{:S(2)}, u32[]{:S(2)}) collective-permute-start(bf16[16,16,128]{2,1,0:T(8,128)(2,1)S(1)} %add_group.11), channel_id=1, source_target_pairs={{0,3},{1,2},{2,1},{3,0},{4,7},{5,6},{6,5},{7,4},{8,11},{9,10},{10,... | collective-permute-start | bytes 196616 | tf_op jit(solution)/shard_map/ppermute | solution.py:309
  144.8 7.1 %collective-permute-start.12 = (bf16[16,16,128]{2,1,0:T(8,128)(2,1)S(1)}, bf16[16,16,128]{2,1,0:T(8,128)(2,1)S(1)}, u32[]{:S(2)}, u32[]{:S(2)}) collective-permute-start(bf16[16,16,128]{2,1,0:T(8,128)(2,1)S(1)} %add_group.13), channel_id=1, source_target_pairs={{0,1},{1,0},{2,3},{3,2},{4,5},{5,4},{6,7},{7,6},{8,9},{9,8},{10,11... | collective-permute-start | bytes 196616 | tf_op jit(solution)/shard_map/ppermute | solution.py:309
  146.5 6.0 %collective-permute-start.13 = (bf16[16,16,128]{2,1,0:T(8,128)(2,1)S(1)}, bf16[16,16,128]{2,1,0:T(8,128)(2,1)S(1)}, u32[]{:S(2)}, u32[]{:S(2)}) collective-permute-start(bf16[16,16,128]{2,1,0:T(8,128)(2,1)S(1)} %add_group.14), channel_id=1, source_target_pairs={{0,2},{1,3},{2,0},{3,1},{4,6},{5,7},{6,4},{7,5},{8,10},{9,11},{10,... | collective-permute-start | bytes 196616 | tf_op jit(solution)/shard_map/ppermute | solution.py:309
  150.1 4.1 %collective-permute-start.14 = (bf16[16,16,128]{2,1,0:T(8,128)(2,1)S(1)}, bf16[16,16,128]{2,1,0:T(8,128)(2,1)S(1)}, u32[]{:S(2)}, u32[]{:S(2)}) collective-permute-start(bf16[16,16,128]{2,1,0:T(8,128)(2,1)S(1)} %add_group.15), channel_id=1, source_target_pairs={{0,3},{1,2},{2,1},{3,0},{4,7},{5,6},{6,5},{7,4},{8,11},{9,10},{10,... | collective-permute-start | bytes 196616 | tf_op jit(solution)/shard_map/ppermute | solution.py:309
